TPU v7x, 256 devices: a whole 4x4x8 slice. The times are simulated.
256 devices in a mesh: grp: 8 (over x, core), own: 32 (over z, y).
Axes of the slice: x: 4, y: 4, z: 8, core: 2. Of those that a mesh axis runs over, the one named last changes fastest.
Arguments:
- orbitals: bfloat16 [256, 32, 1024], P(('grp', 'own')), may hold values from -3 to 3
- offsets: int32 [256, 2], P(('grp', 'own')), may hold values from 0 to 32
- pairs: int32 [256, 2], P('grp'), may hold values from 0 to 31, as said below
- ext_pot: bfloat16 [32, 4096], replicated, may hold values from -6 to 6
Outputs:
- gradient: float32 [256, 32, 1024], P(('grp', 'own'))
Inputs may be any that keep to these rules, and one draw needn't show every extreme that they name: `pairs`: rows g * 32 to g * 32 + 31 belong to group g; each row names two different orbitals of the group. Calling owner o the device holding orbital o of a group, at most 2 rows of a group have orbital o as their first orbital, and in every group some owner has exactly 2.
All inputs are finite; a program needn't handle non-finite values.
Results may differ from a plain program's by a relative error of at most 0.0006.
Values may be sent and summed in bfloat16 or wider, within the bound.
No kernel may reach another device: no remote copies, remote signals or barrier semaphores. Data moves between devices by JAX's collectives and lax.ppermute only.
A program may use at most 64 MiB of HBM per device.

v0:
```python
import math

import jax
import jax.numpy as jnp
import numpy as np
from jax import lax
from jax.experimental import pallas as pl
from jax.experimental.pallas import tpu as pltpu
from jax.sharding import PartitionSpec as P

B = 32
BZ = 32
G = 64
N = 32
HALF = 16
SCREEN = 0.0025
MIXING = 0.25
EXCHANGE_COEF = (3.0 / math.pi) ** (1.0 / 3.0)
F32 = jnp.float32
BF16 = jnp.bfloat16
VM = pl.BlockSpec(memory_space=pltpu.VMEM)
SM = pl.BlockSpec(memory_space=pltpu.SMEM)


def axis_basis():
    position = np.arange(B) - 15.5
    cosine = np.cos(2 * np.pi / G * np.outer(position, np.arange(B)))
    sine = np.sin(2 * np.pi / G * np.outer(position, np.arange(1, B + 1)))
    return cosine, sine


def fold_matrix():
    fold = np.zeros((2, 4, B, 2, 2, 4, HALF))
    for h in range(2):
        for yy in range(4):
            row = yy if h == 0 else 3 - yy
            for x in range(B):
                col = x if x < HALF else B - 1 - x
                for py in range(2):
                    for px in range(2):
                        sign = (-1 if py and h else 1) * (-1 if px and x >= HALF else 1)
                        fold[h, yy, x, py, px, row, col] = sign
    return fold.reshape(256, 256)


def wave_info(parity):
    waves = np.arange(B) + parity
    weight = np.where((waves == 0) | (waves == B), 1.0, 2.0) / G
    return waves, weight


def split(value):
    high = value.astype(BF16)
    low = (value - high.astype(F32)).astype(BF16)
    return high, low


def np_split(value):
    value = value.astype(np.float32)
    high = value.astype(jnp.bfloat16)
    low = (value - high.astype(np.float32)).astype(jnp.bfloat16)
    return high, low


def dot(a, b):
    return jnp.dot(a, b, preferred_element_type=F32)


def torus_roll(load, by_y, by_x):
    lane = lax.broadcasted_iota(jnp.int32, (N, 128), 1)
    by_y = lax.rem(by_y, B)
    by_x = lax.rem(by_x, B)
    rows = lax.div(by_y, 4)
    rest = lax.rem(by_y, 4)
    shift = rest * B + by_x
    near = lax.rem(128 - shift, 128)
    far = lax.rem(128 + B - shift, 128)
    inside = lax.rem(lane, B) < B - by_x
    same = lax.div(lane, B) < 4 - rest
    moved = []
    for s in range(8):
        chunk = load(lax.rem(rows + s, 8))
        moved.append(
            jnp.where(inside, pltpu.roll(chunk, near, 1), pltpu.roll(chunk, far, 1))
        )
    return [jnp.where(same, moved[s], moved[(s + 1) % 8]) for s in range(8)]


def pack_kernel(offsets, box, out, planes):
    oy = offsets[0, 0]
    ox = offsets[0, 1]

    def load(c):
        return box[0, :, pl.ds(pl.multiple_of(c * 128, 128), 128)].astype(F32)

    chunks = torus_roll(load, B - lax.rem(oy, B), B - lax.rem(ox, B))
    for s in range(8):
        planes[pl.ds(s, N, stride=8), :] = chunks[s]
    row = lax.broadcasted_iota(jnp.int32, (8, 128), 0)
    extra = jnp.where(
        row == 0, oy.astype(F32), jnp.where(row == 1, ox.astype(F32), 0.0)
    )
    for z in range(N):
        both = jnp.concatenate([planes[8 * z : 8 * z + 8, :], extra], axis=0)
        out[z] = both.astype(BF16)


def pair_kernel(pairs, recv, rho, dens, phi, code):
    row = lax.broadcasted_iota(jnp.int32, (8, 128), 0)
    lane = lax.broadcasted_iota(jnp.int32, (8, 128), 1)
    y = (row * 4 + lax.div(lane, B)).astype(F32)
    x = lax.rem(lane, B).astype(F32)
    total = [jnp.zeros((8, 128), F32) for _ in range(4)]
    for n in range(N):
        value = recv[n].astype(F32)
        plane = value[:8]
        below = jnp.where(y < value[8:9], 2.0, 0.0)
        quarter = below + jnp.where(x < value[9:10], 1.0, 0.0)
        phi[n] = plane
        code[n] = quarter
        square = plane * plane
        for q in range(4):
            total[q] = total[q] + jnp.where(quarter == float(q), square, 0.0)
    for g in range(8):
        for q in range(4):
            dens[g, q] = total[q]
    for p in range(N):
        a = pairs[p, 0]
        b = pairs[p, 1]
        rho[p] = jnp.where(code[a] == code[b], phi[a] * phi[b], 0.0)


def table_kernel(rows_y, rows_x, cols_y, cols_x, ahead_hi, ahead_lo, back_hi, back_lo, green):
    for par in range(4):
        py, px = par // 2, par % 2
        for c in range(HALF):
            high, low = split(rows_y[py, c : c + 1, :] * rows_x[px])
            ahead_hi[par, c * HALF : (c + 1) * HALF, :] = high
            ahead_lo[par, c * HALF : (c + 1) * HALF, :] = low
        for k in range(B):
            high, low = split(cols_y[py, k : k + 1, :] * cols_x[px])
            back_hi[par, k * B : (k + 1) * B, :] = high
            back_lo[par, k * B : (k + 1) * B, :] = low
        kz = lax.broadcasted_iota(jnp.int32, (G, B * B), 0)
        pos = lax.broadcasted_iota(jnp.int32, (G, B * B), 1)
        kz = jnp.where(kz >= B, kz - (B - 1), kz)
        ky = lax.div(pos, B) + py
        kx = lax.rem(pos, B) + px
        weight = jnp.full((G, B * B), 4.0 * math.pi * 8.0 / G**3, F32)
        squares = jnp.full((G, B * B), SCREEN, F32)
        for k in (kx, ky, kz):
            weight = jnp.where((k == 0) | (k == B), weight * 0.5, weight)
            wave = 2.0 * math.pi / G * k.astype(F32)
            squares = squares + wave * wave
        green[par] = weight / squares


def solve_kernel(
    first, recv, rho, ahead_hi, ahead_lo, back_hi, back_lo, green, fold, unfold, z_ahead, z_back, out
):
    place = recv[first[0]].astype(F32)
    oy = jnp.max(place[8:9, :]).astype(jnp.int32)
    ox = jnp.max(place[9:10, :]).astype(jnp.int32)
    chunks = torus_roll(lambda c: rho[pl.ds(c, N, stride=8), :], oy, ox)
    lane = lax.broadcasted_iota(jnp.int32, (N, 128), 1)
    low_half = lane < 64

    stacked = jnp.concatenate(
        [jnp.concatenate([chunks[s], chunks[7 - s]], axis=1) for s in range(4)], axis=0
    )
    high, low = split(stacked)
    folded = dot(high, fold[...]) + dot(low, fold[...])

    def regroup(tile, par_low, parts):
        first_part, second_part = parts
        if par_low:
            return jnp.where(low_half, first_part, pltpu.roll(second_part, 64, 1))
        return jnp.where(low_half, pltpu.roll(first_part, 64, 1), second_part)

    solved = []
    for par in range(4):
        c = 128 * (par // 2)
        pieces = [folded[N * s : N * s + N, c : c + 128] for s in range(4)]
        data = jnp.concatenate(
            [regroup(t, par % 2 == 0, pieces[2 * t : 2 * t + 2]) for t in range(2)], axis=1
        )
        high, low = split(data)
        both = dot(jnp.concatenate([high, low], axis=0), ahead_hi[par])
        plane_waves = both[:N] + both[N:] + dot(high, ahead_lo[par])
        high, low = split(plane_waves)
        waves = dot(z_ahead[...], jnp.concatenate([high, high, low], axis=0)) * green[par]
        high, low = split(waves)
        back = dot(z_back[...], jnp.concatenate([high, high, low], axis=0))
        high, low = split(back)
        both = dot(jnp.concatenate([high, low], axis=0), back_hi[par])
        solved.append(both[:N] + both[N:] + dot(high, back_lo[par]))

    rows = []
    for s in range(4):
        t = 128 * (s // 2)
        tiles = []
        for half in range(2):
            even = solved[2 * half][:, t : t + 128]
            odd = solved[2 * half + 1][:, t : t + 128]
            tiles.append(regroup(half, s % 2 == 0, (even, odd)))
        rows.append(jnp.concatenate(tiles, axis=1))
    high, low = split(jnp.concatenate(rows, axis=0))
    spread = dot(high, unfold[...]) + dot(low, unfold[...])
    field = [spread[N * s : N * s + N, :128] for s in range(4)] + [
        spread[N * s : N * s + N, 128:] for s in range(3, -1, -1)
    ]
    chunk_store = out
    return field, oy, ox, chunk_store


def solve_and_send(
    first, recv, rho, ahead_hi, ahead_lo, back_hi, back_lo, green, fold, unfold, z_ahead, z_back, out, boxed
):
    field, oy, ox, _ = solve_kernel(
        first, recv, rho, ahead_hi, ahead_lo, back_hi, back_lo, green, fold, unfold, z_ahead, z_back, out
    )
    for s in range(8):
        boxed[s] = field[s]
    chunks = torus_roll(lambda c: boxed[c], B - lax.rem(oy, B), B - lax.rem(ox, B))
    for s in range(8):
        out[pl.ds(s, N, stride=8), :] = chunks[s]


def gradient_kernel(pairs, phi, code, field, pot, out, terms):
    for n in range(N):
        terms[n] = jnp.zeros((8, 128), F32)
    for p in range(N):
        a = pairs[p, 0]
        b = pairs[p, 1]
        value = jnp.where(code[a] == code[b], field[p], 0.0)
        terms[a] = terms[a] + value * phi[b]
        terms[b] = terms[b] + value * phi[a]
    quarters = [pot[q] for q in range(4)]
    for n in range(N):
        quarter = code[n]
        local = jnp.where(
            quarter < 1.5,
            jnp.where(quarter < 0.5, quarters[0], quarters[1]),
            jnp.where(quarter < 2.5, quarters[2], quarters[3]),
        )
        out[n] = local * phi[n] - MIXING * terms[n]


def unpack_kernel(offsets, planes, out):
    chunks = torus_roll(
        lambda c: planes[pl.ds(c, N, stride=8), :], offsets[0, 0], offsets[0, 1]
    )
    for s in range(8):
        out[0, :, 128 * s : 128 * s + 128] = chunks[s]


def shape(dims, dtype=F32):
    return jax.ShapeDtypeStruct(dims, dtype)


def constants():
    cosine, sine = axis_basis()
    bases = [cosine[:HALF], sine[:HALF]]
    rows_y = np.stack([np.repeat(b, B, axis=1) for b in bases])
    rows_x = np.stack([np.tile(b, (1, B)) for b in bases])
    cols_y = np.stack([np.repeat(b.T, HALF, axis=1) for b in bases])
    cols_x = np.stack([np.tile(b.T, (1, HALF)) for b in bases])
    fold = fold_matrix()
    z_basis = np.concatenate([cosine, sine], axis=1)
    ahead_hi, ahead_lo = np_split(z_basis.T)
    back_hi, back_lo = np_split(z_basis)
    return (
        [jnp.asarray(t.astype(np.float32)) for t in (rows_y, rows_x, cols_y, cols_x)],
        [jnp.asarray(t, BF16) for t in (fold, fold.T)],
        [
            jnp.asarray(np.concatenate([ahead_hi, ahead_lo, ahead_hi], axis=1)),
            jnp.asarray(np.concatenate([back_hi, back_lo, back_hi], axis=1)),
        ],
    )


def exchange(x):
    return lax.all_to_all(x, "own", 0, 0, tiled=True)


def body(orbitals, offsets, pairs, ext_pot):
    owner = lax.axis_index("own")
    bases, folds, z_tables = constants()

    sent = pl.pallas_call(
        pack_kernel,
        out_shape=shape((N, 16, 128), BF16),
        in_specs=[SM, VM],
        out_specs=VM,
        scratch_shapes=[pltpu.VMEM((8 * N, 128), F32)],
        name="pack",
    )(offsets, orbitals)
    recv = exchange(sent)

    tables = pl.pallas_call(
        table_kernel,
        out_shape=[
            shape((4, 256, 1024), BF16),
            shape((4, 256, 1024), BF16),
            shape((4, 1024, 256), BF16),
            shape((4, 1024, 256), BF16),
            shape((4, G, 1024)),
        ],
        in_specs=[VM] * 4,
        out_specs=[VM] * 5,
        compiler_params=pltpu.CompilerParams(vmem_limit_bytes=40 << 20),
        cost_estimate=pl.CostEstimate(flops=20_000_000, bytes_accessed=10_000_000, transcendentals=0),
        name="tables",
    )(*bases)

    rho, dens, phi, code = pl.pallas_call(
        pair_kernel,
        out_shape=[
            shape((N, 8, 128)),
            shape((8, 4, 8, 128)),
            shape((N, 8, 128)),
            shape((N, 8, 128)),
        ],
        in_specs=[SM, VM],
        out_specs=[VM] * 4,
        name="pair_products",
    )(pairs, recv)

    mine = exchange(rho)
    densities = lax.all_to_all(dens, "grp", 0, 0, tiled=True)
    first = lax.dynamic_slice_in_dim(pairs, owner, 1, 0)[0, :1]
    field = pl.pallas_call(
        solve_and_send,
        out_shape=shape((8 * N, 128)),
        in_specs=[SM] + [VM] * 11,
        out_specs=VM,
        scratch_shapes=[pltpu.VMEM((8, N, 128), F32)],
        compiler_params=pltpu.CompilerParams(vmem_limit_bytes=40 << 20),
        cost_estimate=pl.CostEstimate(flops=1_000_000_000, bytes_accessed=10_000_000, transcendentals=0),
        name="solve",
    )(first, recv, mine.reshape(8 * N, 128), *tables, *folds, *z_tables)
    fields = exchange(field.reshape(N, 8, 128))

    plane = lax.dynamic_slice_in_dim(ext_pot, owner, 1, 0).astype(F32)
    plane = plane.reshape(2, B, 2, B).transpose(0, 2, 1, 3).reshape(4, 8, 128)
    potential = plane - EXCHANGE_COEF * jnp.cbrt(jnp.sum(densities, axis=0))

    gradient = pl.pallas_call(
        gradient_kernel,
        out_shape=shape((N, 8, 128)),
        in_specs=[SM] + [VM] * 4,
        out_specs=VM,
        scratch_shapes=[pltpu.VMEM((N, 8, 128), F32)],
        name="gradient_planes",
    )(pairs, phi, code, fields, potential)
    back = exchange(gradient)

    return pl.pallas_call(
        unpack_kernel,
        out_shape=shape((1, BZ, B * B)),
        in_specs=[SM, VM],
        out_specs=VM,
        name="unpack",
    )(offsets, back.reshape(8 * N, 128))


def solution(mesh):
    spec = P(("grp", "own"), None, None)
    in_specs = (spec, P(("grp", "own"), None), P("grp", None), P())
    return jax.shard_map(body, mesh=mesh, in_specs=in_specs, out_specs=spec, check_vma=False)
```

profile of v0, /device:TPU:2, one launch (start us, length us, event | category | flops | bytes accessed | tf_op | source)
XLA Modules:
  0.0 95.0 jit_solution(17480674703545133195)
XLA Ops:
  0.0 1.6 %pack.1 = bf16[32,16,128]{2,1,0:T(8,128)(2,1)} custom-call(s32[1,2]{1,0:T(1,128)} %offsets.3, bf16[1,32,1024]{2,1,0:T(8,128)(2,1)} %box.1), custom_call_target="tpu_custom_call" | custom-call | tf_op jit(solution)/shard_map/pack/pallas_call | solution.py:290
  1.6 11.5 %all-to-all-start = ((bf16[32,16,128]{2,1,0:T(8,128)(2,1)}), bf16[32,16,128]{2,1,0:T(8,128)(2,1)S(1)}, u32[]{:S(2)}, u32[]{:S(2)}) async-start(bf16[32,16,128]{2,1,0:T(8,128)(2,1)} %pack.1), calls=%async_computation | async-start | bytes 262144 | tf_op jit(solution)/shard_map/all_to_all | solution.py:283
  13.1 1.4 %copy.15.pairs = s32[32,2]{1,0:T(8,128)} copy(s32[32,2]{0,1:T(2,128)} %param.14) | data formatting | bytes 512 | tf_op args[2]
  14.5 9.1 %all-to-all-done.recv = bf16[32,16,128]{2,1,0:T(8,128)(2,1)S(1)} async-done(((bf16[32,16,128]{2,1,0:T(8,128)(2,1)}), bf16[32,16,128]{2,1,0:T(8,128)(2,1)S(1)}, u32[]{:S(2)}, u32[]{:S(2)}) %all-to-all-start) | async-done | bytes 131104 | tf_op jit(solution)/shard_map/all_to_all | solution.py:283
  23.6 0.0 copy-start
  23.6 0.7 copy-done
  24.2 1.8 %pair_products.1 = (f32[32,8,128]{2,1,0:T(8,128)}, f32[8,4,8,128]{3,2,1,0:T(8,128)}, f32[32,8,128]{2,1,0:T(8,128)}, f32[32,8,128]{2,1,0:T(8,128)}) custom-call(s32[32,2]{1,0:T(8,128)} %copy.15.pairs, bf16[32,16,128]{2,1,0:T(8,128)(2,1)} %copy-done), custom_call_target="tpu_custom_call" | custom-call | tf_op jit(solution)/shard_map/pair_products/pallas_call | solution.py:316
  26.1 3.8 %all-to-all-start.1 = ((f32[32,8,128]{2,1,0:T(8,128)}), f32[32,8,128]{2,1,0:T(8,128)S(1)}, u32[]{:S(2)}, u32[]{:S(2)}) async-start(f32[32,8,128]{2,1,0:T(8,128)} %get-tuple-element.16), calls=%async_computation.1 | async-start | bytes 262144 | tf_op jit(solution)/shard_map/all_to_all | solution.py:283
  29.9 10.6 %all-to-all-done.1 = f32[32,8,128]{2,1,0:T(8,128)S(1)} async-done(((f32[32,8,128]{2,1,0:T(8,128)}), f32[32,8,128]{2,1,0:T(8,128)S(1)}, u32[]{:S(2)}, u32[]{:S(2)}) %all-to-all-start.1) | async-done | bytes 131104 | tf_op jit(solution)/shard_map/all_to_all | solution.py:283
  40.5 4.8 %all-to-all-start.3 = ((f32[8,4,8,128]{3,2,1,0:T(8,128)}), f32[8,4,8,128]{3,2,1,0:T(8,128)S(1)}, u32[]{:S(2)}, u32[]{:S(2)}) async-start(f32[8,4,8,128]{3,2,1,0:T(8,128)} %get-tuple-element.22), calls=%async_computation.3 | async-start | bytes 262144 | tf_op jit(solution)/shard_map/all_to_all | solution.py:330
  45.4 0.7 constant_dynamic-slice_fusion
  46.1 0.5 slice.3
  46.6 0.0 copy-start.4
  46.6 0.9 copy-done.4
  47.5 0.0 copy-start.5
  47.6 0.9 copy-done.5
  48.5 0.0 copy-start.6
  48.5 0.8 copy-done.6
  49.3 0.0 copy-start.7
  49.3 0.8 copy-done.7
  50.1 1.5 %tables.1 = (bf16[4,256,1024]{2,1,0:T(8,128)(2,1)S(1)}, bf16[4,256,1024]{2,1,0:T(8,128)(2,1)S(1)}, bf16[4,1024,256]{2,1,0:T(8,128)(2,1)S(1)}, bf16[4,1024,256]{2,1,0:T(8,128)(2,1)S(1)}, f32[4,64,1024]{2,1,0:T(8,128)S(1)}) custom-call(f32[2,16,1024]{2,1,0:T(8,128)S(1)} %copy-done.5, f32[2,16,1024]{2,1,0:T(8,128)S(1)} %copy-done.4, ...), custom_call_target="tpu_custom_call" | custom-call | flops 20000000 | bytes 10000000 | tf_op jit(solution)/shard_map/tables/pallas_call | solution.py:300
  51.6 0.0 copy-start.1
  51.6 0.9 copy-done.1
  52.5 0.0 copy-start.2
  52.5 0.9 copy-done.2
  53.4 0.0 copy-start.3
  53.4 0.9 copy-done.3
  54.4 0.0 copy-start.8
  54.4 0.7 copy-done.8
  55.1 0.0 copy-start.9
  55.1 0.7 copy-done.9
  55.8 4.7 %solve.1 = f32[256,128]{1,0:T(8,128)} custom-call(s32[1]{0:T(128)} %bitcast.first, bf16[32,16,128]{2,1,0:T(8,128)(2,1)S(1)} %copy-done.1, f32[256,128]{1,0:T(8,128)S(1)} %bitcast.9, bf16[4,256,1024]{2,1,0:T(8,128)(2,1)S(1)} %get-tuple-element.17.ahead_hi, bf16[4,256,1024]{2,1,0:T(8,128)(2,1)S(1)} %get-tuple-element.18.ahead_lo, ...), custom_call_target="tpu_custom_call" | custom-call | flops 1000000000 | bytes 10000000 | tf_op jit(solution)/shard_map/solve/pallas_call | solution.py:332
  60.5 0.0 all-to-all-done.3
  60.5 3.9 %all-to-all-start.2 = ((f32[32,8,128]{2,1,0:T(8,128)}), f32[32,8,128]{2,1,0:T(8,128)S(1)}, u32[]{:S(2)}, u32[]{:S(2)}) async-start(f32[32,8,128]{2,1,0:T(8,128)} %bitcast.2), calls=%async_computation.2 | async-start | bytes 262144 | tf_op jit(solution)/shard_map/all_to_all | solution.py:283
  64.4 0.9 convert_reduce_fusion
  65.3 0.1 reshape.29
  65.4 0.1 reshape.26
  65.5 0.6 multiply_subtract_fusion.pot
  66.1 9.4 %all-to-all-done.2.field = f32[32,8,128]{2,1,0:T(8,128)S(1)} async-done(((f32[32,8,128]{2,1,0:T(8,128)}), f32[32,8,128]{2,1,0:T(8,128)S(1)}, u32[]{:S(2)}, u32[]{:S(2)}) %all-to-all-start.2) | async-done | bytes 131104 | tf_op jit(solution)/shard_map/all_to_all | solution.py:283
  75.5 0.0 copy-start.10
  75.5 0.7 copy-done.10
  76.2 2.0 %gradient_planes.1 = f32[32,8,128]{2,1,0:T(8,128)} custom-call(s32[32,2]{1,0:T(8,128)} %copy.15.pairs, f32[32,8,128]{2,1,0:T(8,128)} %get-tuple-element.14.phi, f32[32,8,128]{2,1,0:T(8,128)} %get-tuple-element.15.code, f32[32,8,128]{2,1,0:T(8,128)} %copy-done.10, f32[4,8,128]{2,1,0:T(8,128)} %multiply_subtract_fusion.pot), custom_call_target="tpu_custom_call" | custom-call | tf_op jit(solution)/shard_map/gradient_planes/pallas_call | solution.py:348
  78.2 15.1 %all_to_all.25 = f32[32,8,128]{2,1,0:T(8,128)} all-to-all(f32[32,8,128]{2,1,0:T(8,128)} %gradient_planes.1), channel_id=1, replica_groups=mesh['grp'=8,'own'=32] {'own'}, dimensions={0} | all-to-all | bytes 262144 | tf_op jit(solution)/shard_map/all_to_all | solution.py:283
  93.3 1.7 %unpack.1 = f32[1,32,1024]{2,1,0:T(8,128)} custom-call(s32[1,2]{1,0:T(1,128)} %offsets.3, f32[256,128]{1,0:T(8,128)} %bitcast.10), custom_call_target="tpu_custom_call" | custom-call | tf_op jit(solution)/shard_map/unpack/pallas_call | solution.py:358
  (2 shorter events, 0.0 us)
Async XLA Ops:
  1.6 21.9 %all-to-all-start = ((bf16[32,16,128]{2,1,0:T(8,128)(2,1)}), bf16[32,16,128]{2,1,0:T(8,128)(2,1)S(1)}, u32[]{:S(2)}, u32[]{:S(2)}) async-start(bf16[32,16,128]{2,1,0:T(8,128)(2,1)} %pack.1), calls=%async_computation | async-start | bytes 262144 | tf_op jit(solution)/shard_map/all_to_all | solution.py:283
  23.6 0.7 copy-start
  26.1 14.5 %all-to-all-start.1 = ((f32[32,8,128]{2,1,0:T(8,128)}), f32[32,8,128]{2,1,0:T(8,128)S(1)}, u32[]{:S(2)}, u32[]{:S(2)}) async-start(f32[32,8,128]{2,1,0:T(8,128)} %get-tuple-element.16), calls=%async_computation.1 | async-start | bytes 262144 | tf_op jit(solution)/shard_map/all_to_all | solution.py:283
  40.5 20.0 %all-to-all-start.3 = ((f32[8,4,8,128]{3,2,1,0:T(8,128)}), f32[8,4,8,128]{3,2,1,0:T(8,128)S(1)}, u32[]{:S(2)}, u32[]{:S(2)}) async-start(f32[8,4,8,128]{3,2,1,0:T(8,128)} %get-tuple-element.22), calls=%async_computation.3 | async-start | bytes 262144 | tf_op jit(solution)/shard_map/all_to_all | solution.py:330
  46.6 0.9 copy-start.4
  47.5 0.9 copy-start.5
  48.5 0.8 copy-start.6
  49.3 0.8 copy-start.7
  51.6 0.9 copy-start.1
  52.5 0.9 copy-start.2
  53.4 0.9 copy-start.3
  54.4 0.7 copy-start.8
  55.1 0.7 copy-start.9
  60.5 15.0 %all-to-all-start.2 = ((f32[32,8,128]{2,1,0:T(8,128)}), f32[32,8,128]{2,1,0:T(8,128)S(1)}, u32[]{:S(2)}, u32[]{:S(2)}) async-start(f32[32,8,128]{2,1,0:T(8,128)} %bitcast.2), calls=%async_computation.2 | async-start | bytes 262144 | tf_op jit(solution)/shard_map/all_to_all | solution.py:283
  75.5 0.7 copy-start.10
where the time goes:
time: 95.9 us; the launch traced here: 95 us
  waiting for transfers between devices  29.1 us (30%)
  starting transfers between devices  24 us (25%)
  blocking collectives  15.1 us (16%)
  Pallas kernels  13.4 us (14%)
  local copies, waits for them, and re-layouts  11.8 us (12%)
  other arithmetic  1.53 us (2%)
    all_to_all x3, waiting for transfers between devices, exchange(): return lax.all_to_all(x, 'own', 0, 0, tiled=True)  29.1 us
    all_to_all x3, starting transfers between devices, exchange(): return lax.all_to_all(x, 'own', 0, 0, tiled=True)  19.2 us
    all_to_all x1, blocking collectives, exchange(): return lax.all_to_all(x, 'own', 0, 0, tiled=True)  15.1 us
    unnamed x23, local copies, waits for them, and re-layouts  10.3 us
    all_to_all x1, starting transfers between devices, body(): densities = lax.all_to_all(dens, 'grp', 0, 0, tiled=True)  4.83 us
    pallas_call x1, Pallas kernels, body(): pl.pallas_call(solve_and_send, out_shape=shape((8 * N, 128)), in_specs=[S...  4.7 us
    pallas_call x1, Pallas kernels, body(): pl.pallas_call(gradient_kernel, out_shape=shape((N, 8, 128)), in_specs=[S...  2.05 us
  transfers between devices with their start and end apart: 4, of which 3 were waited for; matrix products, arithmetic and copies ran while one was open for 5% of the time, Pallas kernels for 7%

commit v1 on v0

--- a/solution.py
+++ b/solution.py
@@ -121,26 +121,30 @@
         square = plane * plane
         for q in range(4):
             total[q] = total[q] + jnp.where(quarter == float(q), square, 0.0)
-    for g in range(8):
-        for q in range(4):
-            dens[g, q] = total[q]
+    for q in range(4):
+        dens[q] = total[q]
     for p in range(N):
-        a = pairs[p, 0]
-        b = pairs[p, 1]
+        a = pairs[0, p]
+        b = pairs[1, p]
         rho[p] = jnp.where(code[a] == code[b], phi[a] * phi[b], 0.0)
 
 
-def table_kernel(rows_y, rows_x, cols_y, cols_x, ahead_hi, ahead_lo, back_hi, back_lo, green):
+def table_kernel(bases, fixed, ahead, back, green):
+    ahead[8, :, :768] = fixed[...]
     for par in range(4):
         py, px = par // 2, par % 2
         for c in range(HALF):
-            high, low = split(rows_y[py, c : c + 1, :] * rows_x[px])
-            ahead_hi[par, c * HALF : (c + 1) * HALF, :] = high
-            ahead_lo[par, c * HALF : (c + 1) * HALF, :] = low
+            row_y = bases[HALF * py + c : HALF * py + c + 1, :]
+            row_x = bases[B + HALF * px : B + HALF * px + HALF, :]
+            high, low = split(row_y * row_x)
+            ahead[2 * par, c * HALF : (c + 1) * HALF, :] = high
+            ahead[2 * par + 1, c * HALF : (c + 1) * HALF, :] = low
         for k in range(B):
-            high, low = split(cols_y[py, k : k + 1, :] * cols_x[px])
-            back_hi[par, k * B : (k + 1) * B, :] = high
-            back_lo[par, k * B : (k + 1) * B, :] = low
+            col_y = bases[2 * B + k : 2 * B + k + 1, 256 * py : 256 * py + 256]
+            col_x = bases[2 * B :, 512 + 256 * px : 768 + 256 * px]
+            high, low = split(col_y * col_x)
+            back[par, 0, k * B : (k + 1) * B, :] = high
+            back[par, 1, k * B : (k + 1) * B, :] = low
         kz = lax.broadcasted_iota(jnp.int32, (G, B * B), 0)
         pos = lax.broadcasted_iota(jnp.int32, (G, B * B), 1)
         kz = jnp.where(kz >= B, kz - (B - 1), kz)
@@ -152,12 +156,28 @@
             weight = jnp.where((k == 0) | (k == B), weight * 0.5, weight)
             wave = 2.0 * math.pi / G * k.astype(F32)
             squares = squares + wave * wave
-        green[par] = weight / squares
+        green[par, :G, :] = weight / squares
 
 
 def solve_kernel(
-    first, recv, rho, ahead_hi, ahead_lo, back_hi, back_lo, green, fold, unfold, z_ahead, z_back, out
+    first, recv, rho, dens, other, ahead_in, back_in, green_in,
+    out, summed, fixed, ahead, back, green, boxed, sems,
 ):
+    fetch = pltpu.make_async_copy(ahead_in.at[8], fixed, sems.at[4, 0])
+    fetch.start()
+    copies = []
+    for par in range(4):
+        for t, (source, target) in enumerate(
+            (
+                (ahead_in.at[pl.ds(2 * par, 2)], ahead.at[par]),
+                (green_in.at[par, pl.ds(0, G)], green.at[par]),
+                (back_in.at[par], back.at[par]),
+            )
+        ):
+            copy = pltpu.make_async_copy(source, target, sems.at[par, t])
+            copy.start()
+            copies.append(copy)
+    summed[...] = dens[...] + other[...]
     place = recv[first[0]].astype(F32)
     oy = jnp.max(place[8:9, :]).astype(jnp.int32)
     ox = jnp.max(place[9:10, :]).astype(jnp.int32)
@@ -165,11 +185,16 @@
     lane = lax.broadcasted_iota(jnp.int32, (N, 128), 1)
     low_half = lane < 64
 
+    fetch.wait()
+    fold = fixed[:, :256]
+    unfold = fixed[:, 256:512]
+    z_ahead = fixed[:G, 512:608]
+    z_back = fixed[G : G + N, 512:704]
     stacked = jnp.concatenate(
         [jnp.concatenate([chunks[s], chunks[7 - s]], axis=1) for s in range(4)], axis=0
     )
     high, low = split(stacked)
-    folded = dot(high, fold[...]) + dot(low, fold[...])
+    folded = dot(high, fold) + dot(low, fold)
 
     def regroup(tile, par_low, parts):
         first_part, second_part = parts
@@ -185,15 +210,18 @@
             [regroup(t, par % 2 == 0, pieces[2 * t : 2 * t + 2]) for t in range(2)], axis=1
         )
         high, low = split(data)
-        both = dot(jnp.concatenate([high, low], axis=0), ahead_hi[par])
-        plane_waves = both[:N] + both[N:] + dot(high, ahead_lo[par])
+        copies[3 * par].wait()
+        both = dot(jnp.concatenate([high, low], axis=0), ahead[par, 0])
+        plane_waves = both[:N] + both[N:] + dot(high, ahead[par, 1])
         high, low = split(plane_waves)
-        waves = dot(z_ahead[...], jnp.concatenate([high, high, low], axis=0)) * green[par]
+        copies[3 * par + 1].wait()
+        waves = dot(z_ahead, jnp.concatenate([high, high, low], axis=0)) * green[par]
         high, low = split(waves)
-        back = dot(z_back[...], jnp.concatenate([high, high, low], axis=0))
-        high, low = split(back)
-        both = dot(jnp.concatenate([high, low], axis=0), back_hi[par])
-        solved.append(both[:N] + both[N:] + dot(high, back_lo[par]))
+        levels = dot(z_back, jnp.concatenate([high, high, low], axis=0))
+        high, low = split(levels)
+        copies[3 * par + 2].wait()
+        both = dot(jnp.concatenate([high, low], axis=0), back[par, 0])
+        solved.append(both[:N] + both[N:] + dot(high, back[par, 1]))
 
     rows = []
     for s in range(4):
@@ -205,20 +233,10 @@
             tiles.append(regroup(half, s % 2 == 0, (even, odd)))
         rows.append(jnp.concatenate(tiles, axis=1))
     high, low = split(jnp.concatenate(rows, axis=0))
-    spread = dot(high, unfold[...]) + dot(low, unfold[...])
+    spread = dot(high, unfold) + dot(low, unfold)
     field = [spread[N * s : N * s + N, :128] for s in range(4)] + [
         spread[N * s : N * s + N, 128:] for s in range(3, -1, -1)
     ]
-    chunk_store = out
-    return field, oy, ox, chunk_store
-
-
-def solve_and_send(
-    first, recv, rho, ahead_hi, ahead_lo, back_hi, back_lo, green, fold, unfold, z_ahead, z_back, out, boxed
-):
-    field, oy, ox, _ = solve_kernel(
-        first, recv, rho, ahead_hi, ahead_lo, back_hi, back_lo, green, fold, unfold, z_ahead, z_back, out
-    )
     for s in range(8):
         boxed[s] = field[s]
     chunks = torus_roll(lambda c: boxed[c], B - lax.rem(oy, B), B - lax.rem(ox, B))
@@ -226,16 +244,25 @@
         out[pl.ds(s, N, stride=8), :] = chunks[s]
 
 
-def gradient_kernel(pairs, phi, code, field, pot, out, terms):
+def cube_root(value):
+    rough = jnp.exp(jnp.log(jnp.where(value > 0.0, value, 1.0)) * (1.0 / 3.0))
+    finer = rough - (rough - value / (rough * rough)) * (1.0 / 3.0)
+    return jnp.where(value > 0.0, finer, 0.0)
+
+
+def gradient_kernel(pairs, phi, code, field, plane, dens, near, far, nearer, out, terms):
     for n in range(N):
         terms[n] = jnp.zeros((8, 128), F32)
     for p in range(N):
-        a = pairs[p, 0]
-        b = pairs[p, 1]
+        a = pairs[0, p]
+        b = pairs[1, p]
         value = jnp.where(code[a] == code[b], field[p], 0.0)
         terms[a] = terms[a] + value * phi[b]
         terms[b] = terms[b] + value * phi[a]
-    quarters = [pot[q] for q in range(4)]
+    quarters = []
+    for q in range(4):
+        density = (dens[q] + far[q]) + (near[q] + nearer[q])
+        quarters.append(plane[q] - EXCHANGE_COEF * cube_root(density))
     for n in range(N):
         quarter = code[n]
         local = jnp.where(
@@ -269,98 +296,124 @@
     z_basis = np.concatenate([cosine, sine], axis=1)
     ahead_hi, ahead_lo = np_split(z_basis.T)
     back_hi, back_lo = np_split(z_basis)
-    return (
-        [jnp.asarray(t.astype(np.float32)) for t in (rows_y, rows_x, cols_y, cols_x)],
-        [jnp.asarray(t, BF16) for t in (fold, fold.T)],
+    fixed = np.zeros((256, 768), jnp.bfloat16)
+    fixed[:, :256] = fold
+    fixed[:, 256:512] = fold.T
+    fixed[:G, 512:608] = np.concatenate([ahead_hi, ahead_lo, ahead_hi], axis=1)
+    fixed[G : G + N, 512:704] = np.concatenate([back_hi, back_lo, back_hi], axis=1)
+    packed = np.concatenate(
         [
-            jnp.asarray(np.concatenate([ahead_hi, ahead_lo, ahead_hi], axis=1)),
-            jnp.asarray(np.concatenate([back_hi, back_lo, back_hi], axis=1)),
-        ],
-    )
+            rows_y.reshape(B, 1024),
+            rows_x.reshape(B, 1024),
+            np.concatenate([*cols_y, *cols_x], axis=1),
+        ]
+    )
+    return jnp.asarray(packed.astype(np.float32)), jnp.asarray(fixed)
 
 
 def exchange(x):
     return lax.all_to_all(x, "own", 0, 0, tiled=True)
 
 
+def kernel(call, out_shape, in_specs, name, vmem, scratch=(), flops=0, moved=0):
+    many = isinstance(out_shape, list)
+    return pl.pallas_call(
+        call,
+        out_shape=out_shape,
+        in_specs=in_specs,
+        out_specs=[VM] * len(out_shape) if many else VM,
+        scratch_shapes=scratch,
+        compiler_params=pltpu.CompilerParams(vmem_limit_bytes=vmem << 20),
+        cost_estimate=pl.CostEstimate(flops=flops, bytes_accessed=moved, transcendentals=0),
+        name=name,
+    )
+
+
+def from_group(x, step):
+    if step == 1:
+        return lax.ppermute(x, "grp", [(g, g ^ 1) for g in range(8)])
+    return lax.ppermute(x, "grp", [(g, (g + step) % 8) for g in range(8)])
+
+
 def body(orbitals, offsets, pairs, ext_pot):
     owner = lax.axis_index("own")
-    bases, folds, z_tables = constants()
-
-    sent = pl.pallas_call(
+    bases, fixed = constants()
+    pairs = pairs.T
+
+    sent = kernel(
         pack_kernel,
-        out_shape=shape((N, 16, 128), BF16),
-        in_specs=[SM, VM],
-        out_specs=VM,
-        scratch_shapes=[pltpu.VMEM((8 * N, 128), F32)],
-        name="pack",
+        shape((N, 16, 128), BF16),
+        [SM, VM],
+        "pack",
+        60,
+        [pltpu.VMEM((8 * N, 128), F32)],
+        moved=200_000,
     )(offsets, orbitals)
+    sent, bases, pairs, ext_pot = lax.optimization_barrier((sent, bases, pairs, ext_pot))
     recv = exchange(sent)
 
-    tables = pl.pallas_call(
+    tables = kernel(
         table_kernel,
-        out_shape=[
-            shape((4, 256, 1024), BF16),
-            shape((4, 256, 1024), BF16),
-            shape((4, 1024, 256), BF16),
-            shape((4, 1024, 256), BF16),
-            shape((4, G, 1024)),
-        ],
-        in_specs=[VM] * 4,
-        out_specs=[VM] * 5,
-        compiler_params=pltpu.CompilerParams(vmem_limit_bytes=40 << 20),
-        cost_estimate=pl.CostEstimate(flops=20_000_000, bytes_accessed=10_000_000, transcendentals=0),
-        name="tables",
-    )(*bases)
-
-    rho, dens, phi, code = pl.pallas_call(
-        pair_kernel,
-        out_shape=[
-            shape((N, 8, 128)),
-            shape((8, 4, 8, 128)),
-            shape((N, 8, 128)),
-            shape((N, 8, 128)),
-        ],
-        in_specs=[SM, VM],
-        out_specs=[VM] * 4,
-        name="pair_products",
-    )(pairs, recv)
-
-    mine = exchange(rho)
-    densities = lax.all_to_all(dens, "grp", 0, 0, tiled=True)
-    first = lax.dynamic_slice_in_dim(pairs, owner, 1, 0)[0, :1]
-    field = pl.pallas_call(
-        solve_and_send,
-        out_shape=shape((8 * N, 128)),
-        in_specs=[SM] + [VM] * 11,
-        out_specs=VM,
-        scratch_shapes=[pltpu.VMEM((8, N, 128), F32)],
-        compiler_params=pltpu.CompilerParams(vmem_limit_bytes=40 << 20),
-        cost_estimate=pl.CostEstimate(flops=1_000_000_000, bytes_accessed=10_000_000, transcendentals=0),
-        name="solve",
-    )(first, recv, mine.reshape(8 * N, 128), *tables, *folds, *z_tables)
-    fields = exchange(field.reshape(N, 8, 128))
-
+        [shape((9, 256, 1024), BF16), shape((4, 2, 1024, 256), BF16), shape((4, 2 * G, 1024))],
+        [VM, VM],
+        "tables",
+        60,
+        flops=20_000_000,
+        moved=10_000_000,
+    )(bases, fixed)
+    first = lax.dynamic_slice_in_dim(pairs, owner, 1, 1)[:1, 0]
     plane = lax.dynamic_slice_in_dim(ext_pot, owner, 1, 0).astype(F32)
     plane = plane.reshape(2, B, 2, B).transpose(0, 2, 1, 3).reshape(4, 8, 128)
-    potential = plane - EXCHANGE_COEF * jnp.cbrt(jnp.sum(densities, axis=0))
-
-    gradient = pl.pallas_call(
+    pairs = jnp.clip(pairs, 0, N - 1)
+    recv, tables, first, plane, pairs = lax.optimization_barrier(
+        (recv, tables, first, plane, pairs)
+    )
+
+    rho, dens, phi, code = kernel(
+        pair_kernel,
+        [shape((N, 8, 128)), shape((4, 8, 128)), shape((N, 8, 128)), shape((N, 8, 128))],
+        [SM, VM],
+        "pair_products",
+        4,
+        moved=600_000,
+    )(pairs, recv)
+
+    mine = exchange(rho)
+    other = from_group(dens, 1)
+    hbm = pl.BlockSpec(memory_space=pltpu.HBM)
+    field, chip_dens = kernel(
+        solve_kernel,
+        [shape((8 * N, 128)), shape((4, 8, 128))],
+        [SM] + [VM] * 4 + [hbm] * 3,
+        "solve",
+        52,
+        [
+            pltpu.VMEM((256, 1024), BF16),
+            pltpu.VMEM((4, 2, 256, 1024), BF16),
+            pltpu.VMEM((4, 2, 1024, 256), BF16),
+            pltpu.VMEM((4, G, 1024), F32),
+            pltpu.VMEM((8, N, 128), F32),
+            pltpu.SemaphoreType.DMA((5, 3)),
+        ],
+        flops=1_000_000_000,
+        moved=10_000_000,
+    )(first, recv, mine.reshape(8 * N, 128), dens, other, *tables)
+    fields = exchange(field.reshape(N, 8, 128))
+    others = [from_group(chip_dens, step) for step in (2, 4, 6)]
+
+    gradient = kernel(
         gradient_kernel,
-        out_shape=shape((N, 8, 128)),
-        in_specs=[SM] + [VM] * 4,
-        out_specs=VM,
-        scratch_shapes=[pltpu.VMEM((N, 8, 128), F32)],
-        name="gradient_planes",
-    )(pairs, phi, code, fields, potential)
+        shape((N, 8, 128)),
+        [SM] + [VM] * 8,
+        "gradient_planes",
+        4,
+        [pltpu.VMEM((N, 8, 128), F32)],
+        moved=600_000,
+    )(pairs, phi, code, fields, plane, chip_dens, *others)
     back = exchange(gradient)
 
-    return pl.pallas_call(
-        unpack_kernel,
-        out_shape=shape((1, BZ, B * B)),
-        in_specs=[SM, VM],
-        out_specs=VM,
-        name="unpack",
+    return kernel(
+        unpack_kernel, shape((1, BZ, B * B)), [SM, VM], "unpack", 4, moved=300_000
     )(offsets, back.reshape(8 * N, 128))
 
 

time: 95.9 us -> 85.8 us (0.89)
  waiting for transfers between devices: 29.1 us -> 17.6 us
  local copies, waits for them, and re-layouts: 11.8 us -> 1.46 us
  Pallas kernels: 13.4 us -> 18.9 us
  starting transfers between devices: 24 us -> 28.6 us
  blocking collectives: 15.1 us -> 16.3 us
    all_to_all x3, waiting for transfers between devices: 29.1 us -> 14.5 us  [exchange(): return lax.all_to_all(x, 'own', 0, 0, tiled=True)]
    unnamed x23 -> x2, local copies, waits for them, and re-layouts: 10.3 us -> 0.01 us
    pallas_call x6, Pallas kernels: 13.4 us -> 18.9 us  [the longest x1 7.82 us: body(): kernel(solve_kernel, [shape((8 * N, 128)), shape((4, 8, 128))], [SM] + [V...]
    ppermute x0 -> x4, starting transfers between devices: none -> 4.92 us  [the longest x3 4.83 us: from_group(): return lax.ppermute(x, 'grp', [(g, (g + step) % 8) for g in range(8)])]
    all_to_all x1 -> x0, starting transfers between devices: 4.83 us -> none  [body(): densities = lax.all_to_all(dens, 'grp', 0, 0, tiled=True)]
    all_to_all x3, starting transfers between devices: 19.2 us -> 23.6 us  [exchange(): return lax.all_to_all(x, 'own', 0, 0, tiled=True)]
    ppermute x0 -> x4, waiting for transfers between devices: none -> 3.11 us  [the longest x3 1.94 us: from_group(): return lax.ppermute(x, 'grp', [(g, (g + step) % 8) for g in range(8)])]
    all_to_all x1, blocking collectives: 15.1 us -> 16.3 us  [exchange(): return lax.all_to_all(x, 'own', 0, 0, tiled=True)]
  transfers between devices with their start and end apart: 4 -> 7, of which waited for: 3 -> 6; matrix products, arithmetic and copies ran while one was open for 5% -> 4% of each run, Pallas kernels for 7% -> 7%
where the time goes in v1:
time: 85.8 us; the launch traced here: 84.5 us
  starting transfers between devices  28.6 us (33%)
  Pallas kernels  18.9 us (22%)
  waiting for transfers between devices  17.6 us (21%)
  blocking collectives  16.3 us (19%)
  other arithmetic  1.57 us (2%)
  local copies, waits for them, and re-layouts  1.46 us (2%)
    all_to_all x3, starting transfers between devices, exchange(): return lax.all_to_all(x, 'own', 0, 0, tiled=True)  23.6 us
    all_to_all x1, blocking collectives, exchange(): return lax.all_to_all(x, 'own', 0, 0, tiled=True)  16.3 us
    all_to_all x3, waiting for transfers between devices, exchange(): return lax.all_to_all(x, 'own', 0, 0, tiled=True)  14.5 us
    pallas_call x1, Pallas kernels, body(): kernel(solve_kernel, [shape((8 * N, 128)), shape((4, 8, 128))], [SM] + [V...  7.82 us
    pallas_call x1, Pallas kernels, body(): kernel(table_kernel, [shape((9, 256, 1024), BF16), shape((4, 2, 1024, 256...  5.91 us
    ppermute x3, starting transfers between devices, from_group(): return lax.ppermute(x, 'grp', [(g, (g + step) % 8) for g in range(8)])  4.83 us
    ppermute x3, waiting for transfers between devices, from_group(): return lax.ppermute(x, 'grp', [(g, (g + step) % 8) for g in range(8)])  1.94 us
  transfers between devices with their start and end apart: 7, of which 6 were waited for; matrix products, arithmetic and copies ran while one was open for 4% of the time, Pallas kernels for 7%

profile of v1, /device:TPU:2, one launch (start us, length us, event | category | flops | bytes accessed | tf_op | source)
XLA Modules:
  0.0 84.5 jit_solution(8456317319914608968)
XLA Ops:
  0.0 1.6 %pack.1 = bf16[32,16,128]{2,1,0:T(8,128)(2,1)} custom-call(s32[1,2]{1,0:T(1,128)} %offsets.3, bf16[1,32,1024]{2,1,0:T(8,128)(2,1)} %box.1), custom_call_target="tpu_custom_call" | custom-call | bytes 200000 | tf_op jit(solution)/shard_map/pack/pallas_call | solution.py:343
  1.6 11.5 %all-to-all-start = ((bf16[32,16,128]{2,1,0:T(8,128)(2,1)}), bf16[32,16,128]{2,1,0:T(8,128)(2,1)S(1)}, u32[]{:S(2)}, u32[]{:S(2)}) async-start(bf16[32,16,128]{2,1,0:T(8,128)(2,1)} %pack.1), calls=%async_computation | async-start | bytes 262144 | tf_op jit(solution)/shard_map/all_to_all | solution.py:315
  13.1 0.8 constant_dynamic-slice_fusion
  13.9 0.5 slice.3
  14.4 0.9 %convert_reduce_fusion = f32[4096]{0:T(1024)S(1)} fusion(bf16[32,4096]{1,0:T(8,128)(2,1)} %param.9, s32[]{:T(128)S(6)} %select_n.4), kind=kLoop, calls=%fused_computation.1 | loop fusion | flops 4096 | bytes 24580 | tf_op jit(solution)/shard_map/reshape | solution.py:366
  15.3 0.1 reshape.29
  15.4 0.1 reshape.26.plane
  15.5 5.9 %tables.1 = (bf16[9,256,1024]{2,1,0:T(8,128)(2,1)}, bf16[4,2,1024,256]{3,2,1,0:T(8,128)(2,1)}, f32[4,128,1024]{2,1,0:T(8,128)}) custom-call(f32[96,1024]{1,0:T(8,128)} %constant.14.clone.bases, bf16[256,768]{1,0:T(8,128)(2,1)} %constant.15.clone.fixed), custom_call_target="tpu_custom_call" | custom-call | flops 20000000 | bytes 10000000 | tf_op jit(solution)/shard_map/tables/pallas_call | solution.py:355
  21.4 0.7 broadcast_clamp_fusion.pairs
  22.1 1.5 %all-to-all-done.recv = bf16[32,16,128]{2,1,0:T(8,128)(2,1)S(1)} async-done(((bf16[32,16,128]{2,1,0:T(8,128)(2,1)}), bf16[32,16,128]{2,1,0:T(8,128)(2,1)S(1)}, u32[]{:S(2)}, u32[]{:S(2)}) %all-to-all-start) | async-done | bytes 131104 | tf_op jit(solution)/shard_map/all_to_all | solution.py:315
  23.6 1.4 %pair_products.1 = (f32[32,8,128]{2,1,0:T(8,128)}, f32[4,8,128]{2,1,0:T(8,128)S(1)}, f32[32,8,128]{2,1,0:T(8,128)S(1)}, f32[32,8,128]{2,1,0:T(8,128)S(1)}) custom-call(s32[2,32]{1,0:T(2,128)S(1)} %broadcast_clamp_fusion.pairs, bf16[32,16,128]{2,1,0:T(8,128)(2,1)S(1)} %all-to-all-done.recv), custom_call_target="tpu_custom_call" | custom-call | bytes 600000 | tf_op jit(solution)/shard_map/pair_products/pallas_call | solution.py:372
  25.0 8.3 %all-to-all-start.1 = ((f32[32,8,128]{2,1,0:T(8,128)}), f32[32,8,128]{2,1,0:T(8,128)S(1)}, u32[]{:S(2)}, u32[]{:S(2)}) async-start(f32[32,8,128]{2,1,0:T(8,128)} %get-tuple-element.37), calls=%async_computation.1 | async-start | bytes 262144 | tf_op jit(solution)/shard_map/all_to_all | solution.py:315
  33.3 0.1 collective-permute-start
  33.4 1.2 %collective-permute-done.other = f32[4,8,128]{2,1,0:T(8,128)S(1)} collective-permute-done((f32[4,8,128]{2,1,0:T(8,128)S(1)}, f32[4,8,128]{2,1,0:T(8,128)S(1)}, u32[]{:S(2)}, u32[]{:S(2)}) %collective-permute-start) | collective-permute-done | bytes 16416 | tf_op jit(solution)/shard_map/ppermute | solution.py:334
  34.5 9.3 %all-to-all-done.1 = f32[32,8,128]{2,1,0:T(8,128)S(1)} async-done(((f32[32,8,128]{2,1,0:T(8,128)}), f32[32,8,128]{2,1,0:T(8,128)S(1)}, u32[]{:S(2)}, u32[]{:S(2)}) %all-to-all-start.1) | async-done | bytes 131104 | tf_op jit(solution)/shard_map/all_to_all | solution.py:315
  43.8 0.0 copy-start
  43.8 7.8 %solve.1 = (f32[256,128]{1,0:T(8,128)}, f32[4,8,128]{2,1,0:T(8,128)S(1)}) custom-call(s32[1]{0:T(128)} %bitcast.1.first, bf16[32,16,128]{2,1,0:T(8,128)(2,1)S(1)} %all-to-all-done.recv, f32[256,128]{1,0:T(8,128)S(1)} %bitcast.10, f32[4,8,128]{2,1,0:T(8,128)S(1)} %get-tuple-element.38.dens, f32[4,8,128]{2,1,0:T(8,128)S(1)} %collective-permute-done.other, ...), custom_call_target="tpu_custom_call" | custom-call | flops 1000000000 | bytes 10000000 | tf_op jit(solution)/shard_map/solve/pallas_call | solution.py:384
  51.6 3.9 %all-to-all-start.2 = ((f32[32,8,128]{2,1,0:T(8,128)}), f32[32,8,128]{2,1,0:T(8,128)S(1)}, u32[]{:S(2)}, u32[]{:S(2)}) async-start(f32[32,8,128]{2,1,0:T(8,128)} %bitcast.4), calls=%async_computation.2 | async-start | bytes 262144 | tf_op jit(solution)/shard_map/all_to_all | solution.py:315
  55.5 0.6 collective-permute-start.3
  56.1 2.4 %collective-permute-start.2 = (f32[4,8,128]{2,1,0:T(8,128)S(1)}, f32[4,8,128]{2,1,0:T(8,128)S(1)}, u32[]{:S(2)}, u32[]{:S(2)}) collective-permute-start(f32[4,8,128]{2,1,0:T(8,128)S(1)} %get-tuple-element.44.dens), channel_id=1, source_target_pairs={{0,128},{32,160},{64,192},{96,224},{128,0},{160,32},{192,64},{224,... | collective-permute-start | bytes 49160 | tf_op jit(solution)/shard_map/ppermute | solution.py:335
  58.5 1.8 %collective-permute-start.1 = (f32[4,8,128]{2,1,0:T(8,128)S(1)}, f32[4,8,128]{2,1,0:T(8,128)S(1)}, u32[]{:S(2)}, u32[]{:S(2)}) collective-permute-start(f32[4,8,128]{2,1,0:T(8,128)S(1)} %get-tuple-element.44.dens), channel_id=1, source_target_pairs={{0,64},{32,96},{64,128},{96,160},{128,192},{160,224},{192,0},{224,... | collective-permute-start | bytes 49160 | tf_op jit(solution)/shard_map/ppermute | solution.py:335
  60.3 0.0 collective-permute-done.3.nearer
  60.3 1.0 %collective-permute-done.2.far = f32[4,8,128]{2,1,0:T(8,128)S(1)} collective-permute-done((f32[4,8,128]{2,1,0:T(8,128)S(1)}, f32[4,8,128]{2,1,0:T(8,128)S(1)}, u32[]{:S(2)}, u32[]{:S(2)}) %collective-permute-start.2) | collective-permute-done | bytes 16416 | tf_op jit(solution)/shard_map/ppermute | solution.py:335
  61.4 0.9 %collective-permute-done.1.near = f32[4,8,128]{2,1,0:T(8,128)S(1)} collective-permute-done((f32[4,8,128]{2,1,0:T(8,128)S(1)}, f32[4,8,128]{2,1,0:T(8,128)S(1)}, u32[]{:S(2)}, u32[]{:S(2)}) %collective-permute-start.1) | collective-permute-done | bytes 16416 | tf_op jit(solution)/shard_map/ppermute | solution.py:335
  62.3 3.8 %all-to-all-done.2.field = f32[32,8,128]{2,1,0:T(8,128)S(1)} async-done(((f32[32,8,128]{2,1,0:T(8,128)}), f32[32,8,128]{2,1,0:T(8,128)S(1)}, u32[]{:S(2)}, u32[]{:S(2)}) %all-to-all-start.2) | async-done | bytes 131104 | tf_op jit(solution)/shard_map/all_to_all | solution.py:315
  66.1 0.8 gradient_planes.1
  66.9 16.3 %all_to_all.20 = f32[32,8,128]{2,1,0:T(8,128)S(1)} all-to-all(f32[32,8,128]{2,1,0:T(8,128)S(1)} %gradient_planes.1), channel_id=1, replica_groups=mesh['grp'=8,'own'=32] {'own'}, dimensions={0} | all-to-all | bytes 262144 | tf_op jit(solution)/shard_map/all_to_all | solution.py:315
  83.2 0.0 copy-done
  83.2 1.3 %unpack.1 = f32[1,32,1024]{2,1,0:T(8,128)} custom-call(s32[1,2]{1,0:T(1,128)S(1)} %copy-done, f32[256,128]{1,0:T(8,128)S(1)} %bitcast.11), custom_call_target="tpu_custom_call" | custom-call | bytes 300000 | tf_op jit(solution)/shard_map/unpack/pallas_call | solution.py:415
  (1 shorter events, 0.0 us)
Async XLA Ops:
  1.6 21.9 %all-to-all-start = ((bf16[32,16,128]{2,1,0:T(8,128)(2,1)}), bf16[32,16,128]{2,1,0:T(8,128)(2,1)S(1)}, u32[]{:S(2)}, u32[]{:S(2)}) async-start(bf16[32,16,128]{2,1,0:T(8,128)(2,1)} %pack.1), calls=%async_computation | async-start | bytes 262144 | tf_op jit(solution)/shard_map/all_to_all | solution.py:315
  25.0 18.8 %all-to-all-start.1 = ((f32[32,8,128]{2,1,0:T(8,128)}), f32[32,8,128]{2,1,0:T(8,128)S(1)}, u32[]{:S(2)}, u32[]{:S(2)}) async-start(f32[32,8,128]{2,1,0:T(8,128)} %get-tuple-element.37), calls=%async_computation.1 | async-start | bytes 262144 | tf_op jit(solution)/shard_map/all_to_all | solution.py:315
  33.3 1.3 %collective-permute-start = (f32[4,8,128]{2,1,0:T(8,128)S(1)}, f32[4,8,128]{2,1,0:T(8,128)S(1)}, u32[]{:S(2)}, u32[]{:S(2)}) collective-permute-start(f32[4,8,128]{2,1,0:T(8,128)S(1)} %get-tuple-element.38.dens), channel_id=1, source_target_pairs={{0,32},{32,0},{64,96},{96,64},{128,160},{160,128},{192,224},{224,1... | collective-permute-start | bytes 49160 | tf_op jit(solution)/shard_map/ppermute | solution.py:334
  43.8 39.4 %copy-start = (s32[1,2]{1,0:T(1,128)S(1)}, s32[1,2]{1,0:T(1,128)}, u32[]{:S(2)}) copy-start(s32[1,2]{1,0:T(1,128)} %offsets.3) | copy-start | bytes 28
  51.6 14.4 %all-to-all-start.2 = ((f32[32,8,128]{2,1,0:T(8,128)}), f32[32,8,128]{2,1,0:T(8,128)S(1)}, u32[]{:S(2)}, u32[]{:S(2)}) async-start(f32[32,8,128]{2,1,0:T(8,128)} %bitcast.4), calls=%async_computation.2 | async-start | bytes 262144 | tf_op jit(solution)/shard_map/all_to_all | solution.py:315
  55.5 4.8 %collective-permute-start.3 = (f32[4,8,128]{2,1,0:T(8,128)S(1)}, f32[4,8,128]{2,1,0:T(8,128)S(1)}, u32[]{:S(2)}, u32[]{:S(2)}) collective-permute-start(f32[4,8,128]{2,1,0:T(8,128)S(1)} %get-tuple-element.44.dens), channel_id=1, source_target_pairs={{0,192},{32,224},{64,0},{96,32},{128,64},{160,96},{192,128},{224,1... | collective-permute-start | bytes 49160 | tf_op jit(solution)/shard_map/ppermute | solution.py:335
  56.1 5.2 %collective-permute-start.2 = (f32[4,8,128]{2,1,0:T(8,128)S(1)}, f32[4,8,128]{2,1,0:T(8,128)S(1)}, u32[]{:S(2)}, u32[]{:S(2)}) collective-permute-start(f32[4,8,128]{2,1,0:T(8,128)S(1)} %get-tuple-element.44.dens), channel_id=1, source_target_pairs={{0,128},{32,160},{64,192},{96,224},{128,0},{160,32},{192,64},{224,... | collective-permute-start | bytes 49160 | tf_op jit(solution)/shard_map/ppermute | solution.py:335
  58.5 3.7 %collective-permute-start.1 = (f32[4,8,128]{2,1,0:T(8,128)S(1)}, f32[4,8,128]{2,1,0:T(8,128)S(1)}, u32[]{:S(2)}, u32[]{:S(2)}) collective-permute-start(f32[4,8,128]{2,1,0:T(8,128)S(1)} %get-tuple-element.44.dens), channel_id=1, source_target_pairs={{0,64},{32,96},{64,128},{96,160},{128,192},{160,224},{192,0},{224,... | collective-permute-start | bytes 49160 | tf_op jit(solution)/shard_map/ppermute | solution.py:335

commit v2 on v1

v2 whole, which is shorter than its diff:
```python
import math

import jax
import jax.numpy as jnp
import numpy as np
from jax import lax
from jax.experimental import pallas as pl
from jax.experimental.pallas import tpu as pltpu
from jax.sharding import PartitionSpec as P

B = 32
BZ = 32
G = 64
N = 32
SCREEN = 0.0025
MIXING = 0.25
EXCHANGE_COEF = (3.0 / math.pi) ** (1.0 / 3.0)
F32 = jnp.float32
BF16 = jnp.bfloat16
VM = pl.BlockSpec(memory_space=pltpu.VMEM)
SM = pl.BlockSpec(memory_space=pltpu.SMEM)


def axis_basis():
    position = np.arange(B) - 15.5
    cosine = np.cos(2 * np.pi / G * np.outer(position, np.arange(B)))
    sine = np.sin(2 * np.pi / G * np.outer(position, np.arange(1, B + 1)))
    return cosine, sine


def split(value):
    high = value.astype(BF16)
    low = (value - high.astype(F32)).astype(BF16)
    return high, low


def np_split(value):
    value = value.astype(np.float32)
    high = value.astype(jnp.bfloat16)
    low = (value - high.astype(np.float32)).astype(jnp.bfloat16)
    return high, low


def dot(a, b):
    return jnp.dot(a, b, preferred_element_type=F32)


def torus_roll(load, by_y, by_x):
    lane = lax.broadcasted_iota(jnp.int32, (N, 128), 1)
    by_y = lax.rem(by_y, B)
    by_x = lax.rem(by_x, B)
    rows = lax.div(by_y, 4)
    rest = lax.rem(by_y, 4)
    shift = rest * B + by_x
    near = lax.rem(128 - shift, 128)
    far = lax.rem(128 + B - shift, 128)
    inside = lax.rem(lane, B) < B - by_x
    same = lax.div(lane, B) < 4 - rest
    moved = []
    for s in range(8):
        chunk = load(lax.rem(rows + s, 8))
        moved.append(
            jnp.where(inside, pltpu.roll(chunk, near, 1), pltpu.roll(chunk, far, 1))
        )
    return [jnp.where(same, moved[s], moved[(s + 1) % 8]) for s in range(8)]


def pack_kernel(offsets, box, out, planes):
    oy = offsets[0, 0]
    ox = offsets[0, 1]

    def load(c):
        return box[0, :, pl.ds(pl.multiple_of(c * 128, 128), 128)].astype(F32)

    chunks = torus_roll(load, B - lax.rem(oy, B), B - lax.rem(ox, B))
    for s in range(8):
        planes[pl.ds(s, N, stride=8), :] = chunks[s]
    row = lax.broadcasted_iota(jnp.int32, (8, 128), 0)
    extra = jnp.where(
        row == 0, oy.astype(F32), jnp.where(row == 1, ox.astype(F32), 0.0)
    )
    for z in range(N):
        both = jnp.concatenate([planes[8 * z : 8 * z + 8, :], extra], axis=0)
        out[z] = both.astype(BF16)


def pair_kernel(pairs, recv, rho, dens, phi, code):
    row = lax.broadcasted_iota(jnp.int32, (8, 128), 0)
    lane = lax.broadcasted_iota(jnp.int32, (8, 128), 1)
    y = (row * 4 + lax.div(lane, B)).astype(F32)
    x = lax.rem(lane, B).astype(F32)
    total = [jnp.zeros((8, 128), F32) for _ in range(4)]
    for n in range(N):
        value = recv[n].astype(F32)
        plane = value[:8]
        below = jnp.where(y < value[8:9], 2.0, 0.0)
        quarter = below + jnp.where(x < value[9:10], 1.0, 0.0)
        phi[n] = plane
        code[n] = quarter
        square = plane * plane
        for q in range(4):
            total[q] = total[q] + jnp.where(quarter == float(q), square, 0.0)
    for q in range(4):
        dens[q] = total[q]
    for p in range(N):
        a = pairs[0, p]
        b = pairs[1, p]
        rho[p] = jnp.where(code[a] == code[b], phi[a] * phi[b], 0.0)


def wave(index):
    return jnp.where(index < B, index, index - (B - 1))


def weigh(index, value):
    k = wave(index)
    return jnp.where((k == 0) | (k == B), value * 0.5, value)


def square(index):
    k = 2.0 * math.pi / G * wave(index).astype(F32)
    return k * k


def table_kernel(fixed_in, pairs_in, offsets_in, fixed, pairs, offsets, green):
    fixed[...] = fixed_in[...]
    pairs[...] = pairs_in[...]
    offsets[...] = offsets_in[...]
    ky = lax.broadcasted_iota(jnp.int32, (G, 256), 0)
    lane = lax.broadcasted_iota(jnp.int32, (G, 256), 1)
    kx = lax.rem(lane, G)
    level = square(ky) + square(kx) + SCREEN
    weight = weigh(ky, weigh(kx, jnp.full((G, 256), 4.0 * math.pi * 8.0 / G**3, F32)))
    top = lax.div(lax.broadcasted_iota(jnp.int32, (8, 256), 1), G)
    for part in range(16):
        kz = top + 4 * part
        factor = weigh(kz, jnp.ones((8, 256), F32))[:1]
        green[G * part : G * part + G, :] = weight * factor / (level + square(kz)[:1])


def exchange_groups(tiles):
    group = lax.div(lax.broadcasted_iota(jnp.int32, (8, 128), 1), B)
    low = group < 2
    even = lax.rem(group, 2) == 0
    t0, t1, t2, t3 = tiles

    def far(first, second):
        return (
            jnp.where(low, first, pltpu.roll(second, 64, 1)),
            jnp.where(low, pltpu.roll(first, 64, 1), second),
        )

    def near(first, second):
        return (
            jnp.where(even, first, pltpu.roll(second, 32, 1)),
            jnp.where(even, pltpu.roll(first, 96, 1), second),
        )

    u0, u2 = far(t0, t2)
    u1, u3 = far(t1, t3)
    v0, v1 = near(u0, u1)
    v2, v3 = near(u2, u3)
    return [v0, v1, v2, v3]


def thrice(value):
    high, low = split(value)
    return jnp.concatenate([high, high, low], axis=0)


def solve_kernel(owner, pairs, recv, rho, dens, other, fixed, green, out, summed, work):
    summed[...] = dens[...] + other[...]
    place = recv[pairs[0, owner[0]]].astype(F32)
    oy = jnp.max(place[8:9, :]).astype(jnp.int32)
    ox = jnp.max(place[9:10, :]).astype(jnp.int32)
    chunks = torus_roll(lambda c: rho[pl.ds(c, N, stride=8), :], oy, ox)

    waves = dot(fixed[:G, 768:864], thrice(jnp.concatenate(chunks, axis=1)))
    for s in range(8):
        work[pl.ds(s, G, stride=8), :] = waves[:, 128 * s : 128 * s + 128]

    ahead_y = fixed[G : 2 * G, 768:864]
    back_y = fixed[160:192, 768:960]
    for part in range(4):
        turned = []
        for c in range(4 * part, 4 * part + 4):
            tiles = [work[8 * k : 8 * k + 8, :] for k in range(4 * c, 4 * c + 4)]
            turned.append(jnp.concatenate(exchange_groups(tiles), axis=0))
        waves = dot(ahead_y, thrice(jnp.concatenate(turned, axis=1)))
        rows = jnp.concatenate([waves[:, 128 * c : 128 * c + 128] for c in range(4)], axis=0)
        high, low = split(rows)
        waves = dot(jnp.concatenate([high, low], axis=1), fixed[:, :256])
        waves = waves + dot(high, fixed[:128, 256:512])
        high, low = split(waves * green[256 * part : 256 * part + 256, :])
        both = dot(high, fixed[:, 512:768])
        rows = both[:, :128] + both[:, 128:] + dot(low, fixed[:, 512:640])
        levels = jnp.concatenate([rows[G * c : G * c + G, :] for c in range(4)], axis=1)
        levels = dot(back_y, thrice(levels))
        for c in range(4):
            tiles = [levels[8 * q : 8 * q + 8, 128 * c : 128 * c + 128] for q in range(4)]
            for i, tile in enumerate(exchange_groups(tiles)):
                k = 16 * part + 4 * c + i
                work[8 * k : 8 * k + 8, :] = tile

    levels = jnp.concatenate([work[pl.ds(s, G, stride=8), :] for s in range(8)], axis=1)
    field = dot(fixed[128:160, 768:960], thrice(levels))
    for s in range(8):
        work[N * s : N * s + N, :] = field[:, 128 * s : 128 * s + 128]

    def load(c):
        return work[pl.ds(pl.multiple_of(c * N, N), N), :]

    chunks = torus_roll(load, B - lax.rem(oy, B), B - lax.rem(ox, B))
    for s in range(8):
        out[pl.ds(s, N, stride=8), :] = chunks[s]


def cube_root(value):
    rough = jnp.exp(jnp.log(jnp.where(value > 0.0, value, 1.0)) * (1.0 / 3.0))
    finer = rough - (rough - value / (rough * rough)) * (1.0 / 3.0)
    return jnp.where(value > 0.0, finer, 0.0)


def gradient_kernel(pairs, phi, code, field, plane, dens, near, far, nearer, out, terms):
    for n in range(N):
        terms[n] = jnp.zeros((8, 128), F32)
    for p in range(N):
        a = pairs[0, p]
        b = pairs[1, p]
        value = jnp.where(code[a] == code[b], field[p], 0.0)
        terms[a] = terms[a] + value * phi[b]
        terms[b] = terms[b] + value * phi[a]
    quarters = []
    for q in range(4):
        density = (dens[q] + far[q]) + (near[q] + nearer[q])
        quarters.append(plane[q] - EXCHANGE_COEF * cube_root(density))
    for n in range(N):
        quarter = code[n]
        local = jnp.where(
            quarter < 1.5,
            jnp.where(quarter < 0.5, quarters[0], quarters[1]),
            jnp.where(quarter < 2.5, quarters[2], quarters[3]),
        )
        out[n] = local * phi[n] - MIXING * terms[n]


def unpack_kernel(offsets, planes, out):
    chunks = torus_roll(
        lambda c: planes[pl.ds(c, N, stride=8), :], offsets[0, 0], offsets[0, 1]
    )
    for s in range(8):
        out[0, :, 128 * s : 128 * s + 128] = chunks[s]


def shape(dims, dtype=F32):
    return jax.ShapeDtypeStruct(dims, dtype)


def constants():
    basis = np.concatenate(axis_basis(), axis=1)
    order = np.array([4 * s + q for q in range(4) for s in range(8)])

    def left(matrix):
        high, low = np_split(matrix)
        return np.concatenate([high, low, high], axis=1)

    high, low = np_split(np.kron(np.eye(4), basis))
    back_high, back_low = np_split(np.kron(np.eye(4), basis.T))
    fixed = np.zeros((256, 1024), jnp.bfloat16)
    fixed[:128, :256] = high
    fixed[128:, :256] = high
    fixed[:128, 256:512] = low
    fixed[:, 512:640] = back_high
    fixed[:, 640:768] = back_low
    fixed[:G, 768:864] = left(basis.T)
    fixed[G : 2 * G, 768:864] = left(basis[order].T)
    fixed[128:160, 768:960] = left(basis)
    fixed[160:192, 768:960] = left(basis[order])
    return jnp.asarray(fixed)


def exchange(x):
    return lax.all_to_all(x, "own", 0, 0, tiled=True)


def kernel(call, out_shape, in_specs, name, vmem, scratch=(), flops=0, moved=0):
    many = isinstance(out_shape, list)
    return pl.pallas_call(
        call,
        out_shape=out_shape,
        in_specs=in_specs,
        out_specs=[VM] * len(out_shape) if many else VM,
        scratch_shapes=scratch,
        compiler_params=pltpu.CompilerParams(vmem_limit_bytes=vmem << 20),
        cost_estimate=pl.CostEstimate(flops=flops, bytes_accessed=moved, transcendentals=0),
        name=name,
    )


def from_group(x, step):
    if step == 1:
        return lax.ppermute(x, "grp", [(g, g ^ 1) for g in range(8)])
    return lax.ppermute(x, "grp", [(g, (g + step) % 8) for g in range(8)])


def body(orbitals, offsets, pairs, ext_pot):
    owner = lax.axis_index("own")
    fixed = constants()
    pairs = pairs.T

    sent = kernel(
        pack_kernel,
        shape((N, 16, 128), BF16),
        [SM, VM],
        "pack",
        60,
        [pltpu.VMEM((8 * N, 128), F32)],
        moved=200_000,
    )(offsets, orbitals)
    sent, fixed, pairs, ext_pot = lax.optimization_barrier((sent, fixed, pairs, ext_pot))
    recv = exchange(sent)

    fixed, pairs, offsets, green = kernel(
        table_kernel,
        [
            shape((256, 1024), BF16),
            shape((2, N), jnp.int32),
            shape((1, 2), jnp.int32),
            shape((1024, 256)),
        ],
        [VM] * 3,
        "tables",
        16,
        flops=2_000_000,
        moved=3_000_000,
    )(fixed, pairs, offsets)
    plane = lax.dynamic_slice_in_dim(ext_pot, owner, 1, 0).astype(F32)
    plane = plane.reshape(2, B, 2, B).transpose(0, 2, 1, 3).reshape(4, 8, 128)
    recv, fixed, pairs, green, plane = lax.optimization_barrier(
        (recv, fixed, pairs, green, plane)
    )

    rho, dens, phi, code = kernel(
        pair_kernel,
        [shape((N, 8, 128)), shape((4, 8, 128)), shape((N, 8, 128)), shape((N, 8, 128))],
        [SM, VM],
        "pair_products",
        4,
        moved=600_000,
    )(pairs, recv)

    mine = exchange(rho)
    other = from_group(dens, 1)
    field, chip_dens = kernel(
        solve_kernel,
        [shape((8 * N, 128)), shape((4, 8, 128))],
        [SM, SM] + [VM] * 6,
        "solve",
        16,
        [pltpu.VMEM((8 * G, 128), F32)],
        flops=1_000_000_000,
        moved=3_000_000,
    )(owner.reshape(1), pairs, recv, mine.reshape(8 * N, 128), dens, other, fixed, green)
    fields = exchange(field.reshape(N, 8, 128))
    others = [from_group(chip_dens, step) for step in (2, 4, 6)]

    gradient = kernel(
        gradient_kernel,
        shape((N, 8, 128)),
        [SM] + [VM] * 8,
        "gradient_planes",
        4,
        [pltpu.VMEM((N, 8, 128), F32)],
        moved=600_000,
    )(pairs, phi, code, fields, plane, chip_dens, *others)
    back = exchange(gradient)

    return kernel(
        unpack_kernel, shape((1, BZ, B * B)), [SM, VM], "unpack", 4, moved=300_000
    )(offsets, back.reshape(8 * N, 128))


def solution(mesh):
    spec = P(("grp", "own"), None, None)
    in_specs = (spec, P(("grp", "own"), None), P("grp", None), P())
    return jax.shard_map(body, mesh=mesh, in_specs=in_specs, out_specs=spec, check_vma=False)
```

time: 85.8 us -> 78.1 us (0.910)
  Pallas kernels: 18.9 us -> 10 us
  waiting for transfers between devices: 17.6 us -> 24.8 us
  starting transfers between devices: 28.6 us -> 24.1 us
    pallas_call x2, Pallas kernels: 13.7 us -> 4.79 us  [the longest x1 4.61 us: body(): kernel(solve_kernel, [shape((8 * N, 128)), shape((4, 8, 128))], [SM, SM]...]
    all_to_all x3, waiting for transfers between devices: 14.5 us -> 21.7 us  [exchange(): return lax.all_to_all(x, 'own', 0, 0, tiled=True)]
    all_to_all x3, starting transfers between devices: 23.6 us -> 19.2 us  [exchange(): return lax.all_to_all(x, 'own', 0, 0, tiled=True)]
  transfers between devices with their start and end apart: 7 -> 7, of which waited for: 6 -> 6; matrix products, arithmetic and copies ran while one was open for 4% -> 1% of each run, Pallas kernels for 7% -> 0%
where the time goes in v2:
time: 78.1 us; the launch traced here: 77 us
  waiting for transfers between devices  24.8 us (32%)
  starting transfers between devices  24.1 us (31%)
  blocking collectives  16.3 us (21%)
  Pallas kernels  10 us (13%)
  other arithmetic  0.89 us (1%)
  local copies, waits for them, and re-layouts  0.79 us (1%)
    all_to_all x3, waiting for transfers between devices, exchange(): return lax.all_to_all(x, 'own', 0, 0, tiled=True)  21.7 us
    all_to_all x3, starting transfers between devices, exchange(): return lax.all_to_all(x, 'own', 0, 0, tiled=True)  19.2 us
    all_to_all x1, blocking collectives, exchange(): return lax.all_to_all(x, 'own', 0, 0, tiled=True)  16.3 us
    ppermute x3, starting transfers between devices, from_group(): return lax.ppermute(x, 'grp', [(g, (g + step) % 8) for g in range(8)])  4.84 us
    pallas_call x1, Pallas kernels, body(): kernel(solve_kernel, [shape((8 * N, 128)), shape((4, 8, 128))], [SM, SM]...  4.61 us
    ppermute x3, waiting for transfers between devices, from_group(): return lax.ppermute(x, 'grp', [(g, (g + step) % 8) for g in range(8)])  1.93 us
    pallas_call x1, Pallas kernels, body(): kernel(pack_kernel, shape((N, 16, 128), BF16), [SM, VM], 'pack', 60, [plt...  1.7 us
  transfers between devices with their start and end apart: 7, of which 6 were waited for; matrix products, arithmetic and copies ran while one was open for 1% of the time, Pallas kernels for 0%

profile of v2, /device:TPU:2, one launch (start us, length us, event | category | flops | bytes accessed | tf_op | source)
XLA Modules:
  0.0 77.0 jit_solution(1704505276145899754)
XLA Ops:
  0.0 0.0 copy-start
  0.0 1.7 %pack.1 = bf16[32,16,128]{2,1,0:T(8,128)(2,1)} custom-call(s32[1,2]{1,0:T(1,128)} %offsets_in.1, bf16[1,32,1024]{2,1,0:T(8,128)(2,1)} %box.1), custom_call_target="tpu_custom_call" | custom-call | bytes 200000 | tf_op jit(solution)/shard_map/pack/pallas_call | solution.py:311
  1.7 11.5 %all-to-all-start = ((bf16[32,16,128]{2,1,0:T(8,128)(2,1)}), bf16[32,16,128]{2,1,0:T(8,128)(2,1)S(1)}, u32[]{:S(2)}, u32[]{:S(2)}) async-start(bf16[32,16,128]{2,1,0:T(8,128)(2,1)} %pack.1), calls=%async_computation | async-start | bytes 262144 | tf_op jit(solution)/shard_map/all_to_all | solution.py:283
  13.2 0.9 %convert_reduce_fusion = f32[4096]{0:T(1024)S(1)} fusion(bf16[32,4096]{1,0:T(8,128)(2,1)} %param.8, s32[]{:T(128)S(6)} %select_n.3), kind=kLoop, calls=%fused_computation.1 | loop fusion | flops 4096 | bytes 24580 | tf_op jit(solution)/shard_map/reshape | solution.py:338
  14.1 0.1 reshape.33
  14.2 0.0 copy-start.1
  14.2 0.0 copy-start.2
  14.3 0.1 reshape.30.plane
  14.3 0.0 copy-done
  14.3 0.5 copy-done.1
  14.9 0.0 copy-done.2
  14.9 0.2 tables.1
  15.1 8.5 %all-to-all-done.recv = bf16[32,16,128]{2,1,0:T(8,128)(2,1)S(1)} async-done(((bf16[32,16,128]{2,1,0:T(8,128)(2,1)}), bf16[32,16,128]{2,1,0:T(8,128)(2,1)S(1)}, u32[]{:S(2)}, u32[]{:S(2)}) %all-to-all-start) | async-done | bytes 131104 | tf_op jit(solution)/shard_map/all_to_all | solution.py:283
  23.6 1.4 %pair_products.1 = (f32[32,8,128]{2,1,0:T(8,128)}, f32[4,8,128]{2,1,0:T(8,128)S(1)}, f32[32,8,128]{2,1,0:T(8,128)S(1)}, f32[32,8,128]{2,1,0:T(8,128)S(1)}) custom-call(s32[2,32]{1,0:T(2,128)S(1)} %get-tuple-element.32.pairs, bf16[32,16,128]{2,1,0:T(8,128)(2,1)S(1)} %all-to-all-done.recv), custom_call_target="tpu_custom_call" | custom-call | bytes 600000 | tf_op jit(solution)/shard_map/pair_products/pallas_call | solution.py:343
  25.0 3.9 %all-to-all-start.1 = ((f32[32,8,128]{2,1,0:T(8,128)}), f32[32,8,128]{2,1,0:T(8,128)S(1)}, u32[]{:S(2)}, u32[]{:S(2)}) async-start(f32[32,8,128]{2,1,0:T(8,128)} %get-tuple-element.36), calls=%async_computation.1 | async-start | bytes 262144 | tf_op jit(solution)/shard_map/all_to_all | solution.py:283
  28.9 0.1 collective-permute-start
  29.0 1.2 %collective-permute-done.other = f32[4,8,128]{2,1,0:T(8,128)S(1)} collective-permute-done((f32[4,8,128]{2,1,0:T(8,128)S(1)}, f32[4,8,128]{2,1,0:T(8,128)S(1)}, u32[]{:S(2)}, u32[]{:S(2)}) %collective-permute-start) | collective-permute-done | bytes 16416 | tf_op jit(solution)/shard_map/ppermute | solution.py:302
  30.1 9.3 %all-to-all-done.1 = f32[32,8,128]{2,1,0:T(8,128)S(1)} async-done(((f32[32,8,128]{2,1,0:T(8,128)}), f32[32,8,128]{2,1,0:T(8,128)S(1)}, u32[]{:S(2)}, u32[]{:S(2)}) %all-to-all-start.1) | async-done | bytes 131104 | tf_op jit(solution)/shard_map/all_to_all | solution.py:283
  39.5 4.6 %solve.1 = (f32[256,128]{1,0:T(8,128)}, f32[4,8,128]{2,1,0:T(8,128)S(1)}) custom-call(s32[1]{0:T(128)} %bitcast.2.owner, s32[2,32]{1,0:T(2,128)S(1)} %get-tuple-element.32.pairs, bf16[32,16,128]{2,1,0:T(8,128)(2,1)S(1)} %all-to-all-done.recv, f32[256,128]{1,0:T(8,128)S(1)} %bitcast.11, f32[4,8,128]{2,1,0:T(8,128)S(1)} %get-tuple-element.37.dens, ...), custom_call_target="tpu_custom_call" | custom-call | flops 1000000000 | bytes 3000000 | tf_op jit(solution)/shard_map/solve/pallas_call | solution.py:354
  44.1 3.9 %all-to-all-start.2 = ((f32[32,8,128]{2,1,0:T(8,128)}), f32[32,8,128]{2,1,0:T(8,128)S(1)}, u32[]{:S(2)}, u32[]{:S(2)}) async-start(f32[32,8,128]{2,1,0:T(8,128)} %bitcast.4), calls=%async_computation.2 | async-start | bytes 262144 | tf_op jit(solution)/shard_map/all_to_all | solution.py:283
  48.0 0.6 collective-permute-start.3
  48.6 2.4 %collective-permute-start.2 = (f32[4,8,128]{2,1,0:T(8,128)S(1)}, f32[4,8,128]{2,1,0:T(8,128)S(1)}, u32[]{:S(2)}, u32[]{:S(2)}) collective-permute-start(f32[4,8,128]{2,1,0:T(8,128)S(1)} %get-tuple-element.42.dens), channel_id=1, source_target_pairs={{0,128},{32,160},{64,192},{96,224},{128,0},{160,32},{192,64},{224,... | collective-permute-start | bytes 49160 | tf_op jit(solution)/shard_map/ppermute | solution.py:303
  51.0 1.8 %collective-permute-start.1 = (f32[4,8,128]{2,1,0:T(8,128)S(1)}, f32[4,8,128]{2,1,0:T(8,128)S(1)}, u32[]{:S(2)}, u32[]{:S(2)}) collective-permute-start(f32[4,8,128]{2,1,0:T(8,128)S(1)} %get-tuple-element.42.dens), channel_id=1, source_target_pairs={{0,64},{32,96},{64,128},{96,160},{128,192},{160,224},{192,0},{224,... | collective-permute-start | bytes 49160 | tf_op jit(solution)/shard_map/ppermute | solution.py:303
  52.8 0.0 collective-permute-done.3.nearer
  52.8 1.0 %collective-permute-done.2.far = f32[4,8,128]{2,1,0:T(8,128)S(1)} collective-permute-done((f32[4,8,128]{2,1,0:T(8,128)S(1)}, f32[4,8,128]{2,1,0:T(8,128)S(1)}, u32[]{:S(2)}, u32[]{:S(2)}) %collective-permute-start.2) | collective-permute-done | bytes 16416 | tf_op jit(solution)/shard_map/ppermute | solution.py:303
  53.8 0.9 %collective-permute-done.1.near = f32[4,8,128]{2,1,0:T(8,128)S(1)} collective-permute-done((f32[4,8,128]{2,1,0:T(8,128)S(1)}, f32[4,8,128]{2,1,0:T(8,128)S(1)}, u32[]{:S(2)}, u32[]{:S(2)}) %collective-permute-start.1) | collective-permute-done | bytes 16416 | tf_op jit(solution)/shard_map/ppermute | solution.py:303
  54.7 3.8 %all-to-all-done.2.field = f32[32,8,128]{2,1,0:T(8,128)S(1)} async-done(((f32[32,8,128]{2,1,0:T(8,128)}), f32[32,8,128]{2,1,0:T(8,128)S(1)}, u32[]{:S(2)}, u32[]{:S(2)}) %all-to-all-start.2) | async-done | bytes 131104 | tf_op jit(solution)/shard_map/all_to_all | solution.py:283
  58.5 0.8 %gradient_planes.1 = f32[32,8,128]{2,1,0:T(8,128)S(1)} custom-call(s32[2,32]{1,0:T(2,128)S(1)} %get-tuple-element.32.pairs, f32[32,8,128]{2,1,0:T(8,128)S(1)} %get-tuple-element.34.phi, f32[32,8,128]{2,1,0:T(8,128)S(1)} %get-tuple-element.35.code, f32[32,8,128]{2,1,0:T(8,128)S(1)} %all-to-all-done.2.field, f32[4,8,128]{2,1,0:T(8,128)S(1)} %reshape.30.plane, ...), custom_call_target="tpu_custom_call" | custom-call | bytes 600000 | tf_op jit(solution)/shard_map/gradient_planes/pallas_call | solution.py:367
  59.4 16.3 %all_to_all.20 = f32[32,8,128]{2,1,0:T(8,128)S(1)} all-to-all(f32[32,8,128]{2,1,0:T(8,128)S(1)} %gradient_planes.1), channel_id=1, replica_groups=mesh['grp'=8,'own'=32] {'own'}, dimensions={0} | all-to-all | bytes 262144 | tf_op jit(solution)/shard_map/all_to_all | solution.py:283
  75.7 1.3 %unpack.1 = f32[1,32,1024]{2,1,0:T(8,128)} custom-call(s32[1,2]{1,0:T(1,128)S(1)} %get-tuple-element.26.offsets, f32[256,128]{1,0:T(8,128)S(1)} %bitcast.10), custom_call_target="tpu_custom_call" | custom-call | bytes 300000 | tf_op jit(solution)/shard_map/unpack/pallas_call | solution.py:378
  (1 shorter events, 0.0 us)
Async XLA Ops:
  0.0 14.3 %copy-start = (bf16[256,1024]{1,0:T(8,128)(2,1)S(1)}, bf16[256,1024]{1,0:T(8,128)(2,1)}, u32[]{:S(2)}) copy-start(bf16[256,1024]{1,0:T(8,128)(2,1)} %constant.10.clone.fixed_in) | copy-start | bytes 1572868
  1.7 21.9 %all-to-all-start = ((bf16[32,16,128]{2,1,0:T(8,128)(2,1)}), bf16[32,16,128]{2,1,0:T(8,128)(2,1)S(1)}, u32[]{:S(2)}, u32[]{:S(2)}) async-start(bf16[32,16,128]{2,1,0:T(8,128)(2,1)} %pack.1), calls=%async_computation | async-start | bytes 262144 | tf_op jit(solution)/shard_map/all_to_all | solution.py:283
  14.2 0.7 copy-start.1
  14.2 0.7 copy-start.2
  25.0 14.5 %all-to-all-start.1 = ((f32[32,8,128]{2,1,0:T(8,128)}), f32[32,8,128]{2,1,0:T(8,128)S(1)}, u32[]{:S(2)}, u32[]{:S(2)}) async-start(f32[32,8,128]{2,1,0:T(8,128)} %get-tuple-element.36), calls=%async_computation.1 | async-start | bytes 262144 | tf_op jit(solution)/shard_map/all_to_all | solution.py:283
  28.9 1.3 %collective-permute-start = (f32[4,8,128]{2,1,0:T(8,128)S(1)}, f32[4,8,128]{2,1,0:T(8,128)S(1)}, u32[]{:S(2)}, u32[]{:S(2)}) collective-permute-start(f32[4,8,128]{2,1,0:T(8,128)S(1)} %get-tuple-element.37.dens), channel_id=1, source_target_pairs={{0,32},{32,0},{64,96},{96,64},{128,160},{160,128},{192,224},{224,1... | collective-permute-start | bytes 49160 | tf_op jit(solution)/shard_map/ppermute | solution.py:302
  44.1 14.4 %all-to-all-start.2 = ((f32[32,8,128]{2,1,0:T(8,128)}), f32[32,8,128]{2,1,0:T(8,128)S(1)}, u32[]{:S(2)}, u32[]{:S(2)}) async-start(f32[32,8,128]{2,1,0:T(8,128)} %bitcast.4), calls=%async_computation.2 | async-start | bytes 262144 | tf_op jit(solution)/shard_map/all_to_all | solution.py:283
  48.0 4.8 %collective-permute-start.3 = (f32[4,8,128]{2,1,0:T(8,128)S(1)}, f32[4,8,128]{2,1,0:T(8,128)S(1)}, u32[]{:S(2)}, u32[]{:S(2)}) collective-permute-start(f32[4,8,128]{2,1,0:T(8,128)S(1)} %get-tuple-element.42.dens), channel_id=1, source_target_pairs={{0,192},{32,224},{64,0},{96,32},{128,64},{160,96},{192,128},{224,1... | collective-permute-start | bytes 49160 | tf_op jit(solution)/shard_map/ppermute | solution.py:303
  48.6 5.2 %collective-permute-start.2 = (f32[4,8,128]{2,1,0:T(8,128)S(1)}, f32[4,8,128]{2,1,0:T(8,128)S(1)}, u32[]{:S(2)}, u32[]{:S(2)}) collective-permute-start(f32[4,8,128]{2,1,0:T(8,128)S(1)} %get-tuple-element.42.dens), channel_id=1, source_target_pairs={{0,128},{32,160},{64,192},{96,224},{128,0},{160,32},{192,64},{224,... | collective-permute-start | bytes 49160 | tf_op jit(solution)/shard_map/ppermute | solution.py:303
  51.0 3.7 %collective-permute-start.1 = (f32[4,8,128]{2,1,0:T(8,128)S(1)}, f32[4,8,128]{2,1,0:T(8,128)S(1)}, u32[]{:S(2)}, u32[]{:S(2)}) collective-permute-start(f32[4,8,128]{2,1,0:T(8,128)S(1)} %get-tuple-element.42.dens), channel_id=1, source_target_pairs={{0,64},{32,96},{64,128},{96,160},{128,192},{160,224},{192,0},{224,... | collective-permute-start | bytes 49160 | tf_op jit(solution)/shard_map/ppermute | solution.py:303

commit v3 on v2

--- a/solution.py
+++ b/solution.py
@@ -168,8 +168,7 @@
     return jnp.concatenate([high, high, low], axis=0)
 
 
-def solve_kernel(owner, pairs, recv, rho, dens, other, fixed, green, out, summed, work):
-    summed[...] = dens[...] + other[...]
+def solve_kernel(owner, pairs, recv, rho, fixed, green, out, work):
     place = recv[pairs[0, owner[0]]].astype(F32)
     oy = jnp.max(place[8:9, :]).astype(jnp.int32)
     ox = jnp.max(place[9:10, :]).astype(jnp.int32)
@@ -221,7 +220,7 @@
     return jnp.where(value > 0.0, finer, 0.0)
 
 
-def gradient_kernel(pairs, phi, code, field, plane, dens, near, far, nearer, out, terms):
+def gradient_kernel(pairs, phi, code, field, plane, dens, other, out, terms):
     for n in range(N):
         terms[n] = jnp.zeros((8, 128), F32)
     for p in range(N):
@@ -232,8 +231,7 @@
         terms[b] = terms[b] + value * phi[a]
     quarters = []
     for q in range(4):
-        density = (dens[q] + far[q]) + (near[q] + nearer[q])
-        quarters.append(plane[q] - EXCHANGE_COEF * cube_root(density))
+        quarters.append(plane[q] - EXCHANGE_COEF * cube_root(dens[q] + other[q]))
     for n in range(N):
         quarter = code[n]
         local = jnp.where(
@@ -350,29 +348,30 @@
     )(pairs, recv)
 
     mine = exchange(rho)
-    other = from_group(dens, 1)
-    field, chip_dens = kernel(
+    others = [from_group(dens, step) for step in (2, 4, 6)]
+    field = kernel(
         solve_kernel,
-        [shape((8 * N, 128)), shape((4, 8, 128))],
-        [SM, SM] + [VM] * 6,
+        shape((8 * N, 128)),
+        [SM, SM] + [VM] * 4,
         "solve",
         16,
         [pltpu.VMEM((8 * G, 128), F32)],
         flops=1_000_000_000,
         moved=3_000_000,
-    )(owner.reshape(1), pairs, recv, mine.reshape(8 * N, 128), dens, other, fixed, green)
+    )(owner.reshape(1), pairs, recv, mine.reshape(8 * N, 128), fixed, green)
     fields = exchange(field.reshape(N, 8, 128))
-    others = [from_group(chip_dens, step) for step in (2, 4, 6)]
+    dens = (dens + others[1]) + (others[0] + others[2])
+    other = from_group(dens, 1)
 
     gradient = kernel(
         gradient_kernel,
         shape((N, 8, 128)),
-        [SM] + [VM] * 8,
+        [SM] + [VM] * 6,
         "gradient_planes",
         4,
         [pltpu.VMEM((N, 8, 128), F32)],
         moved=600_000,
-    )(pairs, phi, code, fields, plane, chip_dens, *others)
+    )(pairs, phi, code, fields, plane, dens, other)
     back = exchange(gradient)
 
     return kernel(

time: 78.1 us -> 75.6 us (0.968)
  blocking collectives: 16.3 us -> 13.8 us
  starting transfers between devices: 24.1 us -> 25.5 us
    all_to_all x1, blocking collectives: 16.3 us -> 13.8 us  [exchange(): return lax.all_to_all(x, 'own', 0, 0, tiled=True)]
    ppermute x3, waiting for transfers between devices: 1.93 us -> 0.01 us  [from_group(): return lax.ppermute(x, 'grp', [(g, (g + step) % 8) for g in range(8)])]
    all_to_all x3, waiting for transfers between devices: 21.7 us -> 22.9 us  [exchange(): return lax.all_to_all(x, 'own', 0, 0, tiled=True)]
  transfers between devices with their start and end apart: 7 -> 7, of which waited for: 6 -> 4; matrix products, arithmetic and copies ran while one was open for 1% -> 1% of each run, Pallas kernels for 0% -> 6%
where the time goes in v3:
time: 75.6 us; the launch traced here: 75.2 us
  starting transfers between devices  25.5 us (34%)
  waiting for transfers between devices  24.1 us (32%)
  blocking collectives  13.8 us (18%)
  Pallas kernels  10 us (13%)
  other arithmetic  0.9 us (1%)
  local copies, waits for them, and re-layouts  0.79 us (1%)
    all_to_all x3, waiting for transfers between devices, exchange(): return lax.all_to_all(x, 'own', 0, 0, tiled=True)  22.9 us
    all_to_all x3, starting transfers between devices, exchange(): return lax.all_to_all(x, 'own', 0, 0, tiled=True)  19.9 us
    all_to_all x1, blocking collectives, exchange(): return lax.all_to_all(x, 'own', 0, 0, tiled=True)  13.8 us
    ppermute x3, starting transfers between devices, from_group(): return lax.ppermute(x, 'grp', [(g, (g + step) % 8) for g in range(8)])  5.44 us
    pallas_call x1, Pallas kernels, body(): kernel(solve_kernel, shape((8 * N, 128)), [SM, SM] + [VM] * 4, 'solve', 1...  4.62 us
    pallas_call x1, Pallas kernels, body(): kernel(pack_kernel, shape((N, 16, 128), BF16), [SM, VM], 'pack', 60, [plt...  1.7 us
  transfers between devices with their start and end apart: 7, of which 4 were waited for; matrix products, arithmetic and copies ran while one was open for 1% of the time, Pallas kernels for 6%

profile of v3, /device:TPU:2, one launch (start us, length us, event | category | flops | bytes accessed | tf_op | source)
XLA Modules:
  0.0 75.2 jit_solution(8486465903214386022)
XLA Ops:
  0.0 0.0 copy-start
  0.0 1.7 %pack.1 = bf16[32,16,128]{2,1,0:T(8,128)(2,1)} custom-call(s32[1,2]{1,0:T(1,128)} %offsets_in.1, bf16[1,32,1024]{2,1,0:T(8,128)(2,1)} %box.1), custom_call_target="tpu_custom_call" | custom-call | bytes 200000 | tf_op jit(solution)/shard_map/pack/pallas_call | solution.py:309
  1.7 11.5 %all-to-all-start = ((bf16[32,16,128]{2,1,0:T(8,128)(2,1)}), bf16[32,16,128]{2,1,0:T(8,128)(2,1)S(1)}, u32[]{:S(2)}, u32[]{:S(2)}) async-start(bf16[32,16,128]{2,1,0:T(8,128)(2,1)} %pack.1), calls=%async_computation | async-start | bytes 262144 | tf_op jit(solution)/shard_map/all_to_all | solution.py:281
  13.2 0.9 %convert_reduce_fusion = f32[4096]{0:T(1024)S(1)} fusion(bf16[32,4096]{1,0:T(8,128)(2,1)} %param.8, s32[]{:T(128)S(6)} %select_n.3), kind=kLoop, calls=%fused_computation.1 | loop fusion | flops 4096 | bytes 24580 | tf_op jit(solution)/shard_map/reshape | solution.py:336
  14.1 0.1 reshape.33
  14.2 0.0 copy-start.1
  14.2 0.0 copy-start.2
  14.3 0.1 reshape.30.plane
  14.3 0.0 copy-done
  14.3 0.5 copy-done.1
  14.9 0.0 copy-done.2
  14.9 0.2 tables.1
  15.1 8.5 %all-to-all-done.recv = bf16[32,16,128]{2,1,0:T(8,128)(2,1)S(1)} async-done(((bf16[32,16,128]{2,1,0:T(8,128)(2,1)}), bf16[32,16,128]{2,1,0:T(8,128)(2,1)S(1)}, u32[]{:S(2)}, u32[]{:S(2)}) %all-to-all-start) | async-done | bytes 131104 | tf_op jit(solution)/shard_map/all_to_all | solution.py:281
  23.6 1.4 %pair_products.1 = (f32[32,8,128]{2,1,0:T(8,128)}, f32[4,8,128]{2,1,0:T(8,128)S(1)}, f32[32,8,128]{2,1,0:T(8,128)S(1)}, f32[32,8,128]{2,1,0:T(8,128)S(1)}) custom-call(s32[2,32]{1,0:T(2,128)S(1)} %get-tuple-element.30.pairs, bf16[32,16,128]{2,1,0:T(8,128)(2,1)S(1)} %all-to-all-done.recv), custom_call_target="tpu_custom_call" | custom-call | bytes 600000 | tf_op jit(solution)/shard_map/pair_products/pallas_call | solution.py:341
  25.0 3.9 %all-to-all-start.1 = ((f32[32,8,128]{2,1,0:T(8,128)}), f32[32,8,128]{2,1,0:T(8,128)S(1)}, u32[]{:S(2)}, u32[]{:S(2)}) async-start(f32[32,8,128]{2,1,0:T(8,128)} %get-tuple-element.34), calls=%async_computation.1 | async-start | bytes 262144 | tf_op jit(solution)/shard_map/all_to_all | solution.py:281
  28.9 0.6 collective-permute-start.2
  29.5 1.5 %collective-permute-start.1 = (f32[4,8,128]{2,1,0:T(8,128)S(1)}, f32[4,8,128]{2,1,0:T(8,128)S(1)}, u32[]{:S(2)}, u32[]{:S(2)}) collective-permute-start(f32[4,8,128]{2,1,0:T(8,128)S(1)} %get-tuple-element.38), channel_id=1, source_target_pairs={{0,64},{32,96},{64,128},{96,160},{128,192},{160,224},{192,0},{224,... | collective-permute-start | bytes 49160 | tf_op jit(solution)/shard_map/ppermute | solution.py:301
  31.0 3.3 %collective-permute-start = (f32[4,8,128]{2,1,0:T(8,128)S(1)}, f32[4,8,128]{2,1,0:T(8,128)S(1)}, u32[]{:S(2)}, u32[]{:S(2)}) collective-permute-start(f32[4,8,128]{2,1,0:T(8,128)S(1)} %get-tuple-element.38), channel_id=1, source_target_pairs={{0,128},{32,160},{64,192},{96,224},{128,0},{160,32},{192,64},{224,... | collective-permute-start | bytes 49160 | tf_op jit(solution)/shard_map/ppermute | solution.py:301
  34.3 5.2 %all-to-all-done.1 = f32[32,8,128]{2,1,0:T(8,128)S(1)} async-done(((f32[32,8,128]{2,1,0:T(8,128)}), f32[32,8,128]{2,1,0:T(8,128)S(1)}, u32[]{:S(2)}, u32[]{:S(2)}) %all-to-all-start.1) | async-done | bytes 131104 | tf_op jit(solution)/shard_map/all_to_all | solution.py:281
  39.5 4.6 %solve.1 = f32[256,128]{1,0:T(8,128)} custom-call(s32[1]{0:T(128)} %bitcast.2.owner, s32[2,32]{1,0:T(2,128)S(1)} %get-tuple-element.30.pairs, bf16[32,16,128]{2,1,0:T(8,128)(2,1)S(1)} %all-to-all-done.recv, f32[256,128]{1,0:T(8,128)S(1)} %bitcast.11, bf16[256,1024]{1,0:T(8,128)(2,1)S(1)} %get-tuple-element.35.fixed, f32[1024,256]{1,0:T(8,128)S(1)} %get-tuple-element.36.green), custom_call_target="tpu_custom_call" | custom-call | flops 1000000000 | bytes 3000000 | tf_op jit(solution)/shard_map/solve/pallas_call | solution.py:352
  44.1 4.6 %all-to-all-start.2 = ((f32[32,8,128]{2,1,0:T(8,128)}), f32[32,8,128]{2,1,0:T(8,128)S(1)}, u32[]{:S(2)}, u32[]{:S(2)}) async-start(f32[32,8,128]{2,1,0:T(8,128)} %bitcast.4), calls=%async_computation.2 | async-start | bytes 262144 | tf_op jit(solution)/shard_map/all_to_all | solution.py:281
  48.7 0.0 collective-permute-done.2
  48.7 0.0 collective-permute-done.1
  48.7 0.0 collective-permute-done
  48.8 0.1 collective-permute-start.3
  48.9 1.2 %collective-permute-done.3.other = f32[4,8,128]{2,1,0:T(8,128)S(1)} collective-permute-done((f32[4,8,128]{2,1,0:T(8,128)S(1)}, f32[4,8,128]{2,1,0:T(8,128)S(1)}, u32[]{:S(2)}, u32[]{:S(2)}) %collective-permute-start.3) | collective-permute-done | bytes 16416 | tf_op jit(solution)/shard_map/ppermute | solution.py:300
  50.0 9.2 %all-to-all-done.2.field = f32[32,8,128]{2,1,0:T(8,128)S(1)} async-done(((f32[32,8,128]{2,1,0:T(8,128)}), f32[32,8,128]{2,1,0:T(8,128)S(1)}, u32[]{:S(2)}, u32[]{:S(2)}) %all-to-all-start.2) | async-done | bytes 131104 | tf_op jit(solution)/shard_map/all_to_all | solution.py:281
  59.2 0.8 %gradient_planes.1 = f32[32,8,128]{2,1,0:T(8,128)S(1)} custom-call(s32[2,32]{1,0:T(2,128)S(1)} %get-tuple-element.30.pairs, f32[32,8,128]{2,1,0:T(8,128)S(1)} %get-tuple-element.32.phi, f32[32,8,128]{2,1,0:T(8,128)S(1)} %get-tuple-element.33.code, f32[32,8,128]{2,1,0:T(8,128)S(1)} %all-to-all-done.2.field, f32[4,8,128]{2,1,0:T(8,128)S(1)} %reshape.30.plane, ...), custom_call_target="tpu_custom_call" | custom-call | bytes 600000 | tf_op jit(solution)/shard_map/gradient_planes/pallas_call | solution.py:366
  60.1 13.8 %all_to_all.20 = f32[32,8,128]{2,1,0:T(8,128)S(1)} all-to-all(f32[32,8,128]{2,1,0:T(8,128)S(1)} %gradient_planes.1), channel_id=1, replica_groups=mesh['grp'=8,'own'=32] {'own'}, dimensions={0} | all-to-all | bytes 262144 | tf_op jit(solution)/shard_map/all_to_all | solution.py:281
  73.8 1.3 %unpack.1 = f32[1,32,1024]{2,1,0:T(8,128)} custom-call(s32[1,2]{1,0:T(1,128)S(1)} %get-tuple-element.24.offsets, f32[256,128]{1,0:T(8,128)S(1)} %bitcast.10), custom_call_target="tpu_custom_call" | custom-call | bytes 300000 | tf_op jit(solution)/shard_map/unpack/pallas_call | solution.py:377
  (2 shorter events, 0.0 us)
Async XLA Ops:
  0.0 14.3 %copy-start = (bf16[256,1024]{1,0:T(8,128)(2,1)S(1)}, bf16[256,1024]{1,0:T(8,128)(2,1)}, u32[]{:S(2)}) copy-start(bf16[256,1024]{1,0:T(8,128)(2,1)} %constant.10.clone.fixed_in) | copy-start | bytes 1572868
  1.7 21.9 %all-to-all-start = ((bf16[32,16,128]{2,1,0:T(8,128)(2,1)}), bf16[32,16,128]{2,1,0:T(8,128)(2,1)S(1)}, u32[]{:S(2)}, u32[]{:S(2)}) async-start(bf16[32,16,128]{2,1,0:T(8,128)(2,1)} %pack.1), calls=%async_computation | async-start | bytes 262144 | tf_op jit(solution)/shard_map/all_to_all | solution.py:281
  14.2 0.7 copy-start.1
  14.2 0.7 copy-start.2
  25.0 14.5 %all-to-all-start.1 = ((f32[32,8,128]{2,1,0:T(8,128)}), f32[32,8,128]{2,1,0:T(8,128)S(1)}, u32[]{:S(2)}, u32[]{:S(2)}) async-start(f32[32,8,128]{2,1,0:T(8,128)} %get-tuple-element.34), calls=%async_computation.1 | async-start | bytes 262144 | tf_op jit(solution)/shard_map/all_to_all | solution.py:281
  28.9 19.8 %collective-permute-start.2 = (f32[4,8,128]{2,1,0:T(8,128)S(1)}, f32[4,8,128]{2,1,0:T(8,128)S(1)}, u32[]{:S(2)}, u32[]{:S(2)}) collective-permute-start(f32[4,8,128]{2,1,0:T(8,128)S(1)} %get-tuple-element.38), channel_id=1, source_target_pairs={{0,192},{32,224},{64,0},{96,32},{128,64},{160,96},{192,128},{224,1... | collective-permute-start | bytes 49160 | tf_op jit(solution)/shard_map/ppermute | solution.py:301
  29.5 19.2 %collective-permute-start.1 = (f32[4,8,128]{2,1,0:T(8,128)S(1)}, f32[4,8,128]{2,1,0:T(8,128)S(1)}, u32[]{:S(2)}, u32[]{:S(2)}) collective-permute-start(f32[4,8,128]{2,1,0:T(8,128)S(1)} %get-tuple-element.38), channel_id=1, source_target_pairs={{0,64},{32,96},{64,128},{96,160},{128,192},{160,224},{192,0},{224,... | collective-permute-start | bytes 49160 | tf_op jit(solution)/shard_map/ppermute | solution.py:301
  31.0 17.8 %collective-permute-start = (f32[4,8,128]{2,1,0:T(8,128)S(1)}, f32[4,8,128]{2,1,0:T(8,128)S(1)}, u32[]{:S(2)}, u32[]{:S(2)}) collective-permute-start(f32[4,8,128]{2,1,0:T(8,128)S(1)} %get-tuple-element.38), channel_id=1, source_target_pairs={{0,128},{32,160},{64,192},{96,224},{128,0},{160,32},{192,64},{224,... | collective-permute-start | bytes 49160 | tf_op jit(solution)/shard_map/ppermute | solution.py:301
  44.1 15.1 %all-to-all-start.2 = ((f32[32,8,128]{2,1,0:T(8,128)}), f32[32,8,128]{2,1,0:T(8,128)S(1)}, u32[]{:S(2)}, u32[]{:S(2)}) async-start(f32[32,8,128]{2,1,0:T(8,128)} %bitcast.4), calls=%async_computation.2 | async-start | bytes 262144 | tf_op jit(solution)/shard_map/all_to_all | solution.py:281
  48.8 1.3 %collective-permute-start.3 = (f32[4,8,128]{2,1,0:T(8,128)S(1)}, f32[4,8,128]{2,1,0:T(8,128)S(1)}, u32[]{:S(2)}, u32[]{:S(2)}) collective-permute-start(f32[4,8,128]{2,1,0:T(8,128)S(1)} %add_add_fusion.dens), channel_id=1, source_target_pairs={{0,32},{32,0},{64,96},{96,64},{128,160},{160,128},{192,224},{224,1... | collective-permute-start | bytes 49160 | tf_op jit(solution)/shard_map/ppermute | solution.py:300

commit v4 on v3

--- a/solution.py
+++ b/solution.py
@@ -84,7 +84,9 @@
         out[z] = both.astype(BF16)
 
 
-def pair_kernel(pairs, recv, rho, dens, phi, code):
+def pair_kernel(listed, recv, rho, dens, phi, code, place, pairs, sem):
+    fetch = pltpu.make_async_copy(listed, pairs, sem)
+    fetch.start()
     row = lax.broadcasted_iota(jnp.int32, (8, 128), 0)
     lane = lax.broadcasted_iota(jnp.int32, (8, 128), 1)
     y = (row * 4 + lax.div(lane, B)).astype(F32)
@@ -102,6 +104,8 @@
             total[q] = total[q] + jnp.where(quarter == float(q), square, 0.0)
     for q in range(4):
         dens[q] = total[q]
+    fetch.wait()
+    place[...] = recv[pairs[0, pairs[2, 0]]].astype(F32)[8:]
     for p in range(N):
         a = pairs[0, p]
         b = pairs[1, p]
@@ -122,10 +126,12 @@
     return k * k
 
 
-def table_kernel(fixed_in, pairs_in, offsets_in, fixed, pairs, offsets, green):
+def table_kernel(owner, corner, fixed_in, pairs_in, fixed, pairs, offsets, green):
     fixed[...] = fixed_in[...]
-    pairs[...] = pairs_in[...]
-    offsets[...] = offsets_in[...]
+    pairs[...] = jnp.full((8, 128), owner[0], jnp.int32)
+    pairs[:2, :N] = pairs_in[...]
+    offsets[:1, :] = jnp.full((1, 128), corner[0, 0], jnp.int32)
+    offsets[1:2, :] = jnp.full((1, 128), corner[0, 1], jnp.int32)
     ky = lax.broadcasted_iota(jnp.int32, (G, 256), 0)
     lane = lax.broadcasted_iota(jnp.int32, (G, 256), 1)
     kx = lax.rem(lane, G)
@@ -168,10 +174,9 @@
     return jnp.concatenate([high, high, low], axis=0)
 
 
-def solve_kernel(owner, pairs, recv, rho, fixed, green, out, work):
-    place = recv[pairs[0, owner[0]]].astype(F32)
-    oy = jnp.max(place[8:9, :]).astype(jnp.int32)
-    ox = jnp.max(place[9:10, :]).astype(jnp.int32)
+def solve_kernel(place, rho, fixed, green, out, work):
+    oy = jnp.max(place[0:1, :]).astype(jnp.int32)
+    ox = jnp.max(place[1:2, :]).astype(jnp.int32)
     chunks = torus_roll(lambda c: rho[pl.ds(c, N, stride=8), :], oy, ox)
 
     waves = dot(fixed[:G, 768:864], thrice(jnp.concatenate(chunks, axis=1)))
@@ -180,26 +185,25 @@
 
     ahead_y = fixed[G : 2 * G, 768:864]
     back_y = fixed[160:192, 768:960]
-    for part in range(4):
-        turned = []
-        for c in range(4 * part, 4 * part + 4):
-            tiles = [work[8 * k : 8 * k + 8, :] for k in range(4 * c, 4 * c + 4)]
-            turned.append(jnp.concatenate(exchange_groups(tiles), axis=0))
-        waves = dot(ahead_y, thrice(jnp.concatenate(turned, axis=1)))
-        rows = jnp.concatenate([waves[:, 128 * c : 128 * c + 128] for c in range(4)], axis=0)
-        high, low = split(rows)
-        waves = dot(jnp.concatenate([high, low], axis=1), fixed[:, :256])
-        waves = waves + dot(high, fixed[:128, 256:512])
-        high, low = split(waves * green[256 * part : 256 * part + 256, :])
-        both = dot(high, fixed[:, 512:768])
-        rows = both[:, :128] + both[:, 128:] + dot(low, fixed[:, 512:640])
-        levels = jnp.concatenate([rows[G * c : G * c + G, :] for c in range(4)], axis=1)
-        levels = dot(back_y, thrice(levels))
-        for c in range(4):
-            tiles = [levels[8 * q : 8 * q + 8, 128 * c : 128 * c + 128] for q in range(4)]
-            for i, tile in enumerate(exchange_groups(tiles)):
-                k = 16 * part + 4 * c + i
-                work[8 * k : 8 * k + 8, :] = tile
+    turned = []
+    for c in range(16):
+        tiles = [work[8 * k : 8 * k + 8, :] for k in range(4 * c, 4 * c + 4)]
+        turned.append(jnp.concatenate(exchange_groups(tiles), axis=0))
+    waves = dot(ahead_y, thrice(jnp.concatenate(turned, axis=1)))
+    rows = jnp.concatenate([waves[:, 128 * c : 128 * c + 128] for c in range(16)], axis=0)
+    high, low = split(rows)
+    waves = dot(jnp.concatenate([high, low], axis=1), fixed[:, :256])
+    waves = waves + dot(high, fixed[:128, 256:512])
+    high, low = split(waves * green[...])
+    both = dot(high, fixed[:, 512:768])
+    rows = both[:, :128] + both[:, 128:] + dot(low, fixed[:, 512:640])
+    levels = jnp.concatenate([rows[G * c : G * c + G, :] for c in range(16)], axis=1)
+    levels = dot(back_y, thrice(levels))
+    for c in range(16):
+        tiles = [levels[8 * q : 8 * q + 8, 128 * c : 128 * c + 128] for q in range(4)]
+        for i, tile in enumerate(exchange_groups(tiles)):
+            k = 4 * c + i
+            work[8 * k : 8 * k + 8, :] = tile
 
     levels = jnp.concatenate([work[pl.ds(s, G, stride=8), :] for s in range(8)], axis=1)
     field = dot(fixed[128:160, 768:960], thrice(levels))
@@ -220,18 +224,21 @@
     return jnp.where(value > 0.0, finer, 0.0)
 
 
-def gradient_kernel(pairs, phi, code, field, plane, dens, other, out, terms):
+def gradient_kernel(listed, phi, code, field, plane, dens, other, out, terms, pairs, sem):
+    fetch = pltpu.make_async_copy(listed, pairs, sem)
+    fetch.start()
+    quarters = []
+    for q in range(4):
+        quarters.append(plane[q] - EXCHANGE_COEF * cube_root(dens[q] + other[q]))
     for n in range(N):
         terms[n] = jnp.zeros((8, 128), F32)
+    fetch.wait()
     for p in range(N):
         a = pairs[0, p]
         b = pairs[1, p]
         value = jnp.where(code[a] == code[b], field[p], 0.0)
         terms[a] = terms[a] + value * phi[b]
         terms[b] = terms[b] + value * phi[a]
-    quarters = []
-    for q in range(4):
-        quarters.append(plane[q] - EXCHANGE_COEF * cube_root(dens[q] + other[q]))
     for n in range(N):
         quarter = code[n]
         local = jnp.where(
@@ -243,9 +250,9 @@
 
 
 def unpack_kernel(offsets, planes, out):
-    chunks = torus_roll(
-        lambda c: planes[pl.ds(c, N, stride=8), :], offsets[0, 0], offsets[0, 1]
-    )
+    oy = jnp.max(offsets[0:1, :])
+    ox = jnp.max(offsets[1:2, :])
+    chunks = torus_roll(lambda c: planes[pl.ds(c, N, stride=8), :], oy, ox)
     for s in range(8):
         out[0, :, 128 * s : 128 * s + 128] = chunks[s]
 
@@ -322,28 +329,31 @@
         table_kernel,
         [
             shape((256, 1024), BF16),
-            shape((2, N), jnp.int32),
-            shape((1, 2), jnp.int32),
+            shape((8, 128), jnp.int32),
+            shape((8, 128), jnp.int32),
             shape((1024, 256)),
         ],
-        [VM] * 3,
+        [SM, SM, VM, VM],
         "tables",
         16,
         flops=2_000_000,
         moved=3_000_000,
-    )(fixed, pairs, offsets)
+    )(owner.reshape(1), offsets, fixed, pairs)
     plane = lax.dynamic_slice_in_dim(ext_pot, owner, 1, 0).astype(F32)
     plane = plane.reshape(2, B, 2, B).transpose(0, 2, 1, 3).reshape(4, 8, 128)
-    recv, fixed, pairs, green, plane = lax.optimization_barrier(
-        (recv, fixed, pairs, green, plane)
+    recv, fixed, pairs, offsets, green, plane = lax.optimization_barrier(
+        (recv, fixed, pairs, offsets, green, plane)
     )
 
-    rho, dens, phi, code = kernel(
+    listing = [pltpu.SMEM((8, 128), jnp.int32), pltpu.SemaphoreType.DMA(())]
+    planes = shape((N, 8, 128))
+    rho, dens, phi, code, place = kernel(
         pair_kernel,
-        [shape((N, 8, 128)), shape((4, 8, 128)), shape((N, 8, 128)), shape((N, 8, 128))],
-        [SM, VM],
+        [planes, shape((4, 8, 128)), planes, planes, shape((8, 128))],
+        [VM, VM],
         "pair_products",
         4,
+        listing,
         moved=600_000,
     )(pairs, recv)
 
@@ -352,13 +362,13 @@
     field = kernel(
         solve_kernel,
         shape((8 * N, 128)),
-        [SM, SM] + [VM] * 4,
+        [VM] * 4,
         "solve",
         16,
         [pltpu.VMEM((8 * G, 128), F32)],
         flops=1_000_000_000,
         moved=3_000_000,
-    )(owner.reshape(1), pairs, recv, mine.reshape(8 * N, 128), fixed, green)
+    )(place, mine.reshape(8 * N, 128), fixed, green)
     fields = exchange(field.reshape(N, 8, 128))
     dens = (dens + others[1]) + (others[0] + others[2])
     other = from_group(dens, 1)
@@ -366,16 +376,16 @@
     gradient = kernel(
         gradient_kernel,
         shape((N, 8, 128)),
-        [SM] + [VM] * 6,
+        [VM] * 7,
         "gradient_planes",
         4,
-        [pltpu.VMEM((N, 8, 128), F32)],
+        [pltpu.VMEM((N, 8, 128), F32)] + listing,
         moved=600_000,
     )(pairs, phi, code, fields, plane, dens, other)
     back = exchange(gradient)
 
     return kernel(
-        unpack_kernel, shape((1, BZ, B * B)), [SM, VM], "unpack", 4, moved=300_000
+        unpack_kernel, shape((1, BZ, B * B)), [VM, VM], "unpack", 4, moved=300_000
     )(offsets, back.reshape(8 * N, 128))
 
 

time: 75.6 us -> 73.7 us (0.975)
  Pallas kernels: 10 us -> 8.71 us
    pallas_call x5, Pallas kernels: 8.34 us -> 7.01 us  [the longest x1 3.08 us: body(): kernel(solve_kernel, shape((8 * N, 128)), [VM] * 4, 'solve', 16, [pltpu.V...]
  transfers between devices with their start and end apart: 7 -> 7, of which waited for: 4 -> 4; matrix products, arithmetic and copies ran while one was open for 1% -> 1% of each run, Pallas kernels for 6% -> 5%
where the time goes in v4:
time: 73.7 us; the launch traced here: 73.3 us
  starting transfers between devices  25.5 us (35%)
  waiting for transfers between devices  23.5 us (32%)
  blocking collectives  13.8 us (19%)
  Pallas kernels  8.71 us (12%)
  other arithmetic  0.9 us (1%)
  local copies, waits for them, and re-layouts  0.87 us (1%)
    all_to_all x3, waiting for transfers between devices, exchange(): return lax.all_to_all(x, 'own', 0, 0, tiled=True)  22.3 us
    all_to_all x3, starting transfers between devices, exchange(): return lax.all_to_all(x, 'own', 0, 0, tiled=True)  20 us
    all_to_all x1, blocking collectives, exchange(): return lax.all_to_all(x, 'own', 0, 0, tiled=True)  13.8 us
    ppermute x3, starting transfers between devices, from_group(): return lax.ppermute(x, 'grp', [(g, (g + step) % 8) for g in range(8)])  5.44 us
    pallas_call x1, Pallas kernels, body(): kernel(solve_kernel, shape((8 * N, 128)), [VM] * 4, 'solve', 16, [pltpu.V...  3.08 us
    pallas_call x1, Pallas kernels, body(): kernel(pack_kernel, shape((N, 16, 128), BF16), [SM, VM], 'pack', 60, [plt...  1.7 us
  transfers between devices with their start and end apart: 7, of which 4 were waited for; matrix products, arithmetic and copies ran while one was open for 1% of the time, Pallas kernels for 5%

profile of v4, /device:TPU:2, one launch (start us, length us, event | category | flops | bytes accessed | tf_op | source)
XLA Modules:
  0.0 73.3 jit_solution(2527507081992844918)
XLA Ops:
  0.0 0.0 copy-start
  0.0 1.7 %pack.1 = bf16[32,16,128]{2,1,0:T(8,128)(2,1)} custom-call(s32[1,2]{1,0:T(1,128)} %corner.1, bf16[1,32,1024]{2,1,0:T(8,128)(2,1)} %box.1), custom_call_target="tpu_custom_call" | custom-call | bytes 200000 | tf_op jit(solution)/shard_map/pack/pallas_call | solution.py:316
  1.7 11.5 %all-to-all-start = ((bf16[32,16,128]{2,1,0:T(8,128)(2,1)}), bf16[32,16,128]{2,1,0:T(8,128)(2,1)S(1)}, u32[]{:S(2)}, u32[]{:S(2)}) async-start(bf16[32,16,128]{2,1,0:T(8,128)(2,1)} %pack.1), calls=%async_computation | async-start | bytes 262144 | tf_op jit(solution)/shard_map/all_to_all | solution.py:288
  13.2 0.9 %convert_reduce_fusion = f32[4096]{0:T(1024)S(1)} fusion(bf16[32,4096]{1,0:T(8,128)(2,1)} %param.8, s32[]{:T(128)S(6)} %select_n.3), kind=kLoop, calls=%fused_computation.1 | loop fusion | flops 4096 | bytes 24580 | tf_op jit(solution)/shard_map/reshape | solution.py:343
  14.1 0.1 reshape.33
  14.2 0.1 reshape.30.plane
  14.3 0.0 copy-start.1
  14.3 0.0 copy-start.2
  14.3 0.0 copy-done
  14.3 0.6 copy-done.1
  15.0 0.0 copy-done.2
  15.0 0.7 tables.1
  15.7 7.9 %all-to-all-done.recv = bf16[32,16,128]{2,1,0:T(8,128)(2,1)S(1)} async-done(((bf16[32,16,128]{2,1,0:T(8,128)(2,1)}), bf16[32,16,128]{2,1,0:T(8,128)(2,1)S(1)}, u32[]{:S(2)}, u32[]{:S(2)}) %all-to-all-start) | async-done | bytes 131104 | tf_op jit(solution)/shard_map/all_to_all | solution.py:288
  23.6 1.3 %pair_products.1 = (f32[32,8,128]{2,1,0:T(8,128)}, f32[4,8,128]{2,1,0:T(8,128)S(1)}, f32[32,8,128]{2,1,0:T(8,128)S(1)}, f32[32,8,128]{2,1,0:T(8,128)S(1)}, f32[8,128]{1,0:T(8,128)S(1)}) custom-call(s32[8,128]{1,0:T(8,128)S(1)} %get-tuple-element.33.listed, bf16[32,16,128]{2,1,0:T(8,128)(2,1)S(1)} %all-to-all-done.recv), custom_call_target="tpu_custom_call" | custom-call | bytes 600000 | tf_op jit(solution)/shard_map/pair_products/pallas_call | solution.py:350
  25.0 3.9 %all-to-all-start.1 = ((f32[32,8,128]{2,1,0:T(8,128)}), f32[32,8,128]{2,1,0:T(8,128)S(1)}, u32[]{:S(2)}, u32[]{:S(2)}) async-start(f32[32,8,128]{2,1,0:T(8,128)} %get-tuple-element.38), calls=%async_computation.1 | async-start | bytes 262144 | tf_op jit(solution)/shard_map/all_to_all | solution.py:288
  28.9 0.6 collective-permute-start.2
  29.5 1.5 %collective-permute-start.1 = (f32[4,8,128]{2,1,0:T(8,128)S(1)}, f32[4,8,128]{2,1,0:T(8,128)S(1)}, u32[]{:S(2)}, u32[]{:S(2)}) collective-permute-start(f32[4,8,128]{2,1,0:T(8,128)S(1)} %get-tuple-element.42), channel_id=1, source_target_pairs={{0,64},{32,96},{64,128},{96,160},{128,192},{160,224},{192,0},{224,... | collective-permute-start | bytes 49160 | tf_op jit(solution)/shard_map/ppermute | solution.py:308
  31.0 3.3 %collective-permute-start = (f32[4,8,128]{2,1,0:T(8,128)S(1)}, f32[4,8,128]{2,1,0:T(8,128)S(1)}, u32[]{:S(2)}, u32[]{:S(2)}) collective-permute-start(f32[4,8,128]{2,1,0:T(8,128)S(1)} %get-tuple-element.42), channel_id=1, source_target_pairs={{0,128},{32,160},{64,192},{96,224},{128,0},{160,32},{192,64},{224,... | collective-permute-start | bytes 49160 | tf_op jit(solution)/shard_map/ppermute | solution.py:308
  34.3 5.2 %all-to-all-done.1 = f32[32,8,128]{2,1,0:T(8,128)S(1)} async-done(((f32[32,8,128]{2,1,0:T(8,128)}), f32[32,8,128]{2,1,0:T(8,128)S(1)}, u32[]{:S(2)}, u32[]{:S(2)}) %all-to-all-start.1) | async-done | bytes 131104 | tf_op jit(solution)/shard_map/all_to_all | solution.py:288
  39.5 3.1 %solve.1 = f32[256,128]{1,0:T(8,128)} custom-call(f32[8,128]{1,0:T(8,128)S(1)} %get-tuple-element.37.place, f32[256,128]{1,0:T(8,128)S(1)} %bitcast.11, bf16[256,1024]{1,0:T(8,128)(2,1)S(1)} %get-tuple-element.39.fixed, f32[1024,256]{1,0:T(8,128)S(1)} %get-tuple-element.40.green), custom_call_target="tpu_custom_call" | custom-call | flops 1000000000 | bytes 3000000 | tf_op jit(solution)/shard_map/solve/pallas_call | solution.py:362
  42.6 4.6 %all-to-all-start.2 = ((f32[32,8,128]{2,1,0:T(8,128)}), f32[32,8,128]{2,1,0:T(8,128)S(1)}, u32[]{:S(2)}, u32[]{:S(2)}) async-start(f32[32,8,128]{2,1,0:T(8,128)} %bitcast.4), calls=%async_computation.2 | async-start | bytes 262144 | tf_op jit(solution)/shard_map/all_to_all | solution.py:288
  47.2 0.0 collective-permute-done.2
  47.2 0.0 collective-permute-done.1
  47.2 0.0 collective-permute-done
  47.2 0.1 collective-permute-start.3
  47.3 1.2 %collective-permute-done.3.other = f32[4,8,128]{2,1,0:T(8,128)S(1)} collective-permute-done((f32[4,8,128]{2,1,0:T(8,128)S(1)}, f32[4,8,128]{2,1,0:T(8,128)S(1)}, u32[]{:S(2)}, u32[]{:S(2)}) %collective-permute-start.3) | collective-permute-done | bytes 16416 | tf_op jit(solution)/shard_map/ppermute | solution.py:307
  48.5 9.2 %all-to-all-done.2.field = f32[32,8,128]{2,1,0:T(8,128)S(1)} async-done(((f32[32,8,128]{2,1,0:T(8,128)}), f32[32,8,128]{2,1,0:T(8,128)S(1)}, u32[]{:S(2)}, u32[]{:S(2)}) %all-to-all-start.2) | async-done | bytes 131104 | tf_op jit(solution)/shard_map/all_to_all | solution.py:288
  57.7 0.9 %gradient_planes.1 = f32[32,8,128]{2,1,0:T(8,128)S(1)} custom-call(s32[8,128]{1,0:T(8,128)S(1)} %get-tuple-element.33.listed, f32[32,8,128]{2,1,0:T(8,128)S(1)} %get-tuple-element.35.phi, f32[32,8,128]{2,1,0:T(8,128)S(1)} %get-tuple-element.36.code, f32[32,8,128]{2,1,0:T(8,128)S(1)} %all-to-all-done.2.field, f32[4,8,128]{2,1,0:T(8,128)S(1)} %reshape.30.plane, ...), custom_call_target="tpu_custom_call" | custom-call | bytes 600000 | tf_op jit(solution)/shard_map/gradient_planes/pallas_call | solution.py:376
  58.6 13.8 %all_to_all.20 = f32[32,8,128]{2,1,0:T(8,128)S(1)} all-to-all(f32[32,8,128]{2,1,0:T(8,128)S(1)} %gradient_planes.1), channel_id=1, replica_groups=mesh['grp'=8,'own'=32] {'own'}, dimensions={0} | all-to-all | bytes 262144 | tf_op jit(solution)/shard_map/all_to_all | solution.py:288
  72.3 1.0 %unpack.1 = f32[1,32,1024]{2,1,0:T(8,128)} custom-call(s32[8,128]{1,0:T(8,128)S(1)} %get-tuple-element.32.offsets, f32[256,128]{1,0:T(8,128)S(1)} %bitcast.10), custom_call_target="tpu_custom_call" | custom-call | bytes 300000 | tf_op jit(solution)/shard_map/unpack/pallas_call | solution.py:387
  (2 shorter events, 0.0 us)
Async XLA Ops:
  0.0 14.3 %copy-start = (bf16[256,1024]{1,0:T(8,128)(2,1)S(1)}, bf16[256,1024]{1,0:T(8,128)(2,1)}, u32[]{:S(2)}) copy-start(bf16[256,1024]{1,0:T(8,128)(2,1)} %constant.10.clone.fixed_in) | copy-start | bytes 1572868
  1.7 21.9 %all-to-all-start = ((bf16[32,16,128]{2,1,0:T(8,128)(2,1)}), bf16[32,16,128]{2,1,0:T(8,128)(2,1)S(1)}, u32[]{:S(2)}, u32[]{:S(2)}) async-start(bf16[32,16,128]{2,1,0:T(8,128)(2,1)} %pack.1), calls=%async_computation | async-start | bytes 262144 | tf_op jit(solution)/shard_map/all_to_all | solution.py:288
  14.3 0.7 copy-start.1
  14.3 0.7 copy-start.2
  25.0 14.5 %all-to-all-start.1 = ((f32[32,8,128]{2,1,0:T(8,128)}), f32[32,8,128]{2,1,0:T(8,128)S(1)}, u32[]{:S(2)}, u32[]{:S(2)}) async-start(f32[32,8,128]{2,1,0:T(8,128)} %get-tuple-element.38), calls=%async_computation.1 | async-start | bytes 262144 | tf_op jit(solution)/shard_map/all_to_all | solution.py:288
  28.9 18.3 %collective-permute-start.2 = (f32[4,8,128]{2,1,0:T(8,128)S(1)}, f32[4,8,128]{2,1,0:T(8,128)S(1)}, u32[]{:S(2)}, u32[]{:S(2)}) collective-permute-start(f32[4,8,128]{2,1,0:T(8,128)S(1)} %get-tuple-element.42), channel_id=1, source_target_pairs={{0,192},{32,224},{64,0},{96,32},{128,64},{160,96},{192,128},{224,1... | collective-permute-start | bytes 49160 | tf_op jit(solution)/shard_map/ppermute | solution.py:308
  29.5 17.7 %collective-permute-start.1 = (f32[4,8,128]{2,1,0:T(8,128)S(1)}, f32[4,8,128]{2,1,0:T(8,128)S(1)}, u32[]{:S(2)}, u32[]{:S(2)}) collective-permute-start(f32[4,8,128]{2,1,0:T(8,128)S(1)} %get-tuple-element.42), channel_id=1, source_target_pairs={{0,64},{32,96},{64,128},{96,160},{128,192},{160,224},{192,0},{224,... | collective-permute-start | bytes 49160 | tf_op jit(solution)/shard_map/ppermute | solution.py:308
  31.0 16.2 %collective-permute-start = (f32[4,8,128]{2,1,0:T(8,128)S(1)}, f32[4,8,128]{2,1,0:T(8,128)S(1)}, u32[]{:S(2)}, u32[]{:S(2)}) collective-permute-start(f32[4,8,128]{2,1,0:T(8,128)S(1)} %get-tuple-element.42), channel_id=1, source_target_pairs={{0,128},{32,160},{64,192},{96,224},{128,0},{160,32},{192,64},{224,... | collective-permute-start | bytes 49160 | tf_op jit(solution)/shard_map/ppermute | solution.py:308
  42.6 15.1 %all-to-all-start.2 = ((f32[32,8,128]{2,1,0:T(8,128)}), f32[32,8,128]{2,1,0:T(8,128)S(1)}, u32[]{:S(2)}, u32[]{:S(2)}) async-start(f32[32,8,128]{2,1,0:T(8,128)} %bitcast.4), calls=%async_computation.2 | async-start | bytes 262144 | tf_op jit(solution)/shard_map/all_to_all | solution.py:288
  47.2 1.3 %collective-permute-start.3 = (f32[4,8,128]{2,1,0:T(8,128)S(1)}, f32[4,8,128]{2,1,0:T(8,128)S(1)}, u32[]{:S(2)}, u32[]{:S(2)}) collective-permute-start(f32[4,8,128]{2,1,0:T(8,128)S(1)} %add_add_fusion.dens), channel_id=1, source_target_pairs={{0,32},{32,0},{64,96},{96,64},{128,160},{160,128},{192,224},{224,1... | collective-permute-start | bytes 49160 | tf_op jit(solution)/shard_map/ppermute | solution.py:307

commit v5 on v4

--- a/solution.py
+++ b/solution.py
@@ -84,9 +84,20 @@
         out[z] = both.astype(BF16)
 
 
-def pair_kernel(listed, recv, rho, dens, phi, code, place, pairs, sem):
-    fetch = pltpu.make_async_copy(listed, pairs, sem)
-    fetch.start()
+def pair_numbers(pairs):
+    words = [jnp.max(pairs[r : r + 1, 0:1]) for r in range(11)]
+    numbers = []
+    for p in range(N):
+        pair = lax.shift_right_logical(words[p // 3], jnp.int32(10 * (p % 3)))
+        second = lax.bitwise_and(pair, jnp.int32(31))
+        first = lax.bitwise_and(lax.shift_right_logical(pair, jnp.int32(5)), jnp.int32(31))
+        numbers.append((first, second))
+    return numbers
+
+
+def pair_kernel(pairs, recv, rho, dens, phi, code, place):
+    numbers = pair_numbers(pairs)
+    first = jnp.max(pairs[11:12, 0:1])
     row = lax.broadcasted_iota(jnp.int32, (8, 128), 0)
     lane = lax.broadcasted_iota(jnp.int32, (8, 128), 1)
     y = (row * 4 + lax.div(lane, B)).astype(F32)
@@ -104,11 +115,9 @@
             total[q] = total[q] + jnp.where(quarter == float(q), square, 0.0)
     for q in range(4):
         dens[q] = total[q]
-    fetch.wait()
-    place[...] = recv[pairs[0, pairs[2, 0]]].astype(F32)[8:]
+    place[...] = recv[first].astype(F32)[8:]
     for p in range(N):
-        a = pairs[0, p]
-        b = pairs[1, p]
+        a, b = numbers[p]
         rho[p] = jnp.where(code[a] == code[b], phi[a] * phi[b], 0.0)
 
 
@@ -128,8 +137,16 @@
 
 def table_kernel(owner, corner, fixed_in, pairs_in, fixed, pairs, offsets, green):
     fixed[...] = fixed_in[...]
-    pairs[...] = jnp.full((8, 128), owner[0], jnp.int32)
-    pairs[:2, :N] = pairs_in[...]
+    row = lax.broadcasted_iota(jnp.int32, (16, N), 0)
+    spot = lax.broadcasted_iota(jnp.int32, (16, N), 1) - 3 * row
+    both = pairs_in[0:1, :] * 32 + pairs_in[1:2, :]
+    own = lax.broadcasted_iota(jnp.int32, (1, N), 1) == owner[0]
+    word = jnp.max(jnp.where(own, pairs_in[0:1, :], 0), axis=1, keepdims=True)
+    word = jnp.where(row[:, :1] == 11, word, 0)
+    for i in range(3):
+        part = jnp.max(jnp.where(spot == i, both, 0), axis=1, keepdims=True)
+        word = word + part * (1024**i)
+    pairs[...] = jnp.broadcast_to(word, (16, 128))
     offsets[:1, :] = jnp.full((1, 128), corner[0, 0], jnp.int32)
     offsets[1:2, :] = jnp.full((1, 128), corner[0, 1], jnp.int32)
     ky = lax.broadcasted_iota(jnp.int32, (G, 256), 0)
@@ -224,18 +241,15 @@
     return jnp.where(value > 0.0, finer, 0.0)
 
 
-def gradient_kernel(listed, phi, code, field, plane, dens, other, out, terms, pairs, sem):
-    fetch = pltpu.make_async_copy(listed, pairs, sem)
-    fetch.start()
+def gradient_kernel(pairs, phi, code, field, plane, dens, other, out, terms):
+    numbers = pair_numbers(pairs)
     quarters = []
     for q in range(4):
         quarters.append(plane[q] - EXCHANGE_COEF * cube_root(dens[q] + other[q]))
     for n in range(N):
         terms[n] = jnp.zeros((8, 128), F32)
-    fetch.wait()
     for p in range(N):
-        a = pairs[0, p]
-        b = pairs[1, p]
+        a, b = numbers[p]
         value = jnp.where(code[a] == code[b], field[p], 0.0)
         terms[a] = terms[a] + value * phi[b]
         terms[b] = terms[b] + value * phi[a]
@@ -329,7 +343,7 @@
         table_kernel,
         [
             shape((256, 1024), BF16),
-            shape((8, 128), jnp.int32),
+            shape((16, 128), jnp.int32),
             shape((8, 128), jnp.int32),
             shape((1024, 256)),
         ],
@@ -345,7 +359,6 @@
         (recv, fixed, pairs, offsets, green, plane)
     )
 
-    listing = [pltpu.SMEM((8, 128), jnp.int32), pltpu.SemaphoreType.DMA(())]
     planes = shape((N, 8, 128))
     rho, dens, phi, code, place = kernel(
         pair_kernel,
@@ -353,7 +366,6 @@
         [VM, VM],
         "pair_products",
         4,
-        listing,
         moved=600_000,
     )(pairs, recv)
 
@@ -379,7 +391,7 @@
         [VM] * 7,
         "gradient_planes",
         4,
-        [pltpu.VMEM((N, 8, 128), F32)] + listing,
+        [pltpu.VMEM((N, 8, 128), F32)],
         moved=600_000,
     )(pairs, phi, code, fields, plane, dens, other)
     back = exchange(gradient)

time: 73.7 us -> 72.6 us (0.985)
  Pallas kernels: 8.71 us -> 7.71 us
  transfers between devices with their start and end apart: 7 -> 7, of which waited for: 4 -> 4; matrix products, arithmetic and copies ran while one was open for 1% -> 2% of each run, Pallas kernels for 5% -> 5%
where the time goes in v5:
time: 72.6 us; the launch traced here: 72.2 us
  starting transfers between devices  25.5 us (35%)
  waiting for transfers between devices  23.3 us (32%)
  blocking collectives  13.8 us (19%)
  Pallas kernels  7.71 us (11%)
  other arithmetic  0.9 us (1%)
  local copies, waits for them, and re-layouts  0.87 us (1%)
    all_to_all x3, waiting for transfers between devices, exchange(): return lax.all_to_all(x, 'own', 0, 0, tiled=True)  22.2 us
    all_to_all x3, starting transfers between devices, exchange(): return lax.all_to_all(x, 'own', 0, 0, tiled=True)  19.9 us
    all_to_all x1, blocking collectives, exchange(): return lax.all_to_all(x, 'own', 0, 0, tiled=True)  13.8 us
    ppermute x3, starting transfers between devices, from_group(): return lax.ppermute(x, 'grp', [(g, (g + step) % 8) for g in range(8)])  5.44 us
    pallas_call x1, Pallas kernels, body(): kernel(solve_kernel, shape((8 * N, 128)), [VM] * 4, 'solve', 16, [pltpu.V...  3.08 us
    pallas_call x1, Pallas kernels, body(): kernel(pack_kernel, shape((N, 16, 128), BF16), [SM, VM], 'pack', 60, [plt...  1.7 us
  transfers between devices with their start and end apart: 7, of which 4 were waited for; matrix products, arithmetic and copies ran while one was open for 2% of the time, Pallas kernels for 5%

profile of v5, /device:TPU:2, one launch (start us, length us, event | category | flops | bytes accessed | tf_op | source)
XLA Modules:
  0.0 72.2 jit_solution(1449996221744403832)
XLA Ops:
  0.0 0.0 copy-start
  0.0 1.7 %pack.1 = bf16[32,16,128]{2,1,0:T(8,128)(2,1)} custom-call(s32[1,2]{1,0:T(1,128)} %corner.1, bf16[1,32,1024]{2,1,0:T(8,128)(2,1)} %box.1), custom_call_target="tpu_custom_call" | custom-call | bytes 200000 | tf_op jit(solution)/shard_map/pack/pallas_call | solution.py:330
  1.7 11.5 %all-to-all-start = ((bf16[32,16,128]{2,1,0:T(8,128)(2,1)}), bf16[32,16,128]{2,1,0:T(8,128)(2,1)S(1)}, u32[]{:S(2)}, u32[]{:S(2)}) async-start(bf16[32,16,128]{2,1,0:T(8,128)(2,1)} %pack.1), calls=%async_computation | async-start | bytes 262144 | tf_op jit(solution)/shard_map/all_to_all | solution.py:302
  13.2 0.9 %convert_reduce_fusion = f32[4096]{0:T(1024)S(1)} fusion(bf16[32,4096]{1,0:T(8,128)(2,1)} %param.8, s32[]{:T(128)S(6)} %select_n.3), kind=kLoop, calls=%fused_computation.1 | loop fusion | flops 4096 | bytes 24580 | tf_op jit(solution)/shard_map/reshape | solution.py:357
  14.1 0.1 reshape.33
  14.2 0.1 reshape.30.plane
  14.3 0.0 copy-start.1
  14.3 0.0 copy-start.2
  14.3 0.0 copy-done
  14.3 0.6 copy-done.1
  15.0 0.0 copy-done.2
  15.0 0.8 %tables.1 = (bf16[256,1024]{1,0:T(8,128)(2,1)S(1)}, s32[16,128]{1,0:T(8,128)S(1)}, s32[8,128]{1,0:T(8,128)S(1)}, f32[1024,256]{1,0:T(8,128)S(1)}) custom-call(s32[1]{0:T(128)} %bitcast.1.owner, s32[1,2]{1,0:T(1,128)S(1)} %copy-done.1, bf16[256,1024]{1,0:T(8,128)(2,1)S(1)} %copy-done, s32[2,32]{1,0:T(2,128)S(1)} %bitcast.12), custom_call_target="tpu_custom_call" | custom-call | flops 2000000 | bytes 3000000 | tf_op jit(solution)/shard_map/tables/pallas_call | solution.py:342
  15.8 7.8 %all-to-all-done.recv = bf16[32,16,128]{2,1,0:T(8,128)(2,1)S(1)} async-done(((bf16[32,16,128]{2,1,0:T(8,128)(2,1)}), bf16[32,16,128]{2,1,0:T(8,128)(2,1)S(1)}, u32[]{:S(2)}, u32[]{:S(2)}) %all-to-all-start) | async-done | bytes 131104 | tf_op jit(solution)/shard_map/all_to_all | solution.py:302
  23.6 0.8 %pair_products.1 = (f32[32,8,128]{2,1,0:T(8,128)}, f32[4,8,128]{2,1,0:T(8,128)S(1)}, f32[32,8,128]{2,1,0:T(8,128)S(1)}, f32[32,8,128]{2,1,0:T(8,128)S(1)}, f32[8,128]{1,0:T(8,128)S(1)}) custom-call(s32[16,128]{1,0:T(8,128)S(1)} %get-tuple-element.33.pairs, bf16[32,16,128]{2,1,0:T(8,128)(2,1)S(1)} %all-to-all-done.recv), custom_call_target="tpu_custom_call" | custom-call | bytes 600000 | tf_op jit(solution)/shard_map/pair_products/pallas_call | solution.py:363
  24.4 3.9 %all-to-all-start.1 = ((f32[32,8,128]{2,1,0:T(8,128)}), f32[32,8,128]{2,1,0:T(8,128)S(1)}, u32[]{:S(2)}, u32[]{:S(2)}) async-start(f32[32,8,128]{2,1,0:T(8,128)} %get-tuple-element.38), calls=%async_computation.1 | async-start | bytes 262144 | tf_op jit(solution)/shard_map/all_to_all | solution.py:302
  28.3 0.6 collective-permute-start.2
  28.9 1.5 %collective-permute-start.1 = (f32[4,8,128]{2,1,0:T(8,128)S(1)}, f32[4,8,128]{2,1,0:T(8,128)S(1)}, u32[]{:S(2)}, u32[]{:S(2)}) collective-permute-start(f32[4,8,128]{2,1,0:T(8,128)S(1)} %get-tuple-element.42), channel_id=1, source_target_pairs={{0,64},{32,96},{64,128},{96,160},{128,192},{160,224},{192,0},{224,... | collective-permute-start | bytes 49160 | tf_op jit(solution)/shard_map/ppermute | solution.py:322
  30.4 3.3 %collective-permute-start = (f32[4,8,128]{2,1,0:T(8,128)S(1)}, f32[4,8,128]{2,1,0:T(8,128)S(1)}, u32[]{:S(2)}, u32[]{:S(2)}) collective-permute-start(f32[4,8,128]{2,1,0:T(8,128)S(1)} %get-tuple-element.42), channel_id=1, source_target_pairs={{0,128},{32,160},{64,192},{96,224},{128,0},{160,32},{192,64},{224,... | collective-permute-start | bytes 49160 | tf_op jit(solution)/shard_map/ppermute | solution.py:322
  33.7 5.2 %all-to-all-done.1 = f32[32,8,128]{2,1,0:T(8,128)S(1)} async-done(((f32[32,8,128]{2,1,0:T(8,128)}), f32[32,8,128]{2,1,0:T(8,128)S(1)}, u32[]{:S(2)}, u32[]{:S(2)}) %all-to-all-start.1) | async-done | bytes 131104 | tf_op jit(solution)/shard_map/all_to_all | solution.py:302
  38.9 3.1 %solve.1 = f32[256,128]{1,0:T(8,128)} custom-call(f32[8,128]{1,0:T(8,128)S(1)} %get-tuple-element.37.place, f32[256,128]{1,0:T(8,128)S(1)} %bitcast.11, bf16[256,1024]{1,0:T(8,128)(2,1)S(1)} %get-tuple-element.39.fixed, f32[1024,256]{1,0:T(8,128)S(1)} %get-tuple-element.40.green), custom_call_target="tpu_custom_call" | custom-call | flops 1000000000 | bytes 3000000 | tf_op jit(solution)/shard_map/solve/pallas_call | solution.py:374
  42.0 4.6 %all-to-all-start.2 = ((f32[32,8,128]{2,1,0:T(8,128)}), f32[32,8,128]{2,1,0:T(8,128)S(1)}, u32[]{:S(2)}, u32[]{:S(2)}) async-start(f32[32,8,128]{2,1,0:T(8,128)} %bitcast.4), calls=%async_computation.2 | async-start | bytes 262144 | tf_op jit(solution)/shard_map/all_to_all | solution.py:302
  46.6 0.0 collective-permute-done.2
  46.6 0.0 collective-permute-done.1
  46.6 0.0 collective-permute-done
  46.7 0.1 collective-permute-start.3
  46.8 1.2 %collective-permute-done.3.other = f32[4,8,128]{2,1,0:T(8,128)S(1)} collective-permute-done((f32[4,8,128]{2,1,0:T(8,128)S(1)}, f32[4,8,128]{2,1,0:T(8,128)S(1)}, u32[]{:S(2)}, u32[]{:S(2)}) %collective-permute-start.3) | collective-permute-done | bytes 16416 | tf_op jit(solution)/shard_map/ppermute | solution.py:321
  47.9 9.2 %all-to-all-done.2.field = f32[32,8,128]{2,1,0:T(8,128)S(1)} async-done(((f32[32,8,128]{2,1,0:T(8,128)}), f32[32,8,128]{2,1,0:T(8,128)S(1)}, u32[]{:S(2)}, u32[]{:S(2)}) %all-to-all-start.2) | async-done | bytes 131104 | tf_op jit(solution)/shard_map/all_to_all | solution.py:302
  57.1 0.3 gradient_planes.1
  57.4 13.8 %all_to_all.20 = f32[32,8,128]{2,1,0:T(8,128)S(1)} all-to-all(f32[32,8,128]{2,1,0:T(8,128)S(1)} %gradient_planes.1), channel_id=1, replica_groups=mesh['grp'=8,'own'=32] {'own'}, dimensions={0} | all-to-all | bytes 262144 | tf_op jit(solution)/shard_map/all_to_all | solution.py:302
  71.2 1.0 %unpack.1 = f32[1,32,1024]{2,1,0:T(8,128)} custom-call(s32[8,128]{1,0:T(8,128)S(1)} %get-tuple-element.32.offsets, f32[256,128]{1,0:T(8,128)S(1)} %bitcast.10), custom_call_target="tpu_custom_call" | custom-call | bytes 300000 | tf_op jit(solution)/shard_map/unpack/pallas_call | solution.py:399
  (2 shorter events, 0.0 us)
Async XLA Ops:
  0.0 14.3 %copy-start = (bf16[256,1024]{1,0:T(8,128)(2,1)S(1)}, bf16[256,1024]{1,0:T(8,128)(2,1)}, u32[]{:S(2)}) copy-start(bf16[256,1024]{1,0:T(8,128)(2,1)} %constant.10.clone.fixed_in) | copy-start | bytes 1572868
  1.7 21.9 %all-to-all-start = ((bf16[32,16,128]{2,1,0:T(8,128)(2,1)}), bf16[32,16,128]{2,1,0:T(8,128)(2,1)S(1)}, u32[]{:S(2)}, u32[]{:S(2)}) async-start(bf16[32,16,128]{2,1,0:T(8,128)(2,1)} %pack.1), calls=%async_computation | async-start | bytes 262144 | tf_op jit(solution)/shard_map/all_to_all | solution.py:302
  14.3 0.7 copy-start.1
  14.3 0.7 copy-start.2
  24.4 14.5 %all-to-all-start.1 = ((f32[32,8,128]{2,1,0:T(8,128)}), f32[32,8,128]{2,1,0:T(8,128)S(1)}, u32[]{:S(2)}, u32[]{:S(2)}) async-start(f32[32,8,128]{2,1,0:T(8,128)} %get-tuple-element.38), calls=%async_computation.1 | async-start | bytes 262144 | tf_op jit(solution)/shard_map/all_to_all | solution.py:302
  28.3 18.3 %collective-permute-start.2 = (f32[4,8,128]{2,1,0:T(8,128)S(1)}, f32[4,8,128]{2,1,0:T(8,128)S(1)}, u32[]{:S(2)}, u32[]{:S(2)}) collective-permute-start(f32[4,8,128]{2,1,0:T(8,128)S(1)} %get-tuple-element.42), channel_id=1, source_target_pairs={{0,192},{32,224},{64,0},{96,32},{128,64},{160,96},{192,128},{224,1... | collective-permute-start | bytes 49160 | tf_op jit(solution)/shard_map/ppermute | solution.py:322
  28.9 17.7 %collective-permute-start.1 = (f32[4,8,128]{2,1,0:T(8,128)S(1)}, f32[4,8,128]{2,1,0:T(8,128)S(1)}, u32[]{:S(2)}, u32[]{:S(2)}) collective-permute-start(f32[4,8,128]{2,1,0:T(8,128)S(1)} %get-tuple-element.42), channel_id=1, source_target_pairs={{0,64},{32,96},{64,128},{96,160},{128,192},{160,224},{192,0},{224,... | collective-permute-start | bytes 49160 | tf_op jit(solution)/shard_map/ppermute | solution.py:322
  30.4 16.2 %collective-permute-start = (f32[4,8,128]{2,1,0:T(8,128)S(1)}, f32[4,8,128]{2,1,0:T(8,128)S(1)}, u32[]{:S(2)}, u32[]{:S(2)}) collective-permute-start(f32[4,8,128]{2,1,0:T(8,128)S(1)} %get-tuple-element.42), channel_id=1, source_target_pairs={{0,128},{32,160},{64,192},{96,224},{128,0},{160,32},{192,64},{224,... | collective-permute-start | bytes 49160 | tf_op jit(solution)/shard_map/ppermute | solution.py:322
  42.0 15.1 %all-to-all-start.2 = ((f32[32,8,128]{2,1,0:T(8,128)}), f32[32,8,128]{2,1,0:T(8,128)S(1)}, u32[]{:S(2)}, u32[]{:S(2)}) async-start(f32[32,8,128]{2,1,0:T(8,128)} %bitcast.4), calls=%async_computation.2 | async-start | bytes 262144 | tf_op jit(solution)/shard_map/all_to_all | solution.py:302
  46.7 1.3 %collective-permute-start.3 = (f32[4,8,128]{2,1,0:T(8,128)S(1)}, f32[4,8,128]{2,1,0:T(8,128)S(1)}, u32[]{:S(2)}, u32[]{:S(2)}) collective-permute-start(f32[4,8,128]{2,1,0:T(8,128)S(1)} %add_add_fusion.dens), channel_id=1, source_target_pairs={{0,32},{32,0},{64,96},{96,64},{128,160},{160,128},{192,224},{224,1... | collective-permute-start | bytes 49160 | tf_op jit(solution)/shard_map/ppermute | solution.py:321

commit v6 on v5

--- a/solution.py
+++ b/solution.py
@@ -191,17 +191,45 @@
     return jnp.concatenate([high, high, low], axis=0)
 
 
+def turn(table, wave_index, cell, start):
+    odd = lax.rem(wave(wave_index), 2) == 1
+    return jnp.where(odd & (cell < start), -table.astype(F32), table.astype(F32)).astype(BF16)
+
+
 def solve_kernel(place, rho, fixed, green, out, work):
     oy = jnp.max(place[0:1, :]).astype(jnp.int32)
     ox = jnp.max(place[1:2, :]).astype(jnp.int32)
-    chunks = torus_roll(lambda c: rho[pl.ds(c, N, stride=8), :], oy, ox)
-
+
+    def index(dims, axis):
+        return lax.broadcasted_iota(jnp.int32, dims, axis)
+
+    def row_of(k):
+        k = lax.rem(k, B)
+        return lax.rem(k, 8) * 4 + lax.div(k, 8)
+
+    ahead_y = turn(
+        fixed[G : 2 * G, 768:864], index((G, 96), 0), row_of(index((G, 96), 1)), oy
+    )
+    back_y = turn(
+        fixed[160:192, 768:960],
+        lax.rem(index((N, 192), 1), G),
+        row_of(index((N, 192), 0)),
+        oy,
+    )
+    square = (256, 256)
+    wave_x = lax.rem(index(square, 1), G)
+    cell_x = lax.rem(index(square, 0), B)
+    ahead_x = turn(fixed[:, :256], wave_x, cell_x, ox)
+    ahead_x_low = turn(fixed[:128, 256:512], wave_x[:128], cell_x[:128], ox)
+    wave_x = lax.rem(index(square, 0), G)
+    cell_x = lax.rem(index(square, 1), B)
+    back_x = turn(fixed[:, 512:768], wave_x, cell_x, ox)
+
+    chunks = [rho[pl.ds(s, N, stride=8), :] for s in range(8)]
     waves = dot(fixed[:G, 768:864], thrice(jnp.concatenate(chunks, axis=1)))
     for s in range(8):
         work[pl.ds(s, G, stride=8), :] = waves[:, 128 * s : 128 * s + 128]
 
-    ahead_y = fixed[G : 2 * G, 768:864]
-    back_y = fixed[160:192, 768:960]
     turned = []
     for c in range(16):
         tiles = [work[8 * k : 8 * k + 8, :] for k in range(4 * c, 4 * c + 4)]
@@ -209,11 +237,11 @@
     waves = dot(ahead_y, thrice(jnp.concatenate(turned, axis=1)))
     rows = jnp.concatenate([waves[:, 128 * c : 128 * c + 128] for c in range(16)], axis=0)
     high, low = split(rows)
-    waves = dot(jnp.concatenate([high, low], axis=1), fixed[:, :256])
-    waves = waves + dot(high, fixed[:128, 256:512])
+    waves = dot(jnp.concatenate([high, low], axis=1), ahead_x)
+    waves = waves + dot(high, ahead_x_low)
     high, low = split(waves * green[...])
-    both = dot(high, fixed[:, 512:768])
-    rows = both[:, :128] + both[:, 128:] + dot(low, fixed[:, 512:640])
+    both = dot(high, back_x)
+    rows = both[:, :128] + both[:, 128:] + dot(low, back_x[:, :128])
     levels = jnp.concatenate([rows[G * c : G * c + G, :] for c in range(16)], axis=1)
     levels = dot(back_y, thrice(levels))
     for c in range(16):
@@ -225,14 +253,7 @@
     levels = jnp.concatenate([work[pl.ds(s, G, stride=8), :] for s in range(8)], axis=1)
     field = dot(fixed[128:160, 768:960], thrice(levels))
     for s in range(8):
-        work[N * s : N * s + N, :] = field[:, 128 * s : 128 * s + 128]
-
-    def load(c):
-        return work[pl.ds(pl.multiple_of(c * N, N), N), :]
-
-    chunks = torus_roll(load, B - lax.rem(oy, B), B - lax.rem(ox, B))
-    for s in range(8):
-        out[pl.ds(s, N, stride=8), :] = chunks[s]
+        out[pl.ds(s, N, stride=8), :] = field[:, 128 * s : 128 * s + 128]
 
 
 def cube_root(value):

time: 72.6 us -> 72.3 us (level)
  no operation moved by 1% of the time
where the time goes in v6:
time: 72.3 us; the launch traced here: 71.9 us
  starting transfers between devices  25.5 us (35%)
  waiting for transfers between devices  23.3 us (32%)
  blocking collectives  13.8 us (19%)
  Pallas kernels  7.39 us (10%)
  other arithmetic  0.9 us (1%)
  local copies, waits for them, and re-layouts  0.87 us (1%)
    all_to_all x3, waiting for transfers between devices, exchange(): return lax.all_to_all(x, 'own', 0, 0, tiled=True)  22.2 us
    all_to_all x3, starting transfers between devices, exchange(): return lax.all_to_all(x, 'own', 0, 0, tiled=True)  19.9 us
    all_to_all x1, blocking collectives, exchange(): return lax.all_to_all(x, 'own', 0, 0, tiled=True)  13.8 us
    ppermute x3, starting transfers between devices, from_group(): return lax.ppermute(x, 'grp', [(g, (g + step) % 8) for g in range(8)])  5.44 us
    pallas_call x1, Pallas kernels, body(): kernel(solve_kernel, shape((8 * N, 128)), [VM] * 4, 'solve', 16, [pltpu.V...  2.76 us
    pallas_call x1, Pallas kernels, body(): kernel(pack_kernel, shape((N, 16, 128), BF16), [SM, VM], 'pack', 60, [plt...  1.7 us
  transfers between devices with their start and end apart: 7, of which 4 were waited for; matrix products, arithmetic and copies ran while one was open for 2% of the time, Pallas kernels for 5%

profile of v6, /device:TPU:2, one launch (start us, length us, event | category | flops | bytes accessed | tf_op | source)
XLA Modules:
  0.0 71.9 jit_solution(4701552048681203086)
XLA Ops:
  0.0 0.0 copy-start
  0.0 1.7 %pack.1 = bf16[32,16,128]{2,1,0:T(8,128)(2,1)} custom-call(s32[1,2]{1,0:T(1,128)} %corner.1, bf16[1,32,1024]{2,1,0:T(8,128)(2,1)} %box.1), custom_call_target="tpu_custom_call" | custom-call | bytes 200000 | tf_op jit(solution)/shard_map/pack/pallas_call | solution.py:351
  1.7 11.5 %all-to-all-start = ((bf16[32,16,128]{2,1,0:T(8,128)(2,1)}), bf16[32,16,128]{2,1,0:T(8,128)(2,1)S(1)}, u32[]{:S(2)}, u32[]{:S(2)}) async-start(bf16[32,16,128]{2,1,0:T(8,128)(2,1)} %pack.1), calls=%async_computation | async-start | bytes 262144 | tf_op jit(solution)/shard_map/all_to_all | solution.py:323
  13.2 0.9 %convert_reduce_fusion = f32[4096]{0:T(1024)S(1)} fusion(bf16[32,4096]{1,0:T(8,128)(2,1)} %param.8, s32[]{:T(128)S(6)} %select_n.3), kind=kLoop, calls=%fused_computation.1 | loop fusion | flops 4096 | bytes 24580 | tf_op jit(solution)/shard_map/reshape | solution.py:378
  14.1 0.1 reshape.33
  14.2 0.1 reshape.30.plane
  14.3 0.0 copy-start.1
  14.3 0.0 copy-start.2
  14.3 0.0 copy-done
  14.3 0.6 copy-done.1
  15.0 0.0 copy-done.2
  15.0 0.8 %tables.1 = (bf16[256,1024]{1,0:T(8,128)(2,1)S(1)}, s32[16,128]{1,0:T(8,128)S(1)}, s32[8,128]{1,0:T(8,128)S(1)}, f32[1024,256]{1,0:T(8,128)S(1)}) custom-call(s32[1]{0:T(128)} %bitcast.1.owner, s32[1,2]{1,0:T(1,128)S(1)} %copy-done.1, bf16[256,1024]{1,0:T(8,128)(2,1)S(1)} %copy-done, s32[2,32]{1,0:T(2,128)S(1)} %bitcast.12), custom_call_target="tpu_custom_call" | custom-call | flops 2000000 | bytes 3000000 | tf_op jit(solution)/shard_map/tables/pallas_call | solution.py:363
  15.8 7.8 %all-to-all-done.recv = bf16[32,16,128]{2,1,0:T(8,128)(2,1)S(1)} async-done(((bf16[32,16,128]{2,1,0:T(8,128)(2,1)}), bf16[32,16,128]{2,1,0:T(8,128)(2,1)S(1)}, u32[]{:S(2)}, u32[]{:S(2)}) %all-to-all-start) | async-done | bytes 131104 | tf_op jit(solution)/shard_map/all_to_all | solution.py:323
  23.6 0.8 %pair_products.1 = (f32[32,8,128]{2,1,0:T(8,128)}, f32[4,8,128]{2,1,0:T(8,128)S(1)}, f32[32,8,128]{2,1,0:T(8,128)S(1)}, f32[32,8,128]{2,1,0:T(8,128)S(1)}, f32[8,128]{1,0:T(8,128)S(1)}) custom-call(s32[16,128]{1,0:T(8,128)S(1)} %get-tuple-element.33.pairs, bf16[32,16,128]{2,1,0:T(8,128)(2,1)S(1)} %all-to-all-done.recv), custom_call_target="tpu_custom_call" | custom-call | bytes 600000 | tf_op jit(solution)/shard_map/pair_products/pallas_call | solution.py:384
  24.4 3.9 %all-to-all-start.1 = ((f32[32,8,128]{2,1,0:T(8,128)}), f32[32,8,128]{2,1,0:T(8,128)S(1)}, u32[]{:S(2)}, u32[]{:S(2)}) async-start(f32[32,8,128]{2,1,0:T(8,128)} %get-tuple-element.38), calls=%async_computation.1 | async-start | bytes 262144 | tf_op jit(solution)/shard_map/all_to_all | solution.py:323
  28.3 0.6 collective-permute-start.2
  28.9 1.5 %collective-permute-start.1 = (f32[4,8,128]{2,1,0:T(8,128)S(1)}, f32[4,8,128]{2,1,0:T(8,128)S(1)}, u32[]{:S(2)}, u32[]{:S(2)}) collective-permute-start(f32[4,8,128]{2,1,0:T(8,128)S(1)} %get-tuple-element.42), channel_id=1, source_target_pairs={{0,64},{32,96},{64,128},{96,160},{128,192},{160,224},{192,0},{224,... | collective-permute-start | bytes 49160 | tf_op jit(solution)/shard_map/ppermute | solution.py:343
  30.4 3.3 %collective-permute-start = (f32[4,8,128]{2,1,0:T(8,128)S(1)}, f32[4,8,128]{2,1,0:T(8,128)S(1)}, u32[]{:S(2)}, u32[]{:S(2)}) collective-permute-start(f32[4,8,128]{2,1,0:T(8,128)S(1)} %get-tuple-element.42), channel_id=1, source_target_pairs={{0,128},{32,160},{64,192},{96,224},{128,0},{160,32},{192,64},{224,... | collective-permute-start | bytes 49160 | tf_op jit(solution)/shard_map/ppermute | solution.py:343
  33.8 5.2 %all-to-all-done.1 = f32[32,8,128]{2,1,0:T(8,128)S(1)} async-done(((f32[32,8,128]{2,1,0:T(8,128)}), f32[32,8,128]{2,1,0:T(8,128)S(1)}, u32[]{:S(2)}, u32[]{:S(2)}) %all-to-all-start.1) | async-done | bytes 131104 | tf_op jit(solution)/shard_map/all_to_all | solution.py:323
  38.9 2.8 %solve.1 = f32[256,128]{1,0:T(8,128)} custom-call(f32[8,128]{1,0:T(8,128)S(1)} %get-tuple-element.37.place, f32[256,128]{1,0:T(8,128)S(1)} %bitcast.11, bf16[256,1024]{1,0:T(8,128)(2,1)S(1)} %get-tuple-element.39.fixed, f32[1024,256]{1,0:T(8,128)S(1)} %get-tuple-element.40.green), custom_call_target="tpu_custom_call" | custom-call | flops 1000000000 | bytes 3000000 | tf_op jit(solution)/shard_map/solve/pallas_call | solution.py:395
  41.7 4.6 %all-to-all-start.2 = ((f32[32,8,128]{2,1,0:T(8,128)}), f32[32,8,128]{2,1,0:T(8,128)S(1)}, u32[]{:S(2)}, u32[]{:S(2)}) async-start(f32[32,8,128]{2,1,0:T(8,128)} %bitcast.4), calls=%async_computation.2 | async-start | bytes 262144 | tf_op jit(solution)/shard_map/all_to_all | solution.py:323
  46.3 0.0 collective-permute-done.2
  46.3 0.0 collective-permute-done.1
  46.3 0.0 collective-permute-done
  46.3 0.1 collective-permute-start.3
  46.4 1.2 %collective-permute-done.3.other = f32[4,8,128]{2,1,0:T(8,128)S(1)} collective-permute-done((f32[4,8,128]{2,1,0:T(8,128)S(1)}, f32[4,8,128]{2,1,0:T(8,128)S(1)}, u32[]{:S(2)}, u32[]{:S(2)}) %collective-permute-start.3) | collective-permute-done | bytes 16416 | tf_op jit(solution)/shard_map/ppermute | solution.py:342
  47.6 9.2 %all-to-all-done.2.field = f32[32,8,128]{2,1,0:T(8,128)S(1)} async-done(((f32[32,8,128]{2,1,0:T(8,128)}), f32[32,8,128]{2,1,0:T(8,128)S(1)}, u32[]{:S(2)}, u32[]{:S(2)}) %all-to-all-start.2) | async-done | bytes 131104 | tf_op jit(solution)/shard_map/all_to_all | solution.py:323
  56.8 0.3 gradient_planes.1
  57.1 13.8 %all_to_all.20 = f32[32,8,128]{2,1,0:T(8,128)S(1)} all-to-all(f32[32,8,128]{2,1,0:T(8,128)S(1)} %gradient_planes.1), channel_id=1, replica_groups=mesh['grp'=8,'own'=32] {'own'}, dimensions={0} | all-to-all | bytes 262144 | tf_op jit(solution)/shard_map/all_to_all | solution.py:323
  70.9 1.0 %unpack.1 = f32[1,32,1024]{2,1,0:T(8,128)} custom-call(s32[8,128]{1,0:T(8,128)S(1)} %get-tuple-element.32.offsets, f32[256,128]{1,0:T(8,128)S(1)} %bitcast.10), custom_call_target="tpu_custom_call" | custom-call | bytes 300000 | tf_op jit(solution)/shard_map/unpack/pallas_call | solution.py:420
  (2 shorter events, 0.0 us)
Async XLA Ops:
  0.0 14.3 %copy-start = (bf16[256,1024]{1,0:T(8,128)(2,1)S(1)}, bf16[256,1024]{1,0:T(8,128)(2,1)}, u32[]{:S(2)}) copy-start(bf16[256,1024]{1,0:T(8,128)(2,1)} %constant.10.clone.fixed_in) | copy-start | bytes 1572868
  1.7 21.9 %all-to-all-start = ((bf16[32,16,128]{2,1,0:T(8,128)(2,1)}), bf16[32,16,128]{2,1,0:T(8,128)(2,1)S(1)}, u32[]{:S(2)}, u32[]{:S(2)}) async-start(bf16[32,16,128]{2,1,0:T(8,128)(2,1)} %pack.1), calls=%async_computation | async-start | bytes 262144 | tf_op jit(solution)/shard_map/all_to_all | solution.py:323
  14.3 0.7 copy-start.1
  14.3 0.7 copy-start.2
  24.4 14.5 %all-to-all-start.1 = ((f32[32,8,128]{2,1,0:T(8,128)}), f32[32,8,128]{2,1,0:T(8,128)S(1)}, u32[]{:S(2)}, u32[]{:S(2)}) async-start(f32[32,8,128]{2,1,0:T(8,128)} %get-tuple-element.38), calls=%async_computation.1 | async-start | bytes 262144 | tf_op jit(solution)/shard_map/all_to_all | solution.py:323
  28.3 18.0 %collective-permute-start.2 = (f32[4,8,128]{2,1,0:T(8,128)S(1)}, f32[4,8,128]{2,1,0:T(8,128)S(1)}, u32[]{:S(2)}, u32[]{:S(2)}) collective-permute-start(f32[4,8,128]{2,1,0:T(8,128)S(1)} %get-tuple-element.42), channel_id=1, source_target_pairs={{0,192},{32,224},{64,0},{96,32},{128,64},{160,96},{192,128},{224,1... | collective-permute-start | bytes 49160 | tf_op jit(solution)/shard_map/ppermute | solution.py:343
  28.9 17.4 %collective-permute-start.1 = (f32[4,8,128]{2,1,0:T(8,128)S(1)}, f32[4,8,128]{2,1,0:T(8,128)S(1)}, u32[]{:S(2)}, u32[]{:S(2)}) collective-permute-start(f32[4,8,128]{2,1,0:T(8,128)S(1)} %get-tuple-element.42), channel_id=1, source_target_pairs={{0,64},{32,96},{64,128},{96,160},{128,192},{160,224},{192,0},{224,... | collective-permute-start | bytes 49160 | tf_op jit(solution)/shard_map/ppermute | solution.py:343
  30.4 15.9 %collective-permute-start = (f32[4,8,128]{2,1,0:T(8,128)S(1)}, f32[4,8,128]{2,1,0:T(8,128)S(1)}, u32[]{:S(2)}, u32[]{:S(2)}) collective-permute-start(f32[4,8,128]{2,1,0:T(8,128)S(1)} %get-tuple-element.42), channel_id=1, source_target_pairs={{0,128},{32,160},{64,192},{96,224},{128,0},{160,32},{192,64},{224,... | collective-permute-start | bytes 49160 | tf_op jit(solution)/shard_map/ppermute | solution.py:343
  41.7 15.1 %all-to-all-start.2 = ((f32[32,8,128]{2,1,0:T(8,128)}), f32[32,8,128]{2,1,0:T(8,128)S(1)}, u32[]{:S(2)}, u32[]{:S(2)}) async-start(f32[32,8,128]{2,1,0:T(8,128)} %bitcast.4), calls=%async_computation.2 | async-start | bytes 262144 | tf_op jit(solution)/shard_map/all_to_all | solution.py:323
  46.3 1.3 %collective-permute-start.3 = (f32[4,8,128]{2,1,0:T(8,128)S(1)}, f32[4,8,128]{2,1,0:T(8,128)S(1)}, u32[]{:S(2)}, u32[]{:S(2)}) collective-permute-start(f32[4,8,128]{2,1,0:T(8,128)S(1)} %add_add_fusion.dens), channel_id=1, source_target_pairs={{0,32},{32,0},{64,96},{96,64},{128,160},{160,128},{192,224},{224,1... | collective-permute-start | bytes 49160 | tf_op jit(solution)/shard_map/ppermute | solution.py:342

commit v7 on v6

--- a/solution.py
+++ b/solution.py
@@ -337,10 +337,8 @@
     )
 
 
-def from_group(x, step):
-    if step == 1:
-        return lax.ppermute(x, "grp", [(g, g ^ 1) for g in range(8)])
-    return lax.ppermute(x, "grp", [(g, (g + step) % 8) for g in range(8)])
+def swapped(x, bits):
+    return lax.ppermute(x, "grp", [(g, g ^ bits) for g in range(8)])
 
 
 def body(orbitals, offsets, pairs, ext_pot):
@@ -391,7 +389,7 @@
     )(pairs, recv)
 
     mine = exchange(rho)
-    others = [from_group(dens, step) for step in (2, 4, 6)]
+    others = [swapped(dens, step) for step in (2, 4, 6)]
     field = kernel(
         solve_kernel,
         shape((8 * N, 128)),
@@ -404,7 +402,7 @@
     )(place, mine.reshape(8 * N, 128), fixed, green)
     fields = exchange(field.reshape(N, 8, 128))
     dens = (dens + others[1]) + (others[0] + others[2])
-    other = from_group(dens, 1)
+    other = swapped(dens, 1)
 
     gradient = kernel(
         gradient_kernel,

time: 72.3 us -> 71.6 us (level)
  starting transfers between devices: 25.5 us -> 22.9 us
  waiting for transfers between devices: 23.3 us -> 25.3 us
    all_to_all x3, waiting for transfers between devices: 22.2 us -> 24.1 us  [exchange(): return lax.all_to_all(x, 'own', 0, 0, tiled=True)]
    ppermute x4, starting transfers between devices: 5.53 us -> 3.67 us  [swapped(): return lax.ppermute(x, 'grp', [(g, g ^ bits) for g in range(8)])]
    all_to_all x3, starting transfers between devices: 19.9 us -> 19.2 us  [exchange(): return lax.all_to_all(x, 'own', 0, 0, tiled=True)]
where the time goes in v7:
time: 71.6 us; the launch traced here: 71.1 us
  waiting for transfers between devices  25.3 us (35%)
  starting transfers between devices  22.9 us (32%)
  blocking collectives  13.7 us (19%)
  Pallas kernels  7.39 us (10%)
  other arithmetic  0.9 us (1%)
  local copies, waits for them, and re-layouts  0.87 us (1%)
    all_to_all x3, waiting for transfers between devices, exchange(): return lax.all_to_all(x, 'own', 0, 0, tiled=True)  24.1 us
    all_to_all x3, starting transfers between devices, exchange(): return lax.all_to_all(x, 'own', 0, 0, tiled=True)  19.2 us
    all_to_all x1, blocking collectives, exchange(): return lax.all_to_all(x, 'own', 0, 0, tiled=True)  13.7 us
    ppermute x4, starting transfers between devices, swapped(): return lax.ppermute(x, 'grp', [(g, g ^ bits) for g in range(8)])  3.67 us
    pallas_call x1, Pallas kernels, body(): kernel(solve_kernel, shape((8 * N, 128)), [VM] * 4, 'solve', 16, [pltpu.V...  2.76 us
    pallas_call x1, Pallas kernels, body(): kernel(pack_kernel, shape((N, 16, 128), BF16), [SM, VM], 'pack', 60, [plt...  1.7 us
  transfers between devices with their start and end apart: 7, of which 4 were waited for; matrix products, arithmetic and copies ran while one was open for 2% of the time, Pallas kernels for 5%

profile of v7, /device:TPU:2, one launch (start us, length us, event | category | flops | bytes accessed | tf_op | source)
XLA Modules:
  0.0 71.1 jit_solution(5797001981270655685)
XLA Ops:
  0.0 0.0 copy-start
  0.0 1.7 %pack.1 = bf16[32,16,128]{2,1,0:T(8,128)(2,1)} custom-call(s32[1,2]{1,0:T(1,128)} %corner.1, bf16[1,32,1024]{2,1,0:T(8,128)(2,1)} %box.1), custom_call_target="tpu_custom_call" | custom-call | bytes 200000 | tf_op jit(solution)/shard_map/pack/pallas_call | solution.py:349
  1.7 11.5 %all-to-all-start = ((bf16[32,16,128]{2,1,0:T(8,128)(2,1)}), bf16[32,16,128]{2,1,0:T(8,128)(2,1)S(1)}, u32[]{:S(2)}, u32[]{:S(2)}) async-start(bf16[32,16,128]{2,1,0:T(8,128)(2,1)} %pack.1), calls=%async_computation | async-start | bytes 262144 | tf_op jit(solution)/shard_map/all_to_all | solution.py:323
  13.2 0.9 %convert_reduce_fusion = f32[4096]{0:T(1024)S(1)} fusion(bf16[32,4096]{1,0:T(8,128)(2,1)} %param.8, s32[]{:T(128)S(6)} %select_n.3), kind=kLoop, calls=%fused_computation.1 | loop fusion | flops 4096 | bytes 24580 | tf_op jit(solution)/shard_map/reshape | solution.py:376
  14.1 0.1 reshape.33
  14.2 0.1 reshape.30.plane
  14.3 0.0 copy-start.1
  14.3 0.0 copy-start.2
  14.3 0.0 copy-done
  14.3 0.6 copy-done.1
  15.0 0.0 copy-done.2
  15.0 0.8 %tables.1 = (bf16[256,1024]{1,0:T(8,128)(2,1)S(1)}, s32[16,128]{1,0:T(8,128)S(1)}, s32[8,128]{1,0:T(8,128)S(1)}, f32[1024,256]{1,0:T(8,128)S(1)}) custom-call(s32[1]{0:T(128)} %bitcast.1.owner, s32[1,2]{1,0:T(1,128)S(1)} %copy-done.1, bf16[256,1024]{1,0:T(8,128)(2,1)S(1)} %copy-done, s32[2,32]{1,0:T(2,128)S(1)} %bitcast.12), custom_call_target="tpu_custom_call" | custom-call | flops 2000000 | bytes 3000000 | tf_op jit(solution)/shard_map/tables/pallas_call | solution.py:361
  15.8 7.8 %all-to-all-done.recv = bf16[32,16,128]{2,1,0:T(8,128)(2,1)S(1)} async-done(((bf16[32,16,128]{2,1,0:T(8,128)(2,1)}), bf16[32,16,128]{2,1,0:T(8,128)(2,1)S(1)}, u32[]{:S(2)}, u32[]{:S(2)}) %all-to-all-start) | async-done | bytes 131104 | tf_op jit(solution)/shard_map/all_to_all | solution.py:323
  23.6 0.8 %pair_products.1 = (f32[32,8,128]{2,1,0:T(8,128)}, f32[4,8,128]{2,1,0:T(8,128)S(1)}, f32[32,8,128]{2,1,0:T(8,128)S(1)}, f32[32,8,128]{2,1,0:T(8,128)S(1)}, f32[8,128]{1,0:T(8,128)S(1)}) custom-call(s32[16,128]{1,0:T(8,128)S(1)} %get-tuple-element.33.pairs, bf16[32,16,128]{2,1,0:T(8,128)(2,1)S(1)} %all-to-all-done.recv), custom_call_target="tpu_custom_call" | custom-call | bytes 600000 | tf_op jit(solution)/shard_map/pair_products/pallas_call | solution.py:382
  24.4 3.9 %all-to-all-start.1 = ((f32[32,8,128]{2,1,0:T(8,128)}), f32[32,8,128]{2,1,0:T(8,128)S(1)}, u32[]{:S(2)}, u32[]{:S(2)}) async-start(f32[32,8,128]{2,1,0:T(8,128)} %get-tuple-element.38), calls=%async_computation.1 | async-start | bytes 262144 | tf_op jit(solution)/shard_map/all_to_all | solution.py:323
  28.3 1.6 %collective-permute-start.2 = (f32[4,8,128]{2,1,0:T(8,128)S(1)}, f32[4,8,128]{2,1,0:T(8,128)S(1)}, u32[]{:S(2)}, u32[]{:S(2)}) collective-permute-start(f32[4,8,128]{2,1,0:T(8,128)S(1)} %get-tuple-element.42), channel_id=1, source_target_pairs={{0,192},{32,224},{64,128},{96,160},{128,64},{160,96},{192,0},{224,... | collective-permute-start | bytes 49160 | tf_op jit(solution)/shard_map/ppermute | solution.py:341
  29.9 1.8 %collective-permute-start.1 = (f32[4,8,128]{2,1,0:T(8,128)S(1)}, f32[4,8,128]{2,1,0:T(8,128)S(1)}, u32[]{:S(2)}, u32[]{:S(2)}) collective-permute-start(f32[4,8,128]{2,1,0:T(8,128)S(1)} %get-tuple-element.42), channel_id=1, source_target_pairs={{0,64},{32,96},{64,0},{96,32},{128,192},{160,224},{192,128},{224,1... | collective-permute-start | bytes 49160 | tf_op jit(solution)/shard_map/ppermute | solution.py:341
  31.7 0.2 collective-permute-start
  31.9 7.0 %all-to-all-done.1 = f32[32,8,128]{2,1,0:T(8,128)S(1)} async-done(((f32[32,8,128]{2,1,0:T(8,128)}), f32[32,8,128]{2,1,0:T(8,128)S(1)}, u32[]{:S(2)}, u32[]{:S(2)}) %all-to-all-start.1) | async-done | bytes 131104 | tf_op jit(solution)/shard_map/all_to_all | solution.py:323
  38.9 2.8 %solve.1 = f32[256,128]{1,0:T(8,128)} custom-call(f32[8,128]{1,0:T(8,128)S(1)} %get-tuple-element.37.place, f32[256,128]{1,0:T(8,128)S(1)} %bitcast.11, bf16[256,1024]{1,0:T(8,128)(2,1)S(1)} %get-tuple-element.39.fixed, f32[1024,256]{1,0:T(8,128)S(1)} %get-tuple-element.40.green), custom_call_target="tpu_custom_call" | custom-call | flops 1000000000 | bytes 3000000 | tf_op jit(solution)/shard_map/solve/pallas_call | solution.py:393
  41.7 3.9 %all-to-all-start.2 = ((f32[32,8,128]{2,1,0:T(8,128)}), f32[32,8,128]{2,1,0:T(8,128)S(1)}, u32[]{:S(2)}, u32[]{:S(2)}) async-start(f32[32,8,128]{2,1,0:T(8,128)} %bitcast.4), calls=%async_computation.2 | async-start | bytes 262144 | tf_op jit(solution)/shard_map/all_to_all | solution.py:323
  45.6 0.0 collective-permute-done.2
  45.6 0.0 collective-permute-done.1
  45.6 0.0 collective-permute-done
  45.6 0.1 collective-permute-start.3
  45.7 1.2 %collective-permute-done.3.other = f32[4,8,128]{2,1,0:T(8,128)S(1)} collective-permute-done((f32[4,8,128]{2,1,0:T(8,128)S(1)}, f32[4,8,128]{2,1,0:T(8,128)S(1)}, u32[]{:S(2)}, u32[]{:S(2)}) %collective-permute-start.3) | collective-permute-done | bytes 16416 | tf_op jit(solution)/shard_map/ppermute | solution.py:341
  46.9 9.2 %all-to-all-done.2.field = f32[32,8,128]{2,1,0:T(8,128)S(1)} async-done(((f32[32,8,128]{2,1,0:T(8,128)}), f32[32,8,128]{2,1,0:T(8,128)S(1)}, u32[]{:S(2)}, u32[]{:S(2)}) %all-to-all-start.2) | async-done | bytes 131104 | tf_op jit(solution)/shard_map/all_to_all | solution.py:323
  56.1 0.3 gradient_planes.1
  56.4 13.7 %all_to_all.20 = f32[32,8,128]{2,1,0:T(8,128)S(1)} all-to-all(f32[32,8,128]{2,1,0:T(8,128)S(1)} %gradient_planes.1), channel_id=1, replica_groups=mesh['grp'=8,'own'=32] {'own'}, dimensions={0} | all-to-all | bytes 262144 | tf_op jit(solution)/shard_map/all_to_all | solution.py:323
  70.1 1.0 %unpack.1 = f32[1,32,1024]{2,1,0:T(8,128)} custom-call(s32[8,128]{1,0:T(8,128)S(1)} %get-tuple-element.32.offsets, f32[256,128]{1,0:T(8,128)S(1)} %bitcast.10), custom_call_target="tpu_custom_call" | custom-call | bytes 300000 | tf_op jit(solution)/shard_map/unpack/pallas_call | solution.py:418
  (2 shorter events, 0.0 us)
Async XLA Ops:
  0.0 14.3 %copy-start = (bf16[256,1024]{1,0:T(8,128)(2,1)S(1)}, bf16[256,1024]{1,0:T(8,128)(2,1)}, u32[]{:S(2)}) copy-start(bf16[256,1024]{1,0:T(8,128)(2,1)} %constant.10.clone.fixed_in) | copy-start | bytes 1572868
  1.7 21.9 %all-to-all-start = ((bf16[32,16,128]{2,1,0:T(8,128)(2,1)}), bf16[32,16,128]{2,1,0:T(8,128)(2,1)S(1)}, u32[]{:S(2)}, u32[]{:S(2)}) async-start(bf16[32,16,128]{2,1,0:T(8,128)(2,1)} %pack.1), calls=%async_computation | async-start | bytes 262144 | tf_op jit(solution)/shard_map/all_to_all | solution.py:323
  14.3 0.7 copy-start.1
  14.3 0.7 copy-start.2
  24.4 14.5 %all-to-all-start.1 = ((f32[32,8,128]{2,1,0:T(8,128)}), f32[32,8,128]{2,1,0:T(8,128)S(1)}, u32[]{:S(2)}, u32[]{:S(2)}) async-start(f32[32,8,128]{2,1,0:T(8,128)} %get-tuple-element.38), calls=%async_computation.1 | async-start | bytes 262144 | tf_op jit(solution)/shard_map/all_to_all | solution.py:323
  28.3 17.2 %collective-permute-start.2 = (f32[4,8,128]{2,1,0:T(8,128)S(1)}, f32[4,8,128]{2,1,0:T(8,128)S(1)}, u32[]{:S(2)}, u32[]{:S(2)}) collective-permute-start(f32[4,8,128]{2,1,0:T(8,128)S(1)} %get-tuple-element.42), channel_id=1, source_target_pairs={{0,192},{32,224},{64,128},{96,160},{128,64},{160,96},{192,0},{224,... | collective-permute-start | bytes 49160 | tf_op jit(solution)/shard_map/ppermute | solution.py:341
  29.9 15.7 %collective-permute-start.1 = (f32[4,8,128]{2,1,0:T(8,128)S(1)}, f32[4,8,128]{2,1,0:T(8,128)S(1)}, u32[]{:S(2)}, u32[]{:S(2)}) collective-permute-start(f32[4,8,128]{2,1,0:T(8,128)S(1)} %get-tuple-element.42), channel_id=1, source_target_pairs={{0,64},{32,96},{64,0},{96,32},{128,192},{160,224},{192,128},{224,1... | collective-permute-start | bytes 49160 | tf_op jit(solution)/shard_map/ppermute | solution.py:341
  31.7 13.9 %collective-permute-start = (f32[4,8,128]{2,1,0:T(8,128)S(1)}, f32[4,8,128]{2,1,0:T(8,128)S(1)}, u32[]{:S(2)}, u32[]{:S(2)}) collective-permute-start(f32[4,8,128]{2,1,0:T(8,128)S(1)} %get-tuple-element.42), channel_id=1, source_target_pairs={{0,128},{32,160},{64,192},{96,224},{128,0},{160,32},{192,64},{224,... | collective-permute-start | bytes 49160 | tf_op jit(solution)/shard_map/ppermute | solution.py:341
  41.7 14.4 %all-to-all-start.2 = ((f32[32,8,128]{2,1,0:T(8,128)}), f32[32,8,128]{2,1,0:T(8,128)S(1)}, u32[]{:S(2)}, u32[]{:S(2)}) async-start(f32[32,8,128]{2,1,0:T(8,128)} %bitcast.4), calls=%async_computation.2 | async-start | bytes 262144 | tf_op jit(solution)/shard_map/all_to_all | solution.py:323
  45.6 1.3 %collective-permute-start.3 = (f32[4,8,128]{2,1,0:T(8,128)S(1)}, f32[4,8,128]{2,1,0:T(8,128)S(1)}, u32[]{:S(2)}, u32[]{:S(2)}) collective-permute-start(f32[4,8,128]{2,1,0:T(8,128)S(1)} %add_add_fusion.dens), channel_id=1, source_target_pairs={{0,32},{32,0},{64,96},{96,64},{128,160},{160,128},{192,224},{224,1... | collective-permute-start | bytes 49160 | tf_op jit(solution)/shard_map/ppermute | solution.py:341

commit v8 on v7

--- a/solution.py
+++ b/solution.py
@@ -113,8 +113,9 @@
         square = plane * plane
         for q in range(4):
             total[q] = total[q] + jnp.where(quarter == float(q), square, 0.0)
-    for q in range(4):
-        dens[q] = total[q]
+    for g in range(8):
+        for q in range(4):
+            dens[g, q] = total[q]
     place[...] = recv[first].astype(F32)[8:]
     for p in range(N):
         a, b = numbers[p]
@@ -262,11 +263,10 @@
     return jnp.where(value > 0.0, finer, 0.0)
 
 
-def gradient_kernel(pairs, phi, code, field, plane, dens, other, out, terms):
+def gradient_kernel(pairs, phi, code, field, plane, gathered, out, terms, dens, sem):
+    fetch = pltpu.make_async_copy(gathered.at[:, 0], dens, sem)
+    fetch.start()
     numbers = pair_numbers(pairs)
-    quarters = []
-    for q in range(4):
-        quarters.append(plane[q] - EXCHANGE_COEF * cube_root(dens[q] + other[q]))
     for n in range(N):
         terms[n] = jnp.zeros((8, 128), F32)
     for p in range(N):
@@ -274,6 +274,13 @@
         value = jnp.where(code[a] == code[b], field[p], 0.0)
         terms[a] = terms[a] + value * phi[b]
         terms[b] = terms[b] + value * phi[a]
+    fetch.wait()
+    quarters = []
+    for q in range(4):
+        total = dens[0, q]
+        for g in range(1, 8):
+            total = total + dens[g, q]
+        quarters.append(plane[q] - EXCHANGE_COEF * cube_root(total))
     for n in range(N):
         quarter = code[n]
         local = jnp.where(
@@ -335,10 +342,6 @@
         cost_estimate=pl.CostEstimate(flops=flops, bytes_accessed=moved, transcendentals=0),
         name=name,
     )
-
-
-def swapped(x, bits):
-    return lax.ppermute(x, "grp", [(g, g ^ bits) for g in range(8)])
 
 
 def body(orbitals, offsets, pairs, ext_pot):
@@ -381,7 +384,7 @@
     planes = shape((N, 8, 128))
     rho, dens, phi, code, place = kernel(
         pair_kernel,
-        [planes, shape((4, 8, 128)), planes, planes, shape((8, 128))],
+        [planes, shape((8, 4, 8, 128)), planes, planes, shape((8, 128))],
         [VM, VM],
         "pair_products",
         4,
@@ -389,7 +392,7 @@
     )(pairs, recv)
 
     mine = exchange(rho)
-    others = [swapped(dens, step) for step in (2, 4, 6)]
+    gathered = lax.all_gather(dens, "grp", axis=0)
     field = kernel(
         solve_kernel,
         shape((8 * N, 128)),
@@ -401,18 +404,19 @@
         moved=3_000_000,
     )(place, mine.reshape(8 * N, 128), fixed, green)
     fields = exchange(field.reshape(N, 8, 128))
-    dens = (dens + others[1]) + (others[0] + others[2])
-    other = swapped(dens, 1)
-
     gradient = kernel(
         gradient_kernel,
         shape((N, 8, 128)),
-        [VM] * 7,
+        [VM] * 5 + [pl.BlockSpec(memory_space=pltpu.HBM)],
         "gradient_planes",
-        4,
-        [pltpu.VMEM((N, 8, 128), F32)],
+        53,
+        [
+            pltpu.VMEM((N, 8, 128), F32),
+            pltpu.VMEM((8, 4, 8, 128), F32),
+            pltpu.SemaphoreType.DMA(()),
+        ],
         moved=600_000,
-    )(pairs, phi, code, fields, plane, dens, other)
+    )(pairs, phi, code, fields, plane, gathered)
     back = exchange(gradient)
 
     return kernel(

time: 71.6 us -> 84 us (1.17)
  blocking collectives: 13.7 us -> 41.4 us
  waiting for transfers between devices: 25.3 us -> 7.79 us
  between operations: 0.12 us -> 13.5 us
  starting transfers between devices: 22.9 us -> 11.5 us
    all_to_all x1 -> x3, blocking collectives: 13.7 us -> 41.4 us  [exchange(): return lax.all_to_all(x, 'own', 0, 0, tiled=True)]
    all_to_all x3 -> x1, waiting for transfers between devices: 24.1 us -> 7.77 us  [exchange(): return lax.all_to_all(x, 'own', 0, 0, tiled=True)]
    all_to_all x3 -> x1, starting transfers between devices: 19.2 us -> 11.5 us  [exchange(): return lax.all_to_all(x, 'own', 0, 0, tiled=True)]
    ppermute x4 -> x0, starting transfers between devices: 3.67 us -> none  [swapped(): return lax.ppermute(x, 'grp', [(g, g ^ bits) for g in range(8)])]
    ppermute x4 -> x0, waiting for transfers between devices: 1.18 us -> none  [swapped(): return lax.ppermute(x, 'grp', [(g, g ^ bits) for g in range(8)])]
    pallas_call x2, Pallas kernels: 1.11 us -> 2.04 us  [the longest x1 1.21 us: body(): kernel(gradient_kernel, shape((N, 8, 128)), [VM] * 5 + [pl.BlockSpec(memo...]
  transfers between devices with their start and end apart: 7 -> 2, of which waited for: 4 -> 1; matrix products, arithmetic and copies ran while one was open for 2% -> 1% of each run, Pallas kernels for 5% -> 3%
where the time goes in v8:
time: 84 us; the launch traced here: 83.6 us
  blocking collectives  41.4 us (49%)
  between operations  13.5 us (16%)
  starting transfers between devices  11.5 us (14%)
  waiting for transfers between devices  7.79 us (9%)
  Pallas kernels  7.67 us (9%)
  other arithmetic  0.89 us (1%)
  local copies, waits for them, and re-layouts  0.87 us (1%)
    all_to_all x3, blocking collectives, exchange(): return lax.all_to_all(x, 'own', 0, 0, tiled=True)  41.4 us
    all_to_all x1, starting transfers between devices, exchange(): return lax.all_to_all(x, 'own', 0, 0, tiled=True)  11.5 us
    all_to_all x1, waiting for transfers between devices, exchange(): return lax.all_to_all(x, 'own', 0, 0, tiled=True)  7.77 us
    pallas_call x1, Pallas kernels, body(): kernel(solve_kernel, shape((8 * N, 128)), [VM] * 4, 'solve', 16, [pltpu.V...  2.11 us
    pallas_call x1, Pallas kernels, body(): kernel(pack_kernel, shape((N, 16, 128), BF16), [SM, VM], 'pack', 60, [plt...  1.7 us
  transfers between devices with their start and end apart: 2, of which 1 were waited for; matrix products, arithmetic and copies ran while one was open for 1% of the time, Pallas kernels for 3%

profile of v8, /device:TPU:2, one launch (start us, length us, event | category | flops | bytes accessed | tf_op | source)
XLA Modules:
  0.0 83.6 jit_solution(5368220772487256347)
XLA Ops:
  6.5 0.0 copy-start
  6.5 1.7 %pack.1 = bf16[32,16,128]{2,1,0:T(8,128)(2,1)} custom-call(s32[1,2]{1,0:T(1,128)} %corner.1, bf16[1,32,1024]{2,1,0:T(8,128)(2,1)} %box.1), custom_call_target="tpu_custom_call" | custom-call | bytes 200000 | tf_op jit(solution)/shard_map/pack/pallas_call | solution.py:352
  8.2 11.5 %all-to-all-start = ((bf16[32,16,128]{2,1,0:T(8,128)(2,1)}), bf16[32,16,128]{2,1,0:T(8,128)(2,1)S(1)}, u32[]{:S(2)}, u32[]{:S(2)}) async-start(bf16[32,16,128]{2,1,0:T(8,128)(2,1)} %pack.1), calls=%async_computation | async-start | bytes 262144 | tf_op jit(solution)/shard_map/all_to_all | solution.py:330
  19.7 0.0 all-gather.3.cloned.1.call-start
  19.8 0.9 %convert_reduce_fusion = f32[4096]{0:T(1024)S(1)} fusion(bf16[32,4096]{1,0:T(8,128)(2,1)} %param.8, s32[]{:T(128)S(6)} %select_n.3), kind=kLoop, calls=%fused_computation.1 | loop fusion | flops 4096 | bytes 24580 | tf_op jit(solution)/shard_map/reshape | solution.py:379
  20.7 0.1 reshape.33
  20.8 0.1 reshape.30.plane
  20.9 0.0 copy-start.1
  20.9 0.0 copy-start.2
  20.9 0.0 copy-done
  20.9 0.6 copy-done.1
  21.6 0.0 copy-done.2
  21.6 0.8 tables.1
  22.4 7.8 %all-to-all-done.recv = bf16[32,16,128]{2,1,0:T(8,128)(2,1)S(1)} async-done(((bf16[32,16,128]{2,1,0:T(8,128)(2,1)}), bf16[32,16,128]{2,1,0:T(8,128)(2,1)S(1)}, u32[]{:S(2)}, u32[]{:S(2)}) %all-to-all-start) | async-done | bytes 131104 | tf_op jit(solution)/shard_map/all_to_all | solution.py:330
  30.2 0.8 pair_products.1
  31.0 0.0 all-gather.3.cloned.1.call-update
  31.0 13.9 %all_to_all.20 = f32[32,8,128]{2,1,0:T(8,128)S(1)} all-to-all(f32[32,8,128]{2,1,0:T(8,128)S(1)} %get-tuple-element.38), channel_id=1, replica_groups=mesh['grp'=8,'own'=32] {'own'}, dimensions={0} | all-to-all | bytes 262144 | tf_op jit(solution)/shard_map/all_to_all | solution.py:330
  45.0 2.1 %solve.1 = f32[256,128]{1,0:T(8,128)S(1)} custom-call(f32[8,128]{1,0:T(8,128)S(1)} %get-tuple-element.37.place, f32[256,128]{1,0:T(8,128)S(1)} %bitcast.12, bf16[256,1024]{1,0:T(8,128)(2,1)S(1)} %get-tuple-element.39.fixed, f32[1024,256]{1,0:T(8,128)S(1)} %get-tuple-element.40.green), custom_call_target="tpu_custom_call" | custom-call | flops 1000000000 | bytes 3000000 | tf_op jit(solution)/shard_map/solve/pallas_call | solution.py:396
  47.1 13.6 %all_to_all.21.field = f32[32,8,128]{2,1,0:T(8,128)S(1)} all-to-all(f32[32,8,128]{2,1,0:T(8,128)S(1)} %bitcast.13), channel_id=1, replica_groups=mesh['grp'=8,'own'=32] {'own'}, dimensions={0} | all-to-all | bytes 262144 | tf_op jit(solution)/shard_map/all_to_all | solution.py:330
  60.7 0.0 all-gather.3.cloned.1.call-done
  60.7 1.2 %gradient_planes.1 = f32[32,8,128]{2,1,0:T(8,128)S(1)} custom-call(s32[16,128]{1,0:T(8,128)S(1)} %get-tuple-element.33.pairs, f32[32,8,128]{2,1,0:T(8,128)S(1)} %get-tuple-element.35.phi, f32[32,8,128]{2,1,0:T(8,128)S(1)} %get-tuple-element.36.code, f32[32,8,128]{2,1,0:T(8,128)S(1)} %all_to_all.21.field, f32[4,8,128]{2,1,0:T(8,128)S(1)} %reshape.30.plane, ...), custom_call_target="tpu_custom_call" | custom-call | bytes 600000 | tf_op jit(solution)/shard_map/gradient_planes/pallas_call | solution.py:407
  61.9 13.9 %all_to_all.22 = f32[32,8,128]{2,1,0:T(8,128)S(1)} all-to-all(f32[32,8,128]{2,1,0:T(8,128)S(1)} %gradient_planes.1), channel_id=1, replica_groups=mesh['grp'=8,'own'=32] {'own'}, dimensions={0} | all-to-all | bytes 262144 | tf_op jit(solution)/shard_map/all_to_all | solution.py:330
  75.8 1.0 %unpack.1 = f32[1,32,1024]{2,1,0:T(8,128)} custom-call(s32[8,128]{1,0:T(8,128)S(1)} %get-tuple-element.32.offsets, f32[256,128]{1,0:T(8,128)S(1)} %bitcast.11), custom_call_target="tpu_custom_call" | custom-call | bytes 300000 | tf_op jit(solution)/shard_map/unpack/pallas_call | solution.py:422
  (1 shorter events, 0.0 us)
Async XLA Ops:
  6.5 14.4 %copy-start = (bf16[256,1024]{1,0:T(8,128)(2,1)S(1)}, bf16[256,1024]{1,0:T(8,128)(2,1)}, u32[]{:S(2)}) copy-start(bf16[256,1024]{1,0:T(8,128)(2,1)} %constant.10.clone.fixed_in) | copy-start | bytes 1572868
  8.2 21.9 %all-to-all-start = ((bf16[32,16,128]{2,1,0:T(8,128)(2,1)}), bf16[32,16,128]{2,1,0:T(8,128)(2,1)S(1)}, u32[]{:S(2)}, u32[]{:S(2)}) async-start(bf16[32,16,128]{2,1,0:T(8,128)(2,1)} %pack.1), calls=%async_computation | async-start | bytes 262144 | tf_op jit(solution)/shard_map/all_to_all | solution.py:330
  19.7 40.9 %all-gather.3.cloned.1.call-start = ((), (), s32[]{:S(2)}) async-start(), calls=%async_computation.4 | async-start | bytes 1179648 | tf_op jit(solution)/shard_map/all_gather | solution.py:395
  20.9 0.7 copy-start.1
  20.9 0.7 copy-start.2
Sparse Core Ops, SparseCore 0:
  31.2 19.3 all-gather.2

commit v9 on v7

--- a/solution.py
+++ b/solution.py
@@ -389,7 +389,10 @@
     )(pairs, recv)
 
     mine = exchange(rho)
-    others = [swapped(dens, step) for step in (2, 4, 6)]
+    dens = dens + swapped(dens, 2)
+    dens = dens + swapped(dens, 4)
+    mine, dens = lax.optimization_barrier((mine, dens))
+    other = swapped(dens, 1)
     field = kernel(
         solve_kernel,
         shape((8 * N, 128)),
@@ -400,9 +403,8 @@
         flops=1_000_000_000,
         moved=3_000_000,
     )(place, mine.reshape(8 * N, 128), fixed, green)
+    field, other = lax.optimization_barrier((field, other))
     fields = exchange(field.reshape(N, 8, 128))
-    dens = (dens + others[1]) + (others[0] + others[2])
-    other = swapped(dens, 1)
 
     gradient = kernel(
         gradient_kernel,

time: 71.6 us -> 75.8 us (1.059)
  blocking collectives: 13.7 us -> 33.1 us
  waiting for transfers between devices: 25.3 us -> 15.7 us
  starting transfers between devices: 22.9 us -> 18.1 us
    all_to_all x1 -> x2, blocking collectives: 13.7 us -> 33.1 us  [exchange(): return lax.all_to_all(x, 'own', 0, 0, tiled=True)]
    all_to_all x3 -> x2, waiting for transfers between devices: 24.1 us -> 9.35 us  [exchange(): return lax.all_to_all(x, 'own', 0, 0, tiled=True)]
    ppermute x4 -> x3, waiting for transfers between devices: 1.18 us -> 6.33 us  [swapped(): return lax.ppermute(x, 'grp', [(g, g ^ bits) for g in range(8)])]
    all_to_all x3 -> x2, starting transfers between devices: 19.2 us -> 15.3 us  [exchange(): return lax.all_to_all(x, 'own', 0, 0, tiled=True)]
    ppermute x4 -> x3, starting transfers between devices: 3.67 us -> 2.75 us  [swapped(): return lax.ppermute(x, 'grp', [(g, g ^ bits) for g in range(8)])]
  transfers between devices with their start and end apart: 7 -> 5, of which waited for: 4 -> 4; matrix products, arithmetic and copies ran while one was open for 2% -> 1% of each run, Pallas kernels for 5% -> 4%
where the time goes in v9:
time: 75.8 us; the launch traced here: 75.5 us
  blocking collectives  33.1 us (44%)
  starting transfers between devices  18.1 us (24%)
  waiting for transfers between devices  15.7 us (21%)
  Pallas kernels  6.73 us (9%)
  other arithmetic  0.9 us (1%)
  local copies, waits for them, and re-layouts  0.87 us (1%)
    all_to_all x2, blocking collectives, exchange(): return lax.all_to_all(x, 'own', 0, 0, tiled=True)  33.1 us
    all_to_all x2, starting transfers between devices, exchange(): return lax.all_to_all(x, 'own', 0, 0, tiled=True)  15.3 us
    all_to_all x2, waiting for transfers between devices, exchange(): return lax.all_to_all(x, 'own', 0, 0, tiled=True)  9.35 us
    ppermute x3, waiting for transfers between devices, swapped(): return lax.ppermute(x, 'grp', [(g, g ^ bits) for g in range(8)])  6.33 us
    ppermute x3, starting transfers between devices, swapped(): return lax.ppermute(x, 'grp', [(g, g ^ bits) for g in range(8)])  2.75 us
    pallas_call x1, Pallas kernels, body(): kernel(solve_kernel, shape((8 * N, 128)), [VM] * 4, 'solve', 16, [pltpu.V...  2.1 us
    pallas_call x1, Pallas kernels, body(): kernel(pack_kernel, shape((N, 16, 128), BF16), [SM, VM], 'pack', 60, [plt...  1.7 us
  transfers between devices with their start and end apart: 5, of which 4 were waited for; matrix products, arithmetic and copies ran while one was open for 1% of the time, Pallas kernels for 4%

profile of v9, /device:TPU:2, one launch (start us, length us, event | category | flops | bytes accessed | tf_op | source)
XLA Modules:
  0.0 75.5 jit_solution(1577827426760201120)
XLA Ops:
  0.0 0.0 copy-start
  0.0 1.7 %pack.1 = bf16[32,16,128]{2,1,0:T(8,128)(2,1)} custom-call(s32[1,2]{1,0:T(1,128)} %corner.1, bf16[1,32,1024]{2,1,0:T(8,128)(2,1)} %box.1), custom_call_target="tpu_custom_call" | custom-call | bytes 200000 | tf_op jit(solution)/shard_map/pack/pallas_call | solution.py:349
  1.7 11.5 %all-to-all-start = ((bf16[32,16,128]{2,1,0:T(8,128)(2,1)}), bf16[32,16,128]{2,1,0:T(8,128)(2,1)S(1)}, u32[]{:S(2)}, u32[]{:S(2)}) async-start(bf16[32,16,128]{2,1,0:T(8,128)(2,1)} %pack.1), calls=%async_computation | async-start | bytes 262144 | tf_op jit(solution)/shard_map/all_to_all | solution.py:323
  13.2 0.9 %convert_reduce_fusion = f32[4096]{0:T(1024)S(1)} fusion(bf16[32,4096]{1,0:T(8,128)(2,1)} %param.8, s32[]{:T(128)S(6)} %select_n.3), kind=kLoop, calls=%fused_computation.1 | loop fusion | flops 4096 | bytes 24580 | tf_op jit(solution)/shard_map/reshape | solution.py:376
  14.1 0.1 reshape.33
  14.2 0.1 reshape.30.plane
  14.3 0.0 copy-start.1
  14.3 0.0 copy-start.2
  14.3 0.0 copy-done
  14.3 0.6 copy-done.1
  15.0 0.0 copy-done.2
  15.0 0.8 %tables.1 = (bf16[256,1024]{1,0:T(8,128)(2,1)S(1)}, s32[16,128]{1,0:T(8,128)S(1)}, s32[8,128]{1,0:T(8,128)S(1)}, f32[1024,256]{1,0:T(8,128)S(1)}) custom-call(s32[1]{0:T(128)} %bitcast.1.owner, s32[1,2]{1,0:T(1,128)S(1)} %copy-done.1, bf16[256,1024]{1,0:T(8,128)(2,1)S(1)} %copy-done, s32[2,32]{1,0:T(2,128)S(1)} %bitcast.13), custom_call_target="tpu_custom_call" | custom-call | flops 2000000 | bytes 3000000 | tf_op jit(solution)/shard_map/tables/pallas_call | solution.py:361
  15.8 7.8 %all-to-all-done.recv = bf16[32,16,128]{2,1,0:T(8,128)(2,1)S(1)} async-done(((bf16[32,16,128]{2,1,0:T(8,128)(2,1)}), bf16[32,16,128]{2,1,0:T(8,128)(2,1)S(1)}, u32[]{:S(2)}, u32[]{:S(2)}) %all-to-all-start) | async-done | bytes 131104 | tf_op jit(solution)/shard_map/all_to_all | solution.py:323
  23.6 0.8 %pair_products.1 = (f32[32,8,128]{2,1,0:T(8,128)}, f32[4,8,128]{2,1,0:T(8,128)S(1)}, f32[32,8,128]{2,1,0:T(8,128)S(1)}, f32[32,8,128]{2,1,0:T(8,128)S(1)}, f32[8,128]{1,0:T(8,128)S(1)}) custom-call(s32[16,128]{1,0:T(8,128)S(1)} %get-tuple-element.37.pairs, bf16[32,16,128]{2,1,0:T(8,128)(2,1)S(1)} %all-to-all-done.recv), custom_call_target="tpu_custom_call" | custom-call | bytes 600000 | tf_op jit(solution)/shard_map/pair_products/pallas_call | solution.py:382
  24.4 3.9 %all-to-all-start.1 = ((f32[32,8,128]{2,1,0:T(8,128)}), f32[32,8,128]{2,1,0:T(8,128)S(1)}, u32[]{:S(2)}, u32[]{:S(2)}) async-start(f32[32,8,128]{2,1,0:T(8,128)} %get-tuple-element.42), calls=%async_computation.1 | async-start | bytes 262144 | tf_op jit(solution)/shard_map/all_to_all | solution.py:323
  28.3 0.6 collective-permute-start
  28.9 3.2 %collective-permute-done = f32[4,8,128]{2,1,0:T(8,128)S(1)} collective-permute-done((f32[4,8,128]{2,1,0:T(8,128)S(1)}, f32[4,8,128]{2,1,0:T(8,128)S(1)}, u32[]{:S(2)}, u32[]{:S(2)}) %collective-permute-start) | collective-permute-done | bytes 16416 | tf_op jit(solution)/shard_map/ppermute | solution.py:341
  32.1 2.1 %collective-permute-start.1 = (f32[4,8,128]{2,1,0:T(8,128)S(1)}, f32[4,8,128]{2,1,0:T(8,128)S(1)}, u32[]{:S(2)}, u32[]{:S(2)}) collective-permute-start(f32[4,8,128]{2,1,0:T(8,128)S(1)} %add.10), channel_id=1, source_target_pairs={{0,128},{32,160},{64,192},{96,224},{128,0},{160,32},{192,64},{224,... | collective-permute-start | bytes 49160 | tf_op jit(solution)/shard_map/ppermute | solution.py:341
  34.3 3.1 %collective-permute-done.1 = f32[4,8,128]{2,1,0:T(8,128)S(1)} collective-permute-done((f32[4,8,128]{2,1,0:T(8,128)S(1)}, f32[4,8,128]{2,1,0:T(8,128)S(1)}, u32[]{:S(2)}, u32[]{:S(2)}) %collective-permute-start.1) | collective-permute-done | bytes 16416 | tf_op jit(solution)/shard_map/ppermute | solution.py:341
  37.4 1.5 %all-to-all-done.1 = f32[32,8,128]{2,1,0:T(8,128)S(1)} async-done(((f32[32,8,128]{2,1,0:T(8,128)}), f32[32,8,128]{2,1,0:T(8,128)S(1)}, u32[]{:S(2)}, u32[]{:S(2)}) %all-to-all-start.1) | async-done | bytes 131104 | tf_op jit(solution)/shard_map/all_to_all | solution.py:323
  38.9 0.0 collective-permute-start.2
  38.9 2.1 %solve.1 = f32[256,128]{1,0:T(8,128)S(1)} custom-call(f32[8,128]{1,0:T(8,128)S(1)} %get-tuple-element.41.place, f32[256,128]{1,0:T(8,128)S(1)} %bitcast.11, bf16[256,1024]{1,0:T(8,128)(2,1)S(1)} %get-tuple-element.45.fixed, f32[1024,256]{1,0:T(8,128)S(1)} %get-tuple-element.46.green), custom_call_target="tpu_custom_call" | custom-call | flops 1000000000 | bytes 3000000 | tf_op jit(solution)/shard_map/solve/pallas_call | solution.py:396
  41.0 0.0 collective-permute-done.2.other
  41.0 19.2 %all_to_all.20.field = f32[32,8,128]{2,1,0:T(8,128)S(1)} all-to-all(f32[32,8,128]{2,1,0:T(8,128)S(1)} %bitcast.12), channel_id=1, replica_groups=mesh['grp'=8,'own'=32] {'own'}, dimensions={0} | all-to-all | bytes 262144 | tf_op jit(solution)/shard_map/all_to_all | solution.py:323
  60.2 0.3 gradient_planes.1
  60.6 13.9 %all_to_all.21 = f32[32,8,128]{2,1,0:T(8,128)S(1)} all-to-all(f32[32,8,128]{2,1,0:T(8,128)S(1)} %gradient_planes.1), channel_id=1, replica_groups=mesh['grp'=8,'own'=32] {'own'}, dimensions={0} | all-to-all | bytes 262144 | tf_op jit(solution)/shard_map/all_to_all | solution.py:323
  74.5 1.0 %unpack.1 = f32[1,32,1024]{2,1,0:T(8,128)} custom-call(s32[8,128]{1,0:T(8,128)S(1)} %get-tuple-element.36.offsets, f32[256,128]{1,0:T(8,128)S(1)} %bitcast.10), custom_call_target="tpu_custom_call" | custom-call | bytes 300000 | tf_op jit(solution)/shard_map/unpack/pallas_call | solution.py:420
  (3 shorter events, 0.0 us)
Async XLA Ops:
  0.0 14.3 %copy-start = (bf16[256,1024]{1,0:T(8,128)(2,1)S(1)}, bf16[256,1024]{1,0:T(8,128)(2,1)}, u32[]{:S(2)}) copy-start(bf16[256,1024]{1,0:T(8,128)(2,1)} %constant.10.clone.fixed_in) | copy-start | bytes 1572868
  1.7 21.9 %all-to-all-start = ((bf16[32,16,128]{2,1,0:T(8,128)(2,1)}), bf16[32,16,128]{2,1,0:T(8,128)(2,1)S(1)}, u32[]{:S(2)}, u32[]{:S(2)}) async-start(bf16[32,16,128]{2,1,0:T(8,128)(2,1)} %pack.1), calls=%async_computation | async-start | bytes 262144 | tf_op jit(solution)/shard_map/all_to_all | solution.py:323
  14.3 0.7 copy-start.1
  14.3 0.7 copy-start.2
  24.4 14.5 %all-to-all-start.1 = ((f32[32,8,128]{2,1,0:T(8,128)}), f32[32,8,128]{2,1,0:T(8,128)S(1)}, u32[]{:S(2)}, u32[]{:S(2)}) async-start(f32[32,8,128]{2,1,0:T(8,128)} %get-tuple-element.42), calls=%async_computation.1 | async-start | bytes 262144 | tf_op jit(solution)/shard_map/all_to_all | solution.py:323
  28.3 3.8 %collective-permute-start = (f32[4,8,128]{2,1,0:T(8,128)S(1)}, f32[4,8,128]{2,1,0:T(8,128)S(1)}, u32[]{:S(2)}, u32[]{:S(2)}) collective-permute-start(f32[4,8,128]{2,1,0:T(8,128)S(1)} %get-tuple-element.43), channel_id=1, source_target_pairs={{0,64},{32,96},{64,0},{96,32},{128,192},{160,224},{192,128},{224,1... | collective-permute-start | bytes 49160 | tf_op jit(solution)/shard_map/ppermute | solution.py:341
  32.1 5.2 %collective-permute-start.1 = (f32[4,8,128]{2,1,0:T(8,128)S(1)}, f32[4,8,128]{2,1,0:T(8,128)S(1)}, u32[]{:S(2)}, u32[]{:S(2)}) collective-permute-start(f32[4,8,128]{2,1,0:T(8,128)S(1)} %add.10), channel_id=1, source_target_pairs={{0,128},{32,160},{64,192},{96,224},{128,0},{160,32},{192,64},{224,... | collective-permute-start | bytes 49160 | tf_op jit(solution)/shard_map/ppermute | solution.py:341
  38.9 2.1 %collective-permute-start.2 = (f32[4,8,128]{2,1,0:T(8,128)S(1)}, f32[4,8,128]{2,1,0:T(8,128)S(1)}, u32[]{:S(2)}, u32[]{:S(2)}) collective-permute-start(f32[4,8,128]{2,1,0:T(8,128)S(1)} %add.11.dens), channel_id=1, source_target_pairs={{0,32},{32,0},{64,96},{96,64},{128,160},{160,128},{192,224},{224,1... | collective-permute-start | bytes 49160 | tf_op jit(solution)/shard_map/ppermute | solution.py:341

commit v10 on v7

--- a/solution.py
+++ b/solution.py
@@ -236,12 +236,17 @@
         turned.append(jnp.concatenate(exchange_groups(tiles), axis=0))
     waves = dot(ahead_y, thrice(jnp.concatenate(turned, axis=1)))
     rows = jnp.concatenate([waves[:, 128 * c : 128 * c + 128] for c in range(16)], axis=0)
-    high, low = split(rows)
-    waves = dot(jnp.concatenate([high, low], axis=1), ahead_x)
-    waves = waves + dot(high, ahead_x_low)
-    high, low = split(waves * green[...])
-    both = dot(high, back_x)
-    rows = both[:, :128] + both[:, 128:] + dot(low, back_x[:, :128])
+    halves = []
+    for half in range(2):
+        high, low = split(rows[512 * half : 512 * half + 512])
+        waves = dot(jnp.concatenate([high, low], axis=1), ahead_x)
+        halves.append(waves + dot(high, ahead_x_low))
+    pieces = []
+    for half in range(2):
+        high, low = split(halves[half] * green[512 * half : 512 * half + 512, :])
+        both = dot(high, back_x)
+        pieces.append(both[:, :128] + both[:, 128:] + dot(low, back_x[:, :128]))
+    rows = jnp.concatenate(pieces, axis=0)
     levels = jnp.concatenate([rows[G * c : G * c + G, :] for c in range(16)], axis=1)
     levels = dot(back_y, thrice(levels))
     for c in range(16):

time: 71.6 us -> 71.3 us (level)
  no operation moved by 1% of the time
where the time goes in v10:
time: 71.3 us; the launch traced here: 70.7 us
  waiting for transfers between devices  25.2 us (35%)
  starting transfers between devices  22.9 us (32%)
  blocking collectives  13.7 us (19%)
  Pallas kernels  7.04 us (10%)
  other arithmetic  0.9 us (1%)
  local copies, waits for them, and re-layouts  0.87 us (1%)
    all_to_all x3, waiting for transfers between devices, exchange(): return lax.all_to_all(x, 'own', 0, 0, tiled=True)  24 us
    all_to_all x3, starting transfers between devices, exchange(): return lax.all_to_all(x, 'own', 0, 0, tiled=True)  19.2 us
    all_to_all x1, blocking collectives, exchange(): return lax.all_to_all(x, 'own', 0, 0, tiled=True)  13.7 us
    ppermute x4, starting transfers between devices, swapped(): return lax.ppermute(x, 'grp', [(g, g ^ bits) for g in range(8)])  3.67 us
    pallas_call x1, Pallas kernels, body(): kernel(solve_kernel, shape((8 * N, 128)), [VM] * 4, 'solve', 16, [pltpu.V...  2.41 us
    pallas_call x1, Pallas kernels, body(): kernel(pack_kernel, shape((N, 16, 128), BF16), [SM, VM], 'pack', 60, [plt...  1.7 us
  transfers between devices with their start and end apart: 7, of which 4 were waited for; matrix products, arithmetic and copies ran while one was open for 2% of the time, Pallas kernels for 5%

profile of v10, /device:TPU:2, one launch (start us, length us, event | category | flops | bytes accessed | tf_op | source)
XLA Modules:
  0.0 70.7 jit_solution(9937961135532758599)
XLA Ops:
  0.0 0.0 copy-start
  0.0 1.7 %pack.1 = bf16[32,16,128]{2,1,0:T(8,128)(2,1)} custom-call(s32[1,2]{1,0:T(1,128)} %corner.1, bf16[1,32,1024]{2,1,0:T(8,128)(2,1)} %box.1), custom_call_target="tpu_custom_call" | custom-call | bytes 200000 | tf_op jit(solution)/shard_map/pack/pallas_call | solution.py:354
  1.7 11.5 %all-to-all-start = ((bf16[32,16,128]{2,1,0:T(8,128)(2,1)}), bf16[32,16,128]{2,1,0:T(8,128)(2,1)S(1)}, u32[]{:S(2)}, u32[]{:S(2)}) async-start(bf16[32,16,128]{2,1,0:T(8,128)(2,1)} %pack.1), calls=%async_computation | async-start | bytes 262144 | tf_op jit(solution)/shard_map/all_to_all | solution.py:328
  13.2 0.9 %convert_reduce_fusion = f32[4096]{0:T(1024)S(1)} fusion(bf16[32,4096]{1,0:T(8,128)(2,1)} %param.8, s32[]{:T(128)S(6)} %select_n.3), kind=kLoop, calls=%fused_computation.1 | loop fusion | flops 4096 | bytes 24580 | tf_op jit(solution)/shard_map/reshape | solution.py:381
  14.1 0.1 reshape.33
  14.2 0.1 reshape.30.plane
  14.3 0.0 copy-start.1
  14.3 0.0 copy-start.2
  14.3 0.0 copy-done
  14.3 0.6 copy-done.1
  15.0 0.0 copy-done.2
  15.0 0.8 %tables.1 = (bf16[256,1024]{1,0:T(8,128)(2,1)S(1)}, s32[16,128]{1,0:T(8,128)S(1)}, s32[8,128]{1,0:T(8,128)S(1)}, f32[1024,256]{1,0:T(8,128)S(1)}) custom-call(s32[1]{0:T(128)} %bitcast.1.owner, s32[1,2]{1,0:T(1,128)S(1)} %copy-done.1, bf16[256,1024]{1,0:T(8,128)(2,1)S(1)} %copy-done, s32[2,32]{1,0:T(2,128)S(1)} %bitcast.12), custom_call_target="tpu_custom_call" | custom-call | flops 2000000 | bytes 3000000 | tf_op jit(solution)/shard_map/tables/pallas_call | solution.py:366
  15.8 7.8 %all-to-all-done.recv = bf16[32,16,128]{2,1,0:T(8,128)(2,1)S(1)} async-done(((bf16[32,16,128]{2,1,0:T(8,128)(2,1)}), bf16[32,16,128]{2,1,0:T(8,128)(2,1)S(1)}, u32[]{:S(2)}, u32[]{:S(2)}) %all-to-all-start) | async-done | bytes 131104 | tf_op jit(solution)/shard_map/all_to_all | solution.py:328
  23.6 0.8 %pair_products.1 = (f32[32,8,128]{2,1,0:T(8,128)}, f32[4,8,128]{2,1,0:T(8,128)S(1)}, f32[32,8,128]{2,1,0:T(8,128)S(1)}, f32[32,8,128]{2,1,0:T(8,128)S(1)}, f32[8,128]{1,0:T(8,128)S(1)}) custom-call(s32[16,128]{1,0:T(8,128)S(1)} %get-tuple-element.33.pairs, bf16[32,16,128]{2,1,0:T(8,128)(2,1)S(1)} %all-to-all-done.recv), custom_call_target="tpu_custom_call" | custom-call | bytes 600000 | tf_op jit(solution)/shard_map/pair_products/pallas_call | solution.py:387
  24.4 3.9 %all-to-all-start.1 = ((f32[32,8,128]{2,1,0:T(8,128)}), f32[32,8,128]{2,1,0:T(8,128)S(1)}, u32[]{:S(2)}, u32[]{:S(2)}) async-start(f32[32,8,128]{2,1,0:T(8,128)} %get-tuple-element.38), calls=%async_computation.1 | async-start | bytes 262144 | tf_op jit(solution)/shard_map/all_to_all | solution.py:328
  28.3 1.6 %collective-permute-start.2 = (f32[4,8,128]{2,1,0:T(8,128)S(1)}, f32[4,8,128]{2,1,0:T(8,128)S(1)}, u32[]{:S(2)}, u32[]{:S(2)}) collective-permute-start(f32[4,8,128]{2,1,0:T(8,128)S(1)} %get-tuple-element.42), channel_id=1, source_target_pairs={{0,192},{32,224},{64,128},{96,160},{128,64},{160,96},{192,0},{224,... | collective-permute-start | bytes 49160 | tf_op jit(solution)/shard_map/ppermute | solution.py:346
  29.9 1.8 %collective-permute-start.1 = (f32[4,8,128]{2,1,0:T(8,128)S(1)}, f32[4,8,128]{2,1,0:T(8,128)S(1)}, u32[]{:S(2)}, u32[]{:S(2)}) collective-permute-start(f32[4,8,128]{2,1,0:T(8,128)S(1)} %get-tuple-element.42), channel_id=1, source_target_pairs={{0,64},{32,96},{64,0},{96,32},{128,192},{160,224},{192,128},{224,1... | collective-permute-start | bytes 49160 | tf_op jit(solution)/shard_map/ppermute | solution.py:346
  31.7 0.2 collective-permute-start
  31.9 7.0 %all-to-all-done.1 = f32[32,8,128]{2,1,0:T(8,128)S(1)} async-done(((f32[32,8,128]{2,1,0:T(8,128)}), f32[32,8,128]{2,1,0:T(8,128)S(1)}, u32[]{:S(2)}, u32[]{:S(2)}) %all-to-all-start.1) | async-done | bytes 131104 | tf_op jit(solution)/shard_map/all_to_all | solution.py:328
  38.9 2.4 %solve.1 = f32[256,128]{1,0:T(8,128)} custom-call(f32[8,128]{1,0:T(8,128)S(1)} %get-tuple-element.37.place, f32[256,128]{1,0:T(8,128)S(1)} %bitcast.11, bf16[256,1024]{1,0:T(8,128)(2,1)S(1)} %get-tuple-element.39.fixed, f32[1024,256]{1,0:T(8,128)S(1)} %get-tuple-element.40.green), custom_call_target="tpu_custom_call" | custom-call | flops 1000000000 | bytes 3000000 | tf_op jit(solution)/shard_map/solve/pallas_call | solution.py:398
  41.3 3.9 %all-to-all-start.2 = ((f32[32,8,128]{2,1,0:T(8,128)}), f32[32,8,128]{2,1,0:T(8,128)S(1)}, u32[]{:S(2)}, u32[]{:S(2)}) async-start(f32[32,8,128]{2,1,0:T(8,128)} %bitcast.4), calls=%async_computation.2 | async-start | bytes 262144 | tf_op jit(solution)/shard_map/all_to_all | solution.py:328
  45.1 0.0 collective-permute-done.2
  45.1 0.0 collective-permute-done.1
  45.2 0.0 collective-permute-done
  45.2 0.1 collective-permute-start.3
  45.3 1.2 %collective-permute-done.3.other = f32[4,8,128]{2,1,0:T(8,128)S(1)} collective-permute-done((f32[4,8,128]{2,1,0:T(8,128)S(1)}, f32[4,8,128]{2,1,0:T(8,128)S(1)}, u32[]{:S(2)}, u32[]{:S(2)}) %collective-permute-start.3) | collective-permute-done | bytes 16416 | tf_op jit(solution)/shard_map/ppermute | solution.py:346
  46.5 9.2 %all-to-all-done.2.field = f32[32,8,128]{2,1,0:T(8,128)S(1)} async-done(((f32[32,8,128]{2,1,0:T(8,128)}), f32[32,8,128]{2,1,0:T(8,128)S(1)}, u32[]{:S(2)}, u32[]{:S(2)}) %all-to-all-start.2) | async-done | bytes 131104 | tf_op jit(solution)/shard_map/all_to_all | solution.py:328
  55.7 0.3 gradient_planes.1
  56.0 13.7 %all_to_all.20 = f32[32,8,128]{2,1,0:T(8,128)S(1)} all-to-all(f32[32,8,128]{2,1,0:T(8,128)S(1)} %gradient_planes.1), channel_id=1, replica_groups=mesh['grp'=8,'own'=32] {'own'}, dimensions={0} | all-to-all | bytes 262144 | tf_op jit(solution)/shard_map/all_to_all | solution.py:328
  69.7 1.0 %unpack.1 = f32[1,32,1024]{2,1,0:T(8,128)} custom-call(s32[8,128]{1,0:T(8,128)S(1)} %get-tuple-element.32.offsets, f32[256,128]{1,0:T(8,128)S(1)} %bitcast.10), custom_call_target="tpu_custom_call" | custom-call | bytes 300000 | tf_op jit(solution)/shard_map/unpack/pallas_call | solution.py:423
  (2 shorter events, 0.0 us)
Async XLA Ops:
  0.0 14.3 %copy-start = (bf16[256,1024]{1,0:T(8,128)(2,1)S(1)}, bf16[256,1024]{1,0:T(8,128)(2,1)}, u32[]{:S(2)}) copy-start(bf16[256,1024]{1,0:T(8,128)(2,1)} %constant.10.clone.fixed_in) | copy-start | bytes 1572868
  1.7 21.9 %all-to-all-start = ((bf16[32,16,128]{2,1,0:T(8,128)(2,1)}), bf16[32,16,128]{2,1,0:T(8,128)(2,1)S(1)}, u32[]{:S(2)}, u32[]{:S(2)}) async-start(bf16[32,16,128]{2,1,0:T(8,128)(2,1)} %pack.1), calls=%async_computation | async-start | bytes 262144 | tf_op jit(solution)/shard_map/all_to_all | solution.py:328
  14.3 0.7 copy-start.1
  14.3 0.7 copy-start.2
  24.4 14.4 %all-to-all-start.1 = ((f32[32,8,128]{2,1,0:T(8,128)}), f32[32,8,128]{2,1,0:T(8,128)S(1)}, u32[]{:S(2)}, u32[]{:S(2)}) async-start(f32[32,8,128]{2,1,0:T(8,128)} %get-tuple-element.38), calls=%async_computation.1 | async-start | bytes 262144 | tf_op jit(solution)/shard_map/all_to_all | solution.py:328
  28.3 16.8 %collective-permute-start.2 = (f32[4,8,128]{2,1,0:T(8,128)S(1)}, f32[4,8,128]{2,1,0:T(8,128)S(1)}, u32[]{:S(2)}, u32[]{:S(2)}) collective-permute-start(f32[4,8,128]{2,1,0:T(8,128)S(1)} %get-tuple-element.42), channel_id=1, source_target_pairs={{0,192},{32,224},{64,128},{96,160},{128,64},{160,96},{192,0},{224,... | collective-permute-start | bytes 49160 | tf_op jit(solution)/shard_map/ppermute | solution.py:346
  29.9 15.3 %collective-permute-start.1 = (f32[4,8,128]{2,1,0:T(8,128)S(1)}, f32[4,8,128]{2,1,0:T(8,128)S(1)}, u32[]{:S(2)}, u32[]{:S(2)}) collective-permute-start(f32[4,8,128]{2,1,0:T(8,128)S(1)} %get-tuple-element.42), channel_id=1, source_target_pairs={{0,64},{32,96},{64,0},{96,32},{128,192},{160,224},{192,128},{224,1... | collective-permute-start | bytes 49160 | tf_op jit(solution)/shard_map/ppermute | solution.py:346
  31.7 13.5 %collective-permute-start = (f32[4,8,128]{2,1,0:T(8,128)S(1)}, f32[4,8,128]{2,1,0:T(8,128)S(1)}, u32[]{:S(2)}, u32[]{:S(2)}) collective-permute-start(f32[4,8,128]{2,1,0:T(8,128)S(1)} %get-tuple-element.42), channel_id=1, source_target_pairs={{0,128},{32,160},{64,192},{96,224},{128,0},{160,32},{192,64},{224,... | collective-permute-start | bytes 49160 | tf_op jit(solution)/shard_map/ppermute | solution.py:346
  41.3 14.4 %all-to-all-start.2 = ((f32[32,8,128]{2,1,0:T(8,128)}), f32[32,8,128]{2,1,0:T(8,128)S(1)}, u32[]{:S(2)}, u32[]{:S(2)}) async-start(f32[32,8,128]{2,1,0:T(8,128)} %bitcast.4), calls=%async_computation.2 | async-start | bytes 262144 | tf_op jit(solution)/shard_map/all_to_all | solution.py:328
  45.2 1.3 %collective-permute-start.3 = (f32[4,8,128]{2,1,0:T(8,128)S(1)}, f32[4,8,128]{2,1,0:T(8,128)S(1)}, u32[]{:S(2)}, u32[]{:S(2)}) collective-permute-start(f32[4,8,128]{2,1,0:T(8,128)S(1)} %add_add_fusion.dens), channel_id=1, source_target_pairs={{0,32},{32,0},{64,96},{96,64},{128,160},{160,128},{192,224},{224,1... | collective-permute-start | bytes 49160 | tf_op jit(solution)/shard_map/ppermute | solution.py:346

commit v11 on v10

--- a/solution.py
+++ b/solution.py
@@ -95,7 +95,7 @@
     return numbers
 
 
-def pair_kernel(pairs, recv, rho, dens, phi, code, place):
+def pair_kernel(pairs, recv, rho, dens, phi, code, place, made, sem):
     numbers = pair_numbers(pairs)
     first = jnp.max(pairs[11:12, 0:1])
     row = lax.broadcasted_iota(jnp.int32, (8, 128), 0)
@@ -110,15 +110,19 @@
         quarter = below + jnp.where(x < value[9:10], 1.0, 0.0)
         phi[n] = plane
         code[n] = quarter
-        square = plane * plane
+    for p in range(N):
+        a, b = numbers[p]
+        made[p] = jnp.where(code[a] == code[b], phi[a] * phi[b], 0.0)
+    send = pltpu.make_async_copy(made, rho, sem)
+    send.start()
+    place[...] = recv[first].astype(F32)[8:]
+    for n in range(N):
+        square = phi[n] * phi[n]
         for q in range(4):
-            total[q] = total[q] + jnp.where(quarter == float(q), square, 0.0)
+            total[q] = total[q] + jnp.where(code[n] == float(q), square, 0.0)
     for q in range(4):
         dens[q] = total[q]
-    place[...] = recv[first].astype(F32)[8:]
-    for p in range(N):
-        a, b = numbers[p]
-        rho[p] = jnp.where(code[a] == code[b], phi[a] * phi[b], 0.0)
+    send.wait()
 
 
 def wave(index):
@@ -384,13 +388,15 @@
     )
 
     planes = shape((N, 8, 128))
-    rho, dens, phi, code, place = kernel(
+    rho, dens, phi, code, place = pl.pallas_call(
         pair_kernel,
-        [planes, shape((4, 8, 128)), planes, planes, shape((8, 128))],
-        [VM, VM],
-        "pair_products",
-        4,
-        moved=600_000,
+        out_shape=[planes, shape((4, 8, 128)), planes, planes, shape((8, 128))],
+        in_specs=[VM, VM],
+        out_specs=[pl.BlockSpec(memory_space=pltpu.HBM)] + [VM] * 4,
+        scratch_shapes=[pltpu.VMEM((N, 8, 128), F32), pltpu.SemaphoreType.DMA(())],
+        compiler_params=pltpu.CompilerParams(vmem_limit_bytes=4 << 20),
+        cost_estimate=pl.CostEstimate(flops=0, bytes_accessed=600_000, transcendentals=0),
+        name="pair_products",
     )(pairs, recv)
 
     mine = exchange(rho)

time: 71.3 us -> 71.3 us (level)
  no operation moved by 1% of the time
where the time goes in v11:
time: 71.3 us; the launch traced here: 70.8 us
  waiting for transfers between devices  25.3 us (35%)
  starting transfers between devices  22.9 us (32%)
  blocking collectives  13.7 us (19%)
  Pallas kernels  7.04 us (10%)
  other arithmetic  0.9 us (1%)
  local copies, waits for them, and re-layouts  0.87 us (1%)
    all_to_all x3, waiting for transfers between devices, exchange(): return lax.all_to_all(x, 'own', 0, 0, tiled=True)  24.1 us
    all_to_all x3, starting transfers between devices, exchange(): return lax.all_to_all(x, 'own', 0, 0, tiled=True)  19.2 us
    all_to_all x1, blocking collectives, exchange(): return lax.all_to_all(x, 'own', 0, 0, tiled=True)  13.7 us
    ppermute x4, starting transfers between devices, swapped(): return lax.ppermute(x, 'grp', [(g, g ^ bits) for g in range(8)])  3.67 us
    pallas_call x1, Pallas kernels, body(): kernel(solve_kernel, shape((8 * N, 128)), [VM] * 4, 'solve', 16, [pltpu.V...  2.41 us
    pallas_call x1, Pallas kernels, body(): kernel(pack_kernel, shape((N, 16, 128), BF16), [SM, VM], 'pack', 60, [plt...  1.7 us
  transfers between devices with their start and end apart: 7, of which 4 were waited for; matrix products, arithmetic and copies ran while one was open for 2% of the time, Pallas kernels for 5%

profile of v11, /device:TPU:2, one launch (start us, length us, event | category | flops | bytes accessed | tf_op | source)
XLA Modules:
  0.0 70.8 jit_solution(4408419705679527361)
XLA Ops:
  0.0 0.0 copy-start
  0.0 1.7 %pack.1 = bf16[32,16,128]{2,1,0:T(8,128)(2,1)} custom-call(s32[1,2]{1,0:T(1,128)} %corner.1, bf16[1,32,1024]{2,1,0:T(8,128)(2,1)} %box.1), custom_call_target="tpu_custom_call" | custom-call | bytes 200000 | tf_op jit(solution)/shard_map/pack/pallas_call | solution.py:358
  1.7 11.5 %all-to-all-start = ((bf16[32,16,128]{2,1,0:T(8,128)(2,1)}), bf16[32,16,128]{2,1,0:T(8,128)(2,1)S(1)}, u32[]{:S(2)}, u32[]{:S(2)}) async-start(bf16[32,16,128]{2,1,0:T(8,128)(2,1)} %pack.1), calls=%async_computation | async-start | bytes 262144 | tf_op jit(solution)/shard_map/all_to_all | solution.py:332
  13.2 0.9 %convert_reduce_fusion = f32[4096]{0:T(1024)S(1)} fusion(bf16[32,4096]{1,0:T(8,128)(2,1)} %param.8, s32[]{:T(128)S(6)} %select_n.3), kind=kLoop, calls=%fused_computation.1 | loop fusion | flops 4096 | bytes 24580 | tf_op jit(solution)/shard_map/reshape | solution.py:385
  14.1 0.1 reshape.33
  14.2 0.1 reshape.30.plane
  14.3 0.0 copy-start.1
  14.3 0.0 copy-start.2
  14.3 0.0 copy-done
  14.3 0.6 copy-done.1
  15.0 0.0 copy-done.2
  15.0 0.8 %tables.1 = (bf16[256,1024]{1,0:T(8,128)(2,1)S(1)}, s32[16,128]{1,0:T(8,128)S(1)}, s32[8,128]{1,0:T(8,128)S(1)}, f32[1024,256]{1,0:T(8,128)S(1)}) custom-call(s32[1]{0:T(128)} %bitcast.1.owner, s32[1,2]{1,0:T(1,128)S(1)} %copy-done.1, bf16[256,1024]{1,0:T(8,128)(2,1)S(1)} %copy-done, s32[2,32]{1,0:T(2,128)S(1)} %bitcast.12), custom_call_target="tpu_custom_call" | custom-call | flops 2000000 | bytes 3000000 | tf_op jit(solution)/shard_map/tables/pallas_call | solution.py:370
  15.8 7.8 %all-to-all-done.recv = bf16[32,16,128]{2,1,0:T(8,128)(2,1)S(1)} async-done(((bf16[32,16,128]{2,1,0:T(8,128)(2,1)}), bf16[32,16,128]{2,1,0:T(8,128)(2,1)S(1)}, u32[]{:S(2)}, u32[]{:S(2)}) %all-to-all-start) | async-done | bytes 131104 | tf_op jit(solution)/shard_map/all_to_all | solution.py:332
  23.6 0.8 %pair_products.1 = (f32[32,8,128]{2,1,0:T(8,128)}, f32[4,8,128]{2,1,0:T(8,128)S(1)}, f32[32,8,128]{2,1,0:T(8,128)S(1)}, f32[32,8,128]{2,1,0:T(8,128)S(1)}, f32[8,128]{1,0:T(8,128)S(1)}) custom-call(s32[16,128]{1,0:T(8,128)S(1)} %get-tuple-element.33.pairs, bf16[32,16,128]{2,1,0:T(8,128)(2,1)S(1)} %all-to-all-done.recv), custom_call_target="tpu_custom_call" | custom-call | bytes 600000 | tf_op jit(solution)/shard_map/pair_products/pallas_call | solution.py:391
  24.5 3.9 %all-to-all-start.1 = ((f32[32,8,128]{2,1,0:T(8,128)}), f32[32,8,128]{2,1,0:T(8,128)S(1)}, u32[]{:S(2)}, u32[]{:S(2)}) async-start(f32[32,8,128]{2,1,0:T(8,128)} %get-tuple-element.38), calls=%async_computation.1 | async-start | bytes 262144 | tf_op jit(solution)/shard_map/all_to_all | solution.py:332
  28.3 1.6 %collective-permute-start.2 = (f32[4,8,128]{2,1,0:T(8,128)S(1)}, f32[4,8,128]{2,1,0:T(8,128)S(1)}, u32[]{:S(2)}, u32[]{:S(2)}) collective-permute-start(f32[4,8,128]{2,1,0:T(8,128)S(1)} %get-tuple-element.42), channel_id=1, source_target_pairs={{0,192},{32,224},{64,128},{96,160},{128,64},{160,96},{192,0},{224,... | collective-permute-start | bytes 49160 | tf_op jit(solution)/shard_map/ppermute | solution.py:350
  29.9 1.8 %collective-permute-start.1 = (f32[4,8,128]{2,1,0:T(8,128)S(1)}, f32[4,8,128]{2,1,0:T(8,128)S(1)}, u32[]{:S(2)}, u32[]{:S(2)}) collective-permute-start(f32[4,8,128]{2,1,0:T(8,128)S(1)} %get-tuple-element.42), channel_id=1, source_target_pairs={{0,64},{32,96},{64,0},{96,32},{128,192},{160,224},{192,128},{224,1... | collective-permute-start | bytes 49160 | tf_op jit(solution)/shard_map/ppermute | solution.py:350
  31.7 0.2 collective-permute-start
  31.9 7.0 %all-to-all-done.1 = f32[32,8,128]{2,1,0:T(8,128)S(1)} async-done(((f32[32,8,128]{2,1,0:T(8,128)}), f32[32,8,128]{2,1,0:T(8,128)S(1)}, u32[]{:S(2)}, u32[]{:S(2)}) %all-to-all-start.1) | async-done | bytes 131104 | tf_op jit(solution)/shard_map/all_to_all | solution.py:332
  39.0 2.4 %solve.1 = f32[256,128]{1,0:T(8,128)} custom-call(f32[8,128]{1,0:T(8,128)S(1)} %get-tuple-element.37.place, f32[256,128]{1,0:T(8,128)S(1)} %bitcast.11, bf16[256,1024]{1,0:T(8,128)(2,1)S(1)} %get-tuple-element.39.fixed, f32[1024,256]{1,0:T(8,128)S(1)} %get-tuple-element.40.green), custom_call_target="tpu_custom_call" | custom-call | flops 1000000000 | bytes 3000000 | tf_op jit(solution)/shard_map/solve/pallas_call | solution.py:404
  41.4 3.9 %all-to-all-start.2 = ((f32[32,8,128]{2,1,0:T(8,128)}), f32[32,8,128]{2,1,0:T(8,128)S(1)}, u32[]{:S(2)}, u32[]{:S(2)}) async-start(f32[32,8,128]{2,1,0:T(8,128)} %bitcast.4), calls=%async_computation.2 | async-start | bytes 262144 | tf_op jit(solution)/shard_map/all_to_all | solution.py:332
  45.2 0.0 collective-permute-done.2
  45.2 0.0 collective-permute-done.1
  45.3 0.0 collective-permute-done
  45.3 0.1 collective-permute-start.3
  45.4 1.2 %collective-permute-done.3.other = f32[4,8,128]{2,1,0:T(8,128)S(1)} collective-permute-done((f32[4,8,128]{2,1,0:T(8,128)S(1)}, f32[4,8,128]{2,1,0:T(8,128)S(1)}, u32[]{:S(2)}, u32[]{:S(2)}) %collective-permute-start.3) | collective-permute-done | bytes 16416 | tf_op jit(solution)/shard_map/ppermute | solution.py:350
  46.6 9.2 %all-to-all-done.2.field = f32[32,8,128]{2,1,0:T(8,128)S(1)} async-done(((f32[32,8,128]{2,1,0:T(8,128)}), f32[32,8,128]{2,1,0:T(8,128)S(1)}, u32[]{:S(2)}, u32[]{:S(2)}) %all-to-all-start.2) | async-done | bytes 131104 | tf_op jit(solution)/shard_map/all_to_all | solution.py:332
  55.8 0.3 gradient_planes.1
  56.1 13.7 %all_to_all.20 = f32[32,8,128]{2,1,0:T(8,128)S(1)} all-to-all(f32[32,8,128]{2,1,0:T(8,128)S(1)} %gradient_planes.1), channel_id=1, replica_groups=mesh['grp'=8,'own'=32] {'own'}, dimensions={0} | all-to-all | bytes 262144 | tf_op jit(solution)/shard_map/all_to_all | solution.py:332
  69.8 1.0 %unpack.1 = f32[1,32,1024]{2,1,0:T(8,128)} custom-call(s32[8,128]{1,0:T(8,128)S(1)} %get-tuple-element.32.offsets, f32[256,128]{1,0:T(8,128)S(1)} %bitcast.10), custom_call_target="tpu_custom_call" | custom-call | bytes 300000 | tf_op jit(solution)/shard_map/unpack/pallas_call | solution.py:429
  (2 shorter events, 0.0 us)
Async XLA Ops:
  0.0 14.3 %copy-start = (bf16[256,1024]{1,0:T(8,128)(2,1)S(1)}, bf16[256,1024]{1,0:T(8,128)(2,1)}, u32[]{:S(2)}) copy-start(bf16[256,1024]{1,0:T(8,128)(2,1)} %constant.10.clone.fixed_in) | copy-start | bytes 1572868
  1.7 21.9 %all-to-all-start = ((bf16[32,16,128]{2,1,0:T(8,128)(2,1)}), bf16[32,16,128]{2,1,0:T(8,128)(2,1)S(1)}, u32[]{:S(2)}, u32[]{:S(2)}) async-start(bf16[32,16,128]{2,1,0:T(8,128)(2,1)} %pack.1), calls=%async_computation | async-start | bytes 262144 | tf_op jit(solution)/shard_map/all_to_all | solution.py:332
  14.3 0.7 copy-start.1
  14.3 0.7 copy-start.2
  24.5 14.5 %all-to-all-start.1 = ((f32[32,8,128]{2,1,0:T(8,128)}), f32[32,8,128]{2,1,0:T(8,128)S(1)}, u32[]{:S(2)}, u32[]{:S(2)}) async-start(f32[32,8,128]{2,1,0:T(8,128)} %get-tuple-element.38), calls=%async_computation.1 | async-start | bytes 262144 | tf_op jit(solution)/shard_map/all_to_all | solution.py:332
  28.3 16.9 %collective-permute-start.2 = (f32[4,8,128]{2,1,0:T(8,128)S(1)}, f32[4,8,128]{2,1,0:T(8,128)S(1)}, u32[]{:S(2)}, u32[]{:S(2)}) collective-permute-start(f32[4,8,128]{2,1,0:T(8,128)S(1)} %get-tuple-element.42), channel_id=1, source_target_pairs={{0,192},{32,224},{64,128},{96,160},{128,64},{160,96},{192,0},{224,... | collective-permute-start | bytes 49160 | tf_op jit(solution)/shard_map/ppermute | solution.py:350
  29.9 15.3 %collective-permute-start.1 = (f32[4,8,128]{2,1,0:T(8,128)S(1)}, f32[4,8,128]{2,1,0:T(8,128)S(1)}, u32[]{:S(2)}, u32[]{:S(2)}) collective-permute-start(f32[4,8,128]{2,1,0:T(8,128)S(1)} %get-tuple-element.42), channel_id=1, source_target_pairs={{0,64},{32,96},{64,0},{96,32},{128,192},{160,224},{192,128},{224,1... | collective-permute-start | bytes 49160 | tf_op jit(solution)/shard_map/ppermute | solution.py:350
  31.7 13.5 %collective-permute-start = (f32[4,8,128]{2,1,0:T(8,128)S(1)}, f32[4,8,128]{2,1,0:T(8,128)S(1)}, u32[]{:S(2)}, u32[]{:S(2)}) collective-permute-start(f32[4,8,128]{2,1,0:T(8,128)S(1)} %get-tuple-element.42), channel_id=1, source_target_pairs={{0,128},{32,160},{64,192},{96,224},{128,0},{160,32},{192,64},{224,... | collective-permute-start | bytes 49160 | tf_op jit(solution)/shard_map/ppermute | solution.py:350
  41.4 14.4 %all-to-all-start.2 = ((f32[32,8,128]{2,1,0:T(8,128)}), f32[32,8,128]{2,1,0:T(8,128)S(1)}, u32[]{:S(2)}, u32[]{:S(2)}) async-start(f32[32,8,128]{2,1,0:T(8,128)} %bitcast.4), calls=%async_computation.2 | async-start | bytes 262144 | tf_op jit(solution)/shard_map/all_to_all | solution.py:332
  45.3 1.3 %collective-permute-start.3 = (f32[4,8,128]{2,1,0:T(8,128)S(1)}, f32[4,8,128]{2,1,0:T(8,128)S(1)}, u32[]{:S(2)}, u32[]{:S(2)}) collective-permute-start(f32[4,8,128]{2,1,0:T(8,128)S(1)} %add_add_fusion.dens), channel_id=1, source_target_pairs={{0,32},{32,0},{64,96},{96,64},{128,160},{160,128},{192,224},{224,1... | collective-permute-start | bytes 49160 | tf_op jit(solution)/shard_map/ppermute | solution.py:350

commit v12 on v11

--- a/solution.py
+++ b/solution.py
@@ -400,7 +400,10 @@
     )(pairs, recv)
 
     mine = exchange(rho)
-    others = [swapped(dens, step) for step in (2, 4, 6)]
+    others = [swapped(dens, bits) for bits in (2, 4, 6)]
+    dens = (dens + others[1]) + (others[0] + others[2])
+    mine, dens = lax.optimization_barrier((mine, dens))
+    other = swapped(dens, 1)
     field = kernel(
         solve_kernel,
         shape((8 * N, 128)),
@@ -411,9 +414,8 @@
         flops=1_000_000_000,
         moved=3_000_000,
     )(place, mine.reshape(8 * N, 128), fixed, green)
+    field, other = lax.optimization_barrier((field, other))
     fields = exchange(field.reshape(N, 8, 128))
-    dens = (dens + others[1]) + (others[0] + others[2])
-    other = swapped(dens, 1)
 
     gradient = kernel(
         gradient_kernel,

time: 71.3 us -> 75.1 us (1.053)
  blocking collectives: 13.7 us -> 32.7 us
  waiting for transfers between devices: 25.3 us -> 14.9 us
  starting transfers between devices: 22.9 us -> 18.9 us
    all_to_all x1 -> x2, blocking collectives: 13.7 us -> 32.7 us  [exchange(): return lax.all_to_all(x, 'own', 0, 0, tiled=True)]
    all_to_all x3 -> x2, waiting for transfers between devices: 24.1 us -> 9.8 us  [exchange(): return lax.all_to_all(x, 'own', 0, 0, tiled=True)]
    ppermute x4, waiting for transfers between devices: 1.18 us -> 5.05 us  [swapped(): return lax.ppermute(x, 'grp', [(g, g ^ bits) for g in range(8)])]
    all_to_all x3 -> x2, starting transfers between devices: 19.2 us -> 15.4 us  [exchange(): return lax.all_to_all(x, 'own', 0, 0, tiled=True)]
  transfers between devices with their start and end apart: 7 -> 6, of which waited for: 4 -> 5; matrix products, arithmetic and copies ran while one was open for 2% -> 1% of each run, Pallas kernels for 5% -> 3%
where the time goes in v12:
time: 75.1 us; the launch traced here: 74.7 us
  blocking collectives  32.7 us (44%)
  starting transfers between devices  18.9 us (25%)
  waiting for transfers between devices  14.9 us (20%)
  Pallas kernels  6.38 us (8%)
  other arithmetic  0.9 us (1%)
  local copies, waits for them, and re-layouts  0.87 us (1%)
    all_to_all x2, blocking collectives, exchange(): return lax.all_to_all(x, 'own', 0, 0, tiled=True)  32.7 us
    all_to_all x2, starting transfers between devices, exchange(): return lax.all_to_all(x, 'own', 0, 0, tiled=True)  15.4 us
    all_to_all x2, waiting for transfers between devices, exchange(): return lax.all_to_all(x, 'own', 0, 0, tiled=True)  9.8 us
    ppermute x4, waiting for transfers between devices, swapped(): return lax.ppermute(x, 'grp', [(g, g ^ bits) for g in range(8)])  5.05 us
    ppermute x4, starting transfers between devices, swapped(): return lax.ppermute(x, 'grp', [(g, g ^ bits) for g in range(8)])  3.58 us
    pallas_call x1, Pallas kernels, body(): kernel(solve_kernel, shape((8 * N, 128)), [VM] * 4, 'solve', 16, [pltpu.V...  1.75 us
    pallas_call x1, Pallas kernels, body(): kernel(pack_kernel, shape((N, 16, 128), BF16), [SM, VM], 'pack', 60, [plt...  1.7 us
  transfers between devices with their start and end apart: 6, of which 5 were waited for; matrix products, arithmetic and copies ran while one was open for 1% of the time, Pallas kernels for 3%

profile of v12, /device:TPU:2, one launch (start us, length us, event | category | flops | bytes accessed | tf_op | source)
XLA Modules:
  0.0 74.7 jit_solution(9876642209648211440)
XLA Ops:
  0.0 0.0 copy-start
  0.0 1.7 %pack.1 = bf16[32,16,128]{2,1,0:T(8,128)(2,1)} custom-call(s32[1,2]{1,0:T(1,128)} %corner.1, bf16[1,32,1024]{2,1,0:T(8,128)(2,1)} %box.1), custom_call_target="tpu_custom_call" | custom-call | bytes 200000 | tf_op jit(solution)/shard_map/pack/pallas_call | solution.py:358
  1.7 11.5 %all-to-all-start = ((bf16[32,16,128]{2,1,0:T(8,128)(2,1)}), bf16[32,16,128]{2,1,0:T(8,128)(2,1)S(1)}, u32[]{:S(2)}, u32[]{:S(2)}) async-start(bf16[32,16,128]{2,1,0:T(8,128)(2,1)} %pack.1), calls=%async_computation | async-start | bytes 262144 | tf_op jit(solution)/shard_map/all_to_all | solution.py:332
  13.2 0.9 %convert_reduce_fusion = f32[4096]{0:T(1024)S(1)} fusion(bf16[32,4096]{1,0:T(8,128)(2,1)} %param.8, s32[]{:T(128)S(6)} %select_n.3), kind=kLoop, calls=%fused_computation.1 | loop fusion | flops 4096 | bytes 24580 | tf_op jit(solution)/shard_map/reshape | solution.py:385
  14.1 0.1 reshape.33
  14.2 0.1 reshape.30.plane
  14.3 0.0 copy-start.1
  14.3 0.0 copy-start.2
  14.3 0.0 copy-done
  14.3 0.6 copy-done.1
  15.0 0.0 copy-done.2
  15.0 0.8 %tables.1 = (bf16[256,1024]{1,0:T(8,128)(2,1)S(1)}, s32[16,128]{1,0:T(8,128)S(1)}, s32[8,128]{1,0:T(8,128)S(1)}, f32[1024,256]{1,0:T(8,128)S(1)}) custom-call(s32[1]{0:T(128)} %bitcast.1.owner, s32[1,2]{1,0:T(1,128)S(1)} %copy-done.1, bf16[256,1024]{1,0:T(8,128)(2,1)S(1)} %copy-done, s32[2,32]{1,0:T(2,128)S(1)} %bitcast.13), custom_call_target="tpu_custom_call" | custom-call | flops 2000000 | bytes 3000000 | tf_op jit(solution)/shard_map/tables/pallas_call | solution.py:370
  15.8 7.8 %all-to-all-done.recv = bf16[32,16,128]{2,1,0:T(8,128)(2,1)S(1)} async-done(((bf16[32,16,128]{2,1,0:T(8,128)(2,1)}), bf16[32,16,128]{2,1,0:T(8,128)(2,1)S(1)}, u32[]{:S(2)}, u32[]{:S(2)}) %all-to-all-start) | async-done | bytes 131104 | tf_op jit(solution)/shard_map/all_to_all | solution.py:332
  23.6 0.8 %pair_products.1 = (f32[32,8,128]{2,1,0:T(8,128)}, f32[4,8,128]{2,1,0:T(8,128)S(1)}, f32[32,8,128]{2,1,0:T(8,128)S(1)}, f32[32,8,128]{2,1,0:T(8,128)S(1)}, f32[8,128]{1,0:T(8,128)S(1)}) custom-call(s32[16,128]{1,0:T(8,128)S(1)} %get-tuple-element.37.pairs, bf16[32,16,128]{2,1,0:T(8,128)(2,1)S(1)} %all-to-all-done.recv), custom_call_target="tpu_custom_call" | custom-call | bytes 600000 | tf_op jit(solution)/shard_map/pair_products/pallas_call | solution.py:391
  24.5 3.9 %all-to-all-start.1 = ((f32[32,8,128]{2,1,0:T(8,128)}), f32[32,8,128]{2,1,0:T(8,128)S(1)}, u32[]{:S(2)}, u32[]{:S(2)}) async-start(f32[32,8,128]{2,1,0:T(8,128)} %get-tuple-element.42), calls=%async_computation.1 | async-start | bytes 262144 | tf_op jit(solution)/shard_map/all_to_all | solution.py:332
  28.3 1.6 %collective-permute-start.2 = (f32[4,8,128]{2,1,0:T(8,128)S(1)}, f32[4,8,128]{2,1,0:T(8,128)S(1)}, u32[]{:S(2)}, u32[]{:S(2)}) collective-permute-start(f32[4,8,128]{2,1,0:T(8,128)S(1)} %get-tuple-element.43), channel_id=1, source_target_pairs={{0,192},{32,224},{64,128},{96,160},{128,64},{160,96},{192,0},{224,... | collective-permute-start | bytes 49160 | tf_op jit(solution)/shard_map/ppermute | solution.py:350
  29.9 1.8 %collective-permute-start.1 = (f32[4,8,128]{2,1,0:T(8,128)S(1)}, f32[4,8,128]{2,1,0:T(8,128)S(1)}, u32[]{:S(2)}, u32[]{:S(2)}) collective-permute-start(f32[4,8,128]{2,1,0:T(8,128)S(1)} %get-tuple-element.43), channel_id=1, source_target_pairs={{0,64},{32,96},{64,0},{96,32},{128,192},{160,224},{192,128},{224,1... | collective-permute-start | bytes 49160 | tf_op jit(solution)/shard_map/ppermute | solution.py:350
  31.7 0.2 collective-permute-start
  31.9 0.2 collective-permute-done.2
  32.2 1.5 %collective-permute-done.1 = f32[4,8,128]{2,1,0:T(8,128)S(1)} collective-permute-done((f32[4,8,128]{2,1,0:T(8,128)S(1)}, f32[4,8,128]{2,1,0:T(8,128)S(1)}, u32[]{:S(2)}, u32[]{:S(2)}) %collective-permute-start.1) | collective-permute-done | bytes 16416 | tf_op jit(solution)/shard_map/ppermute | solution.py:350
  33.7 3.3 %collective-permute-done = f32[4,8,128]{2,1,0:T(8,128)S(1)} collective-permute-done((f32[4,8,128]{2,1,0:T(8,128)S(1)}, f32[4,8,128]{2,1,0:T(8,128)S(1)}, u32[]{:S(2)}, u32[]{:S(2)}) %collective-permute-start) | collective-permute-done | bytes 16416 | tf_op jit(solution)/shard_map/ppermute | solution.py:350
  37.0 2.0 %all-to-all-done.1 = f32[32,8,128]{2,1,0:T(8,128)S(1)} async-done(((f32[32,8,128]{2,1,0:T(8,128)}), f32[32,8,128]{2,1,0:T(8,128)S(1)}, u32[]{:S(2)}, u32[]{:S(2)}) %all-to-all-start.1) | async-done | bytes 131104 | tf_op jit(solution)/shard_map/all_to_all | solution.py:332
  38.9 0.0 collective-permute-start.3
  39.0 1.8 %solve.1 = f32[256,128]{1,0:T(8,128)S(1)} custom-call(f32[8,128]{1,0:T(8,128)S(1)} %get-tuple-element.41.place, f32[256,128]{1,0:T(8,128)S(1)} %bitcast.11, bf16[256,1024]{1,0:T(8,128)(2,1)S(1)} %get-tuple-element.45.fixed, f32[1024,256]{1,0:T(8,128)S(1)} %get-tuple-element.46.green), custom_call_target="tpu_custom_call" | custom-call | flops 1000000000 | bytes 3000000 | tf_op jit(solution)/shard_map/solve/pallas_call | solution.py:407
  40.7 0.0 collective-permute-done.3.other
  40.7 18.8 %all_to_all.20.field = f32[32,8,128]{2,1,0:T(8,128)S(1)} all-to-all(f32[32,8,128]{2,1,0:T(8,128)S(1)} %bitcast.12), channel_id=1, replica_groups=mesh['grp'=8,'own'=32] {'own'}, dimensions={0} | all-to-all | bytes 262144 | tf_op jit(solution)/shard_map/all_to_all | solution.py:332
  59.5 0.3 gradient_planes.1
  59.8 13.9 %all_to_all.21 = f32[32,8,128]{2,1,0:T(8,128)S(1)} all-to-all(f32[32,8,128]{2,1,0:T(8,128)S(1)} %gradient_planes.1), channel_id=1, replica_groups=mesh['grp'=8,'own'=32] {'own'}, dimensions={0} | all-to-all | bytes 262144 | tf_op jit(solution)/shard_map/all_to_all | solution.py:332
  73.7 1.0 %unpack.1 = f32[1,32,1024]{2,1,0:T(8,128)} custom-call(s32[8,128]{1,0:T(8,128)S(1)} %get-tuple-element.36.offsets, f32[256,128]{1,0:T(8,128)S(1)} %bitcast.10), custom_call_target="tpu_custom_call" | custom-call | bytes 300000 | tf_op jit(solution)/shard_map/unpack/pallas_call | solution.py:431
  (2 shorter events, 0.0 us)
Async XLA Ops:
  0.0 14.3 %copy-start = (bf16[256,1024]{1,0:T(8,128)(2,1)S(1)}, bf16[256,1024]{1,0:T(8,128)(2,1)}, u32[]{:S(2)}) copy-start(bf16[256,1024]{1,0:T(8,128)(2,1)} %constant.10.clone.fixed_in) | copy-start | bytes 1572868
  1.7 21.9 %all-to-all-start = ((bf16[32,16,128]{2,1,0:T(8,128)(2,1)}), bf16[32,16,128]{2,1,0:T(8,128)(2,1)S(1)}, u32[]{:S(2)}, u32[]{:S(2)}) async-start(bf16[32,16,128]{2,1,0:T(8,128)(2,1)} %pack.1), calls=%async_computation | async-start | bytes 262144 | tf_op jit(solution)/shard_map/all_to_all | solution.py:332
  14.3 0.7 copy-start.1
  14.3 0.7 copy-start.2
  24.5 14.5 %all-to-all-start.1 = ((f32[32,8,128]{2,1,0:T(8,128)}), f32[32,8,128]{2,1,0:T(8,128)S(1)}, u32[]{:S(2)}, u32[]{:S(2)}) async-start(f32[32,8,128]{2,1,0:T(8,128)} %get-tuple-element.42), calls=%async_computation.1 | async-start | bytes 262144 | tf_op jit(solution)/shard_map/all_to_all | solution.py:332
  28.3 3.8 %collective-permute-start.2 = (f32[4,8,128]{2,1,0:T(8,128)S(1)}, f32[4,8,128]{2,1,0:T(8,128)S(1)}, u32[]{:S(2)}, u32[]{:S(2)}) collective-permute-start(f32[4,8,128]{2,1,0:T(8,128)S(1)} %get-tuple-element.43), channel_id=1, source_target_pairs={{0,192},{32,224},{64,128},{96,160},{128,64},{160,96},{192,0},{224,... | collective-permute-start | bytes 49160 | tf_op jit(solution)/shard_map/ppermute | solution.py:350
  29.9 3.7 %collective-permute-start.1 = (f32[4,8,128]{2,1,0:T(8,128)S(1)}, f32[4,8,128]{2,1,0:T(8,128)S(1)}, u32[]{:S(2)}, u32[]{:S(2)}) collective-permute-start(f32[4,8,128]{2,1,0:T(8,128)S(1)} %get-tuple-element.43), channel_id=1, source_target_pairs={{0,64},{32,96},{64,0},{96,32},{128,192},{160,224},{192,128},{224,1... | collective-permute-start | bytes 49160 | tf_op jit(solution)/shard_map/ppermute | solution.py:350
  31.7 5.2 %collective-permute-start = (f32[4,8,128]{2,1,0:T(8,128)S(1)}, f32[4,8,128]{2,1,0:T(8,128)S(1)}, u32[]{:S(2)}, u32[]{:S(2)}) collective-permute-start(f32[4,8,128]{2,1,0:T(8,128)S(1)} %get-tuple-element.43), channel_id=1, source_target_pairs={{0,128},{32,160},{64,192},{96,224},{128,0},{160,32},{192,64},{224,... | collective-permute-start | bytes 49160 | tf_op jit(solution)/shard_map/ppermute | solution.py:350
  38.9 1.8 %collective-permute-start.3 = (f32[4,8,128]{2,1,0:T(8,128)S(1)}, f32[4,8,128]{2,1,0:T(8,128)S(1)}, u32[]{:S(2)}, u32[]{:S(2)}) collective-permute-start(f32[4,8,128]{2,1,0:T(8,128)S(1)} %add_add_fusion.dens), channel_id=1, source_target_pairs={{0,32},{32,0},{64,96},{96,64},{128,160},{160,128},{192,224},{224,1... | collective-permute-start | bytes 49160 | tf_op jit(solution)/shard_map/ppermute | solution.py:350

commit v13 on v11

--- a/solution.py
+++ b/solution.py
@@ -240,11 +240,11 @@
         turned.append(jnp.concatenate(exchange_groups(tiles), axis=0))
     waves = dot(ahead_y, thrice(jnp.concatenate(turned, axis=1)))
     rows = jnp.concatenate([waves[:, 128 * c : 128 * c + 128] for c in range(16)], axis=0)
+    both_x = jnp.concatenate([ahead_x, ahead_x_low], axis=0)
     halves = []
     for half in range(2):
         high, low = split(rows[512 * half : 512 * half + 512])
-        waves = dot(jnp.concatenate([high, low], axis=1), ahead_x)
-        halves.append(waves + dot(high, ahead_x_low))
+        halves.append(dot(jnp.concatenate([high, low, high], axis=1), both_x))
     pieces = []
     for half in range(2):
         high, low = split(halves[half] * green[512 * half : 512 * half + 512, :])

time: 71.3 us -> 71.3 us (level)
  no operation moved by 1% of the time
where the time goes in v13:
time: 71.3 us; the launch traced here: 70.8 us
  waiting for transfers between devices  25.3 us (35%)
  starting transfers between devices  22.9 us (32%)
  blocking collectives  13.7 us (19%)
  Pallas kernels  7.05 us (10%)
  other arithmetic  0.9 us (1%)
  local copies, waits for them, and re-layouts  0.87 us (1%)
    all_to_all x3, waiting for transfers between devices, exchange(): return lax.all_to_all(x, 'own', 0, 0, tiled=True)  24.1 us
    all_to_all x3, starting transfers between devices, exchange(): return lax.all_to_all(x, 'own', 0, 0, tiled=True)  19.2 us
    all_to_all x1, blocking collectives, exchange(): return lax.all_to_all(x, 'own', 0, 0, tiled=True)  13.7 us
    ppermute x4, starting transfers between devices, swapped(): return lax.ppermute(x, 'grp', [(g, g ^ bits) for g in range(8)])  3.67 us
    pallas_call x1, Pallas kernels, body(): kernel(solve_kernel, shape((8 * N, 128)), [VM] * 4, 'solve', 16, [pltpu.V...  2.41 us
    pallas_call x1, Pallas kernels, body(): kernel(pack_kernel, shape((N, 16, 128), BF16), [SM, VM], 'pack', 60, [plt...  1.7 us
  transfers between devices with their start and end apart: 7, of which 4 were waited for; matrix products, arithmetic and copies ran while one was open for 2% of the time, Pallas kernels for 5%

profile of v13, /device:TPU:2, one launch (start us, length us, event | category | flops | bytes accessed | tf_op | source)
XLA Modules:
  0.0 70.8 jit_solution(9261680327099342101)
XLA Ops:
  0.0 0.0 copy-start
  0.0 1.7 %pack.1 = bf16[32,16,128]{2,1,0:T(8,128)(2,1)} custom-call(s32[1,2]{1,0:T(1,128)} %corner.1, bf16[1,32,1024]{2,1,0:T(8,128)(2,1)} %box.1), custom_call_target="tpu_custom_call" | custom-call | bytes 200000 | tf_op jit(solution)/shard_map/pack/pallas_call | solution.py:358
  1.7 11.5 %all-to-all-start = ((bf16[32,16,128]{2,1,0:T(8,128)(2,1)}), bf16[32,16,128]{2,1,0:T(8,128)(2,1)S(1)}, u32[]{:S(2)}, u32[]{:S(2)}) async-start(bf16[32,16,128]{2,1,0:T(8,128)(2,1)} %pack.1), calls=%async_computation | async-start | bytes 262144 | tf_op jit(solution)/shard_map/all_to_all | solution.py:332
  13.2 0.9 %convert_reduce_fusion = f32[4096]{0:T(1024)S(1)} fusion(bf16[32,4096]{1,0:T(8,128)(2,1)} %param.8, s32[]{:T(128)S(6)} %select_n.3), kind=kLoop, calls=%fused_computation.1 | loop fusion | flops 4096 | bytes 24580 | tf_op jit(solution)/shard_map/reshape | solution.py:385
  14.1 0.1 reshape.33
  14.2 0.1 reshape.30.plane
  14.3 0.0 copy-start.1
  14.3 0.0 copy-start.2
  14.3 0.0 copy-done
  14.3 0.6 copy-done.1
  15.0 0.0 copy-done.2
  15.0 0.8 %tables.1 = (bf16[256,1024]{1,0:T(8,128)(2,1)S(1)}, s32[16,128]{1,0:T(8,128)S(1)}, s32[8,128]{1,0:T(8,128)S(1)}, f32[1024,256]{1,0:T(8,128)S(1)}) custom-call(s32[1]{0:T(128)} %bitcast.1.owner, s32[1,2]{1,0:T(1,128)S(1)} %copy-done.1, bf16[256,1024]{1,0:T(8,128)(2,1)S(1)} %copy-done, s32[2,32]{1,0:T(2,128)S(1)} %bitcast.12), custom_call_target="tpu_custom_call" | custom-call | flops 2000000 | bytes 3000000 | tf_op jit(solution)/shard_map/tables/pallas_call | solution.py:370
  15.8 7.8 %all-to-all-done.recv = bf16[32,16,128]{2,1,0:T(8,128)(2,1)S(1)} async-done(((bf16[32,16,128]{2,1,0:T(8,128)(2,1)}), bf16[32,16,128]{2,1,0:T(8,128)(2,1)S(1)}, u32[]{:S(2)}, u32[]{:S(2)}) %all-to-all-start) | async-done | bytes 131104 | tf_op jit(solution)/shard_map/all_to_all | solution.py:332
  23.6 0.8 %pair_products.1 = (f32[32,8,128]{2,1,0:T(8,128)}, f32[4,8,128]{2,1,0:T(8,128)S(1)}, f32[32,8,128]{2,1,0:T(8,128)S(1)}, f32[32,8,128]{2,1,0:T(8,128)S(1)}, f32[8,128]{1,0:T(8,128)S(1)}) custom-call(s32[16,128]{1,0:T(8,128)S(1)} %get-tuple-element.33.pairs, bf16[32,16,128]{2,1,0:T(8,128)(2,1)S(1)} %all-to-all-done.recv), custom_call_target="tpu_custom_call" | custom-call | bytes 600000 | tf_op jit(solution)/shard_map/pair_products/pallas_call | solution.py:391
  24.5 3.9 %all-to-all-start.1 = ((f32[32,8,128]{2,1,0:T(8,128)}), f32[32,8,128]{2,1,0:T(8,128)S(1)}, u32[]{:S(2)}, u32[]{:S(2)}) async-start(f32[32,8,128]{2,1,0:T(8,128)} %get-tuple-element.38), calls=%async_computation.1 | async-start | bytes 262144 | tf_op jit(solution)/shard_map/all_to_all | solution.py:332
  28.3 1.6 %collective-permute-start.2 = (f32[4,8,128]{2,1,0:T(8,128)S(1)}, f32[4,8,128]{2,1,0:T(8,128)S(1)}, u32[]{:S(2)}, u32[]{:S(2)}) collective-permute-start(f32[4,8,128]{2,1,0:T(8,128)S(1)} %get-tuple-element.42), channel_id=1, source_target_pairs={{0,192},{32,224},{64,128},{96,160},{128,64},{160,96},{192,0},{224,... | collective-permute-start | bytes 49160 | tf_op jit(solution)/shard_map/ppermute | solution.py:350
  29.9 1.8 %collective-permute-start.1 = (f32[4,8,128]{2,1,0:T(8,128)S(1)}, f32[4,8,128]{2,1,0:T(8,128)S(1)}, u32[]{:S(2)}, u32[]{:S(2)}) collective-permute-start(f32[4,8,128]{2,1,0:T(8,128)S(1)} %get-tuple-element.42), channel_id=1, source_target_pairs={{0,64},{32,96},{64,0},{96,32},{128,192},{160,224},{192,128},{224,1... | collective-permute-start | bytes 49160 | tf_op jit(solution)/shard_map/ppermute | solution.py:350
  31.7 0.2 collective-permute-start
  31.9 7.0 %all-to-all-done.1 = f32[32,8,128]{2,1,0:T(8,128)S(1)} async-done(((f32[32,8,128]{2,1,0:T(8,128)}), f32[32,8,128]{2,1,0:T(8,128)S(1)}, u32[]{:S(2)}, u32[]{:S(2)}) %all-to-all-start.1) | async-done | bytes 131104 | tf_op jit(solution)/shard_map/all_to_all | solution.py:332
  39.0 2.4 %solve.1 = f32[256,128]{1,0:T(8,128)} custom-call(f32[8,128]{1,0:T(8,128)S(1)} %get-tuple-element.37.place, f32[256,128]{1,0:T(8,128)S(1)} %bitcast.11, bf16[256,1024]{1,0:T(8,128)(2,1)S(1)} %get-tuple-element.39.fixed, f32[1024,256]{1,0:T(8,128)S(1)} %get-tuple-element.40.green), custom_call_target="tpu_custom_call" | custom-call | flops 1000000000 | bytes 3000000 | tf_op jit(solution)/shard_map/solve/pallas_call | solution.py:404
  41.4 3.9 %all-to-all-start.2 = ((f32[32,8,128]{2,1,0:T(8,128)}), f32[32,8,128]{2,1,0:T(8,128)S(1)}, u32[]{:S(2)}, u32[]{:S(2)}) async-start(f32[32,8,128]{2,1,0:T(8,128)} %bitcast.4), calls=%async_computation.2 | async-start | bytes 262144 | tf_op jit(solution)/shard_map/all_to_all | solution.py:332
  45.2 0.0 collective-permute-done.2
  45.2 0.0 collective-permute-done.1
  45.3 0.0 collective-permute-done
  45.3 0.1 collective-permute-start.3
  45.4 1.2 %collective-permute-done.3.other = f32[4,8,128]{2,1,0:T(8,128)S(1)} collective-permute-done((f32[4,8,128]{2,1,0:T(8,128)S(1)}, f32[4,8,128]{2,1,0:T(8,128)S(1)}, u32[]{:S(2)}, u32[]{:S(2)}) %collective-permute-start.3) | collective-permute-done | bytes 16416 | tf_op jit(solution)/shard_map/ppermute | solution.py:350
  46.6 9.2 %all-to-all-done.2.field = f32[32,8,128]{2,1,0:T(8,128)S(1)} async-done(((f32[32,8,128]{2,1,0:T(8,128)}), f32[32,8,128]{2,1,0:T(8,128)S(1)}, u32[]{:S(2)}, u32[]{:S(2)}) %all-to-all-start.2) | async-done | bytes 131104 | tf_op jit(solution)/shard_map/all_to_all | solution.py:332
  55.8 0.3 gradient_planes.1
  56.1 13.7 %all_to_all.20 = f32[32,8,128]{2,1,0:T(8,128)S(1)} all-to-all(f32[32,8,128]{2,1,0:T(8,128)S(1)} %gradient_planes.1), channel_id=1, replica_groups=mesh['grp'=8,'own'=32] {'own'}, dimensions={0} | all-to-all | bytes 262144 | tf_op jit(solution)/shard_map/all_to_all | solution.py:332
  69.8 1.0 %unpack.1 = f32[1,32,1024]{2,1,0:T(8,128)} custom-call(s32[8,128]{1,0:T(8,128)S(1)} %get-tuple-element.32.offsets, f32[256,128]{1,0:T(8,128)S(1)} %bitcast.10), custom_call_target="tpu_custom_call" | custom-call | bytes 300000 | tf_op jit(solution)/shard_map/unpack/pallas_call | solution.py:429
  (2 shorter events, 0.0 us)
Async XLA Ops:
  0.0 14.3 %copy-start = (bf16[256,1024]{1,0:T(8,128)(2,1)S(1)}, bf16[256,1024]{1,0:T(8,128)(2,1)}, u32[]{:S(2)}) copy-start(bf16[256,1024]{1,0:T(8,128)(2,1)} %constant.10.clone.fixed_in) | copy-start | bytes 1572868
  1.7 21.9 %all-to-all-start = ((bf16[32,16,128]{2,1,0:T(8,128)(2,1)}), bf16[32,16,128]{2,1,0:T(8,128)(2,1)S(1)}, u32[]{:S(2)}, u32[]{:S(2)}) async-start(bf16[32,16,128]{2,1,0:T(8,128)(2,1)} %pack.1), calls=%async_computation | async-start | bytes 262144 | tf_op jit(solution)/shard_map/all_to_all | solution.py:332
  14.3 0.7 copy-start.1
  14.3 0.7 copy-start.2
  24.5 14.5 %all-to-all-start.1 = ((f32[32,8,128]{2,1,0:T(8,128)}), f32[32,8,128]{2,1,0:T(8,128)S(1)}, u32[]{:S(2)}, u32[]{:S(2)}) async-start(f32[32,8,128]{2,1,0:T(8,128)} %get-tuple-element.38), calls=%async_computation.1 | async-start | bytes 262144 | tf_op jit(solution)/shard_map/all_to_all | solution.py:332
  28.3 16.9 %collective-permute-start.2 = (f32[4,8,128]{2,1,0:T(8,128)S(1)}, f32[4,8,128]{2,1,0:T(8,128)S(1)}, u32[]{:S(2)}, u32[]{:S(2)}) collective-permute-start(f32[4,8,128]{2,1,0:T(8,128)S(1)} %get-tuple-element.42), channel_id=1, source_target_pairs={{0,192},{32,224},{64,128},{96,160},{128,64},{160,96},{192,0},{224,... | collective-permute-start | bytes 49160 | tf_op jit(solution)/shard_map/ppermute | solution.py:350
  29.9 15.3 %collective-permute-start.1 = (f32[4,8,128]{2,1,0:T(8,128)S(1)}, f32[4,8,128]{2,1,0:T(8,128)S(1)}, u32[]{:S(2)}, u32[]{:S(2)}) collective-permute-start(f32[4,8,128]{2,1,0:T(8,128)S(1)} %get-tuple-element.42), channel_id=1, source_target_pairs={{0,64},{32,96},{64,0},{96,32},{128,192},{160,224},{192,128},{224,1... | collective-permute-start | bytes 49160 | tf_op jit(solution)/shard_map/ppermute | solution.py:350
  31.7 13.5 %collective-permute-start = (f32[4,8,128]{2,1,0:T(8,128)S(1)}, f32[4,8,128]{2,1,0:T(8,128)S(1)}, u32[]{:S(2)}, u32[]{:S(2)}) collective-permute-start(f32[4,8,128]{2,1,0:T(8,128)S(1)} %get-tuple-element.42), channel_id=1, source_target_pairs={{0,128},{32,160},{64,192},{96,224},{128,0},{160,32},{192,64},{224,... | collective-permute-start | bytes 49160 | tf_op jit(solution)/shard_map/ppermute | solution.py:350
  41.4 14.4 %all-to-all-start.2 = ((f32[32,8,128]{2,1,0:T(8,128)}), f32[32,8,128]{2,1,0:T(8,128)S(1)}, u32[]{:S(2)}, u32[]{:S(2)}) async-start(f32[32,8,128]{2,1,0:T(8,128)} %bitcast.4), calls=%async_computation.2 | async-start | bytes 262144 | tf_op jit(solution)/shard_map/all_to_all | solution.py:332
  45.3 1.3 %collective-permute-start.3 = (f32[4,8,128]{2,1,0:T(8,128)S(1)}, f32[4,8,128]{2,1,0:T(8,128)S(1)}, u32[]{:S(2)}, u32[]{:S(2)}) collective-permute-start(f32[4,8,128]{2,1,0:T(8,128)S(1)} %add_add_fusion.dens), channel_id=1, source_target_pairs={{0,32},{32,0},{64,96},{96,64},{128,160},{160,128},{192,224},{224,1... | collective-permute-start | bytes 49160 | tf_op jit(solution)/shard_map/ppermute | solution.py:350
